TPU v7x, 32 devices: a whole 2x2x4 slice. The times are simulated.
32 devices in a mesh: gx: 8 (over z, core), gy: 4 (over y, x).
Axes of the slice: x: 2, y: 2, z: 4, core: 2. Of those that a mesh axis runs over, the one named last changes fastest.
Arguments:
- key_rows: bfloat16 [16384, 3072], P(('gx', 'gy')), may hold values from -6 to 6
- value_rows: bfloat16 [16384, 3072], P(('gx', 'gy')), may hold values from -6 to 6
- query_rows: bfloat16 [16384, 3072], P(('gx', 'gy')), may hold values from -6 to 6
- token_rates: float32 [16384, 48], P(('gx', 'gy')), may hold values from 0.1 to 1
- fast_weights: float32 [3072, 512], P(('gx', 'gy')), may hold values from -0.6 to 0.6
- momentum: float32 [3072, 512], P(('gx', 'gy')), may hold values from -0.3 to 0.3
- norm_gain: float32 [48, 64], replicated, may hold values from 0.5 to 1.5
- norm_bias: float32 [48, 64], replicated, may hold values from -1.5 to 1.5
Outputs:
- mixed: bfloat16 [16384, 3072], P(('gx', 'gy'))
- new_fast: float32 [3072, 512], P(('gx', 'gy'))
- new_moment: float32 [3072, 512], P(('gx', 'gy'))
All inputs are finite; a program needn't handle non-finite values.
Results may differ from a plain program's by a relative error of at most 0.0095.
Values may be sent and summed in bfloat16 or wider, within the bound.
No kernel may reach another device: no remote copies, remote signals or barrier semaphores. Data moves between devices by JAX's collectives and lax.ppermute only.
A program may use at most 128 MiB of HBM per device.

v0:
```python
import jax
import jax.numpy as jnp
from jax import lax
from jax.sharding import PartitionSpec as P

STEPS = 2


momentum_keep = 0.9
inner_rate = 0.5


def normalize(hidden, gain, bias):
    centre = hidden - jnp.mean(hidden, axis=-1, keepdims=True)
    spread = jnp.mean(centre * centre, axis=-1, keepdims=True)
    return centre * lax.rsqrt(spread + 1e-06) * gain + bias


def predict(inputs, packed, gain, bias):
    width = packed.shape[-1] // 2
    first = jnp.einsum("tgd,gdf->tgf", inputs, packed[:, :, :width])
    active = jax.nn.gelu(first)
    second = jnp.einsum("tgf,gdf->tgd", active, packed[:, :, width:])
    return normalize(second, gain, bias)


def grouped(array, heads):
    return jnp.moveaxis(array.reshape(array.shape[0], heads // 2, 2, -1), 1, 0)


def shard_gradient(key_rows, value_rows, token_rates, weights, gain, bias, total):
    heads = token_rates.shape[1]
    inputs = grouped(key_rows.astype(jnp.float32), heads)
    targets = grouped(value_rows.astype(jnp.float32), heads) - inputs
    rates = jnp.moveaxis(token_rates.reshape(token_rates.shape[0], heads // 2, 2), 1, 0)
    packed = weights.reshape(heads // 2, 2, -1, weights.shape[1])
    gains = gain.reshape(heads // 2, 2, -1)
    biases = bias.reshape(heads // 2, 2, -1)

    def per_group(items):
        inputs_g, targets_g, rates_g, packed_g, gain_g, bias_g = items

        def loss(packed_now):
            error = predict(inputs_g, packed_now, gain_g, bias_g) - targets_g
            return 0.5 * jnp.sum(rates_g[..., None] * error * error) / total

        return jax.grad(loss)(packed_g)

    grads = lax.map(per_group, (inputs, targets, rates, packed, gains, biases))
    return grads.reshape(weights.shape)


def shard_output(query_rows, weights, gain, bias):
    heads = gain.shape[0]
    inputs = grouped(query_rows.astype(jnp.float32), heads)
    packed = weights.reshape(heads // 2, 2, -1, weights.shape[1])
    gains = gain.reshape(heads // 2, 2, -1)
    biases = bias.reshape(heads // 2, 2, -1)

    def per_group(items):
        return predict(items[0], items[1], items[2], items[3])

    outputs = lax.map(per_group, (inputs, packed, gains, biases))
    outputs = jnp.moveaxis(outputs, 0, 1).reshape(query_rows.shape)
    return (query_rows.astype(jnp.float32) + outputs).astype(jnp.bfloat16)


def rounded(array):
    return lax.optimization_barrier(array.astype(jnp.bfloat16)).astype(jnp.float32)


def fetch(fast):
    narrow = fast.astype(jnp.bfloat16)
    inner = lax.all_gather(narrow, "gy", axis=0, tiled=True)
    whole = lax.all_gather(inner, "gx", axis=0, tiled=True)
    return whole.astype(jnp.float32)


def collect(part):
    outer = lax.psum_scatter(part.astype(jnp.bfloat16), "gx", scatter_dimension=0, tiled=True)
    return lax.psum_scatter(outer, "gy", scatter_dimension=0, tiled=True).astype(jnp.float32)


def per_device(
    key_rows, value_rows, query_rows, token_rates, fast_weights, momentum, norm_gain, norm_bias
):
    total = key_rows.shape[0] * lax.axis_size("gx") * lax.axis_size("gy")
    fast, moment = (fast_weights, momentum)
    for step in range(STEPS):
        part = shard_gradient(
            key_rows, value_rows, token_rates, fetch(fast), norm_gain, norm_bias, total
        )
        grad = collect(rounded(part))
        moment = momentum_keep * moment + grad
        fast = fast - inner_rate * moment
    weights = fetch(fast)
    mixed = shard_output(query_rows, weights, norm_gain, norm_bias)
    return (mixed, fast, moment)


def solution(mesh):
    placed = (
        P(("gx", "gy"), None),
        P(("gx", "gy"), None),
        P(("gx", "gy"), None),
        P(("gx", "gy"), None),
        P(("gx", "gy"), None),
        P(("gx", "gy"), None),
        P(),
        P(),
    )
    return jax.shard_map(
        per_device,
        mesh=mesh,
        in_specs=placed,
        out_specs=(P(("gx", "gy"), None), P(("gx", "gy"), None), P(("gx", "gy"), None)),
        check_vma=False,
    )
```

profile of v0, /device:TPU:0, one launch (start us, length us, event | category | flops | bytes accessed | tf_op | source)
XLA Modules:
  0.0 816.1 jit_solution(3768390731659860334)
XLA Ops:
  8.2 11.7 %all_gather.18 = bf16[384,512]{1,0:T(8,128)(2,1)} all-gather(bf16[96,512]{1,0:T(8,128)(2,1)S(1)} %convert_element_type.46), channel_id=1, replica_groups=mesh['gx'=8,'gy'=4] {'gy'}, dimensions={0}, use_global_device_ids=true | all-gather | bytes 491520 | tf_op jit(solution)/shard_map/all_gather | solution.py:74
  19.9 5.4 copy.26
  25.4 5.7 copy.27
  31.0 5.1 convert.53
  36.1 7.1 sub.74
  43.3 15.2 %all-gather.4.cloned.1.call-done = bf16[3072,512]{1,0:T(8,128)(2,1)} async-done(((bf16[384,512]{1,0:T(8,128)(2,1)}), bf16[3072,512]{1,0:T(8,128)(2,1)}) %all-gather.4.cloned.1.call-update) | async-done | bytes 3145744 | tf_op jit(solution)/shard_map/all_gather | solution.py:75
  58.5 2.0 broadcast.323.clone
  60.6 213.6 %while.34 = (s32[]{:T(128)}, bf16[24,2,64,512]{3,2,1,0:T(8,128)(2,1)}, f32[24,512,2]{1,2,0:T(2,128)S(1)}, bf16[24,2,64,512]{3,2,1,0:T(8,128)(2,1)}, bf16[24,512,...) while((s32[]{:T(128)}, ...), condition=%wide.region_5.6_spmd, body=%wide.region_0.5_spmd.sunk | while | flops 179445760 | bytes 8181361 | solution.py:49
  66.8 2.0 fusion.233
  75.7 2.0 fusion.233
  274.3 39.2 %reduce-scatter.5.cloned.1.call-done = bf16[384,512]{1,0:T(8,128)(2,1)} async-done(((bf16[3072,512]{1,0:T(8,128)(2,1)}), bf16[384,512]{1,0:T(8,128)(2,1)}) %reduce-scatter.5.cloned.1.call-update) | async-done | bytes 393232 | tf_op jit(solution)/shard_map/reduce_scatter | solution.py:80
  313.5 26.8 %reduce-scatter.7.cloned.1.call-done = bf16[96,512]{1,0:T(8,128)(2,1)} async-done(((bf16[384,512]{1,0:T(8,128)(2,1)}), bf16[96,512]{1,0:T(8,128)(2,1)}) %reduce-scatter.7.cloned.1.call-update) | async-done | bytes 98320 | tf_op jit(solution)/shard_map/reduce_scatter | solution.py:81
  341.2 10.1 %all_gather.20 = bf16[384,512]{1,0:T(8,128)(2,1)} all-gather(bf16[96,512]{1,0:T(8,128)(2,1)S(1)} %fusion.177), channel_id=1, replica_groups=mesh['gx'=8,'gy'=4] {'gy'}, dimensions={0}, use_global_device_ids=true | all-gather | bytes 491520 | tf_op jit(solution)/shard_map/all_gather | solution.py:74
  351.4 38.3 %all-gather.6.cloned.1.call-done = bf16[3072,512]{1,0:T(8,128)(2,1)} async-done(((bf16[384,512]{1,0:T(8,128)(2,1)}), bf16[3072,512]{1,0:T(8,128)(2,1)}) %all-gather.6.cloned.1.call-update) | async-done | bytes 3145744 | tf_op jit(solution)/shard_map/all_gather | solution.py:75
  389.7 2.0 broadcast.323
  391.8 213.6 %while.35 = (s32[]{:T(128)}, bf16[24,2,64,512]{3,2,1,0:T(8,128)(2,1)}, f32[24,512,2]{1,2,0:T(2,128)S(1)}, bf16[24,2,64,512]{3,2,1,0:T(8,128)(2,1)}, bf16[24,512,...) while((s32[]{:T(128)}, ...), condition=%wide.region_13.14_spmd, body=%wide.region_8.13_spmd.sunk | while | flops 179445760 | bytes 8181361 | solution.py:49
  605.4 39.4 %reduce-scatter.9.cloned.1.call-done = bf16[384,512]{1,0:T(8,128)(2,1)} async-done(((bf16[3072,512]{1,0:T(8,128)(2,1)}), bf16[384,512]{1,0:T(8,128)(2,1)}) %reduce-scatter.9.cloned.1.call-update) | async-done | bytes 393232 | tf_op jit(solution)/shard_map/reduce_scatter | solution.py:80
  644.9 26.6 %reduce-scatter.11.cloned.1.call-done = bf16[96,512]{1,0:T(8,128)(2,1)} async-done(((bf16[384,512]{1,0:T(8,128)(2,1)}), bf16[96,512]{1,0:T(8,128)(2,1)}) %reduce-scatter.11.cloned.1.call-update) | async-done | bytes 98320 | tf_op jit(solution)/shard_map/reduce_scatter | solution.py:81
  673.2 10.1 %all_gather.22 = bf16[384,512]{1,0:T(8,128)(2,1)} all-gather(bf16[96,512]{1,0:T(8,128)(2,1)S(1)} %get-tuple-element.295), channel_id=1, replica_groups=mesh['gx'=8,'gy'=4] {'gy'}, dimensions={0}, use_global_device_ids=true | all-gather | bytes 491520 | tf_op jit(solution)/shard_map/all_gather | solution.py:74
  683.4 3.2 copy.25
  686.6 35.2 %all-gather.8.cloned.1.call-done = bf16[3072,512]{1,0:T(8,128)(2,1)} async-done(((bf16[384,512]{1,0:T(8,128)(2,1)}), bf16[3072,512]{1,0:T(8,128)(2,1)}) %all-gather.8.cloned.1.call-update) | async-done | bytes 3145744 | tf_op jit(solution)/shard_map/all_gather | solution.py:75
  721.7 77.4 %while.36 = (s32[]{:T(128)}, f32[24,512,2,64]{1,3,2,0:T(8,128)}, bf16[24,2,64,512]{3,2,1,0:T(8,128)(2,1)}, bf16[24,512,2,64]{1,3,2,0:T(8,128)(2,1)S(1)}, f32[24,...) while((s32[]{:T(128)}, f32[24,512,2,64]{1,3,2,0:T(8,128)}, bf16[24,2,64,512]{3,2,1,0:T(8,128)(2,1)}, ...), condition=%wide.region_19.20_spmd, body=%wide.region_16.19_spmd.sunk | while | flops 69993472 | bytes 1613401 | solution.py:63
  799.1 5.6 fusion.176
  804.6 4.6 copy.28
  (870 shorter events, 500.8 us)
Async XLA Ops:
  7.2 51.4 %all-gather.4.cloned.1.call-start = ((), (), s32[]{:S(2)}) async-start(), calls=%async_computation.4 | async-start | bytes 3538944 | tf_op jit(solution)/shard_map/all_gather | solution.py:75
  19.9 293.6 %reduce-scatter.5.cloned.1.call-start = ((), (), s32[]{:S(2)}) async-start(), calls=%async_computation.5 | async-start | bytes 3538944 | tf_op jit(solution)/shard_map/reduce_scatter | solution.py:80
  25.3 10.8 %slice-start = ((s8[6291456]{0:T(1024)(128)(4,1)}), s8[2097152]{0:T(1024)(128)(4,1)S(1)}, s32[]{:S(2)}) async-start(s8[6291456]{0:T(1024)(128)(4,1)} %bitcast.181), calls=%async_computation.11 | async-start | bytes 4194304
  31.0 5.1 slice-start.1
  36.1 7.1 copy-start.3
  274.2 66.1 %copy-start = (f32[96,512]{1,0:T(8,128)S(1)}, f32[96,512]{1,0:T(8,128)}, u32[]{:S(2)}) copy-start(f32[96,512]{1,0:T(8,128)} %param.18) | copy-start | bytes 589828
  274.2 66.1 %copy-start.1 = (f32[96,512]{1,0:T(8,128)S(1)}, f32[96,512]{1,0:T(8,128)}, u32[]{:S(2)}) copy-start(f32[96,512]{1,0:T(8,128)} %param.19) | copy-start | bytes 589828
  274.2 66.1 %reduce-scatter.7.cloned.1.call-start = ((), (), s32[]{:S(2)}) async-start(), calls=%async_computation.6 | async-start | bytes 491520 | tf_op jit(solution)/shard_map/reduce_scatter | solution.py:81
  313.5 76.3 %all-gather.6.cloned.1.call-start = ((), (), s32[]{:S(2)}) async-start(), calls=%async_computation.7 | async-start | bytes 3538944 | tf_op jit(solution)/shard_map/all_gather | solution.py:75
  351.4 293.4 %reduce-scatter.9.cloned.1.call-start = ((), (), s32[]{:S(2)}) async-start(), calls=%async_computation.8 | async-start | bytes 3538944 | tf_op jit(solution)/shard_map/reduce_scatter | solution.py:80
  605.3 66.2 %copy-start.2 = (bf16[96,512]{1,0:T(8,128)(2,1)S(1)}, bf16[96,512]{1,0:T(8,128)(2,1)}, u32[]{:S(2)}) copy-start(bf16[96,512]{1,0:T(8,128)(2,1)} %reduce-scatter.7.cloned.1.call-done) | copy-start | bytes 294916
  605.4 66.2 %reduce-scatter.11.cloned.1.call-start = ((), (), s32[]{:S(2)}) async-start(), calls=%async_computation.9 | async-start | bytes 491520 | tf_op jit(solution)/shard_map/reduce_scatter | solution.py:81
  644.8 76.9 %all-gather.8.cloned.1.call-start = ((), (), s32[]{:S(2)}) async-start(), calls=%async_computation.10 | async-start | bytes 3538944 | tf_op jit(solution)/shard_map/all_gather | solution.py:75
Sparse Core Ops, SparseCore 0:
  20.0 38.4 all-gather.3
  274.3 39.0 reduce-scatter.4
  316.2 24.0 reduce-scatter.6
  351.5 38.2 all-gather.5
  605.5 39.2 reduce-scatter.8
  647.4 24.0 reduce-scatter.10
  683.5 38.2 all-gather.7
where the time goes:
time: 824 us; the launch traced here: 816 us
  waiting for transfers between devices  221 us (27%)
  matrix products  217 us (26%)
  other arithmetic  189 us (23%)
  local copies, waits for them, and re-layouts  139 us (17%)
  blocking collectives  31.9 us (4%)
  between operations  14.2 us (2%)
    dot_general x96, matrix products, predict(): first = jnp.einsum('tgd,gdf->tgf', inputs, packed[:, :, :width])  154 us
    all_gather x3, waiting for transfers between devices, fetch(): whole = lax.all_gather(inner, 'gx', axis=0, tiled=True)  88.7 us
    reduce_scatter x2, waiting for transfers between devices, collect(): lax.psum_scatter(part.astype(jnp.bfloat16), 'gx', scatter_dimension=0, ti...  78.6 us
    squeeze x72, local copies, waits for them, and re-layouts, shard_gradient(): grads = lax.map(per_group, (inputs, targets, rates, packed, gains, biases))  65.7 us
    dot_general x120, matrix products, predict(): second = jnp.einsum('tgf,gdf->tgd', active, packed[:, :, width:])  63.1 us
    reduce_sum x48, other arithmetic, normalize(): centre = hidden - jnp.mean(hidden, axis=-1, keepdims=True)  55.6 us
    reduce_sum x48, other arithmetic, normalize(): return centre * lax.rsqrt(spread + 1e-06) * gain + bias  53.9 us
    reduce_scatter x2, waiting for transfers between devices, collect(): lax.psum_scatter(outer, 'gy', scatter_dimension=0, tiled=True)  53.4 us
  transfers between devices with their start and end apart: 7, of which 7 were waited for; matrix products, arithmetic and copies ran while one was open for 3% of the time, Pallas kernels for 0%

commit v1 on v0

v1 whole, which is shorter than its diff:
```python
import functools
import jax
import jax.numpy as jnp
from jax import lax
from jax.experimental import pallas as pl
from jax.experimental.pallas import tpu as pltpu

from jax.sharding import PartitionSpec as P

STEPS = 2

momentum_keep = 0.9
inner_rate = 0.5

KIND = jnp.float32
GELU_SCALE = 0.7978845608028654
GELU_CUBIC = 0.044715
NT = (((1,), (1,)), ((), ()))
NN = (((1,), (0,)), ((), ()))

def dot(a, b, dims=NN):
    return lax.dot_general(a, b, dims, preferred_element_type=jnp.float32)

def blocks(packed, size):
    width = packed.shape[1] // 2
    top, low = packed[:size], packed[size:]
    def diag(a, b):
        a = jnp.concatenate([a, jnp.zeros_like(a)], axis=1)
        b = jnp.concatenate([jnp.zeros_like(b), b], axis=1)
        return jnp.concatenate([a, b], axis=0).astype(jnp.bfloat16)
    def centred(a):
        a = a[:, width:].astype(jnp.float32)
        return a - jnp.mean(a, axis=0, keepdims=True)
    return diag(top[:, :width], low[:, :width]), diag(centred(top), centred(low))

def pair_mean(size):
    row = lax.broadcasted_iota(jnp.int32, (2 * size, 2 * size), 0) // size
    col = lax.broadcasted_iota(jnp.int32, (2 * size, 2 * size), 1) // size
    return jnp.where(row == col, 1.0 / size, 0.0).astype(jnp.bfloat16)

def activate(first, grad, kind):
    first = first.astype(kind)
    square = first * first
    inner = first * (square * jnp.asarray(GELU_SCALE * GELU_CUBIC, kind) + jnp.asarray(GELU_SCALE, kind))
    half = jnp.tanh(inner) * jnp.asarray(0.5, kind) + jnp.asarray(0.5, kind)
    active = first * half
    if not grad:
        return active.astype(jnp.bfloat16), None
    poly = square * jnp.asarray(6 * GELU_SCALE * GELU_CUBIC, kind) + jnp.asarray(2 * GELU_SCALE, kind)
    slope = half + active * (jnp.asarray(1.0, kind) - half) * poly
    return active.astype(jnp.bfloat16), slope

def grad_kernel(size, chunk, total, kind, key_ref, value_ref, rate_ref, packed_ref, gain_ref, bias_ref, out_ref,
                active_ref, dfirst_ref, dsecond_ref):
    tokens = key_ref.shape[0]
    width = packed_ref.shape[1] // 2
    first_w, second_w = blocks(packed_ref[...], size)
    mean = pair_mean(size)
    gain = gain_ref[0]
    bias = bias_ref[0]
    scaled = gain * (1.0 / total)
    for at in range(0, tokens, chunk):
        rows = pl.ds(at, chunk)
        keys = key_ref[rows, :]
        first = dot(keys, first_w)
        active, slope = activate(first, True, kind)
        active_ref[rows, :] = active
        centre = dot(active, second_w, NT)
        spread = dot((centre * centre).astype(jnp.bfloat16), mean)
        inverse = lax.rsqrt(spread + 1e-06)
        unit = centre * inverse
        target = value_ref[rows, :].astype(jnp.float32) - keys.astype(jnp.float32)
        error = unit * gain + (bias - target)
        dunit = error * (rate_ref[rows, :].astype(jnp.float32) * scaled)
        along = dot((dunit * unit).astype(jnp.bfloat16), mean)
        dsecond = (inverse * (dunit - unit * along)).astype(jnp.bfloat16)
        dsecond_ref[rows, :] = dsecond
        dactive = dot(dsecond, second_w)
        dfirst_ref[rows, :] = (dactive.astype(kind) * slope).astype(jnp.bfloat16)
    keys_t = key_ref[...].T
    dsecond_t = dsecond_ref[...].T
    for head in range(2):
        mine = slice(head * size, (head + 1) * size)
        cols = slice(head * width, (head + 1) * width)
        out_ref[mine, :width] = dot(keys_t[mine], dfirst_ref[:, cols]).astype(out_ref.dtype)
        second = dot(dsecond_t[mine], active_ref[:, cols])
        out_ref[mine, width:] = (second - jnp.mean(second, axis=0, keepdims=True)).astype(out_ref.dtype)

def apply_kernel(size, chunk, kind, query_ref, packed_ref, gain_ref, bias_ref, out_ref):
    tokens = query_ref.shape[0]
    first_w, second_w = blocks(packed_ref[...], size)
    mean = pair_mean(size)
    gain = gain_ref[0]
    bias = bias_ref[0]
    for at in range(0, tokens, chunk):
        rows = pl.ds(at, chunk)
        queries = query_ref[rows, :]
        first = dot(queries, first_w)
        active, _ = activate(first, False, kind)
        centre = dot(active, second_w, NT)
        spread = dot((centre * centre).astype(jnp.bfloat16), mean)
        unit = centre * lax.rsqrt(spread + 1e-06)
        out_ref[rows, :] = (queries.astype(jnp.float32) + unit * gain + bias).astype(out_ref.dtype)

def gradient(keys, values, rates, packed, gain, bias, total, size, chunk=128, kind=jnp.float32):
    tokens = keys.shape[0]
    rows, two = packed.shape
    pairs = rows // (2 * size)
    col = pl.BlockSpec((tokens, 2 * size), lambda i: (0, i))
    vec = pl.BlockSpec((1, 1, 2 * size), lambda i: (i, 0, 0))
    mat = pl.BlockSpec((2 * size, two), lambda i: (i, 0))
    return pl.pallas_call(
        functools.partial(grad_kernel, size, chunk, total, kind),
        out_shape=jax.ShapeDtypeStruct((rows, two), jnp.bfloat16),
        grid=(pairs,),
        in_specs=[col, col, col, mat, vec, vec],
        out_specs=mat,
        scratch_shapes=[pltpu.VMEM((tokens, two), jnp.bfloat16), pltpu.VMEM((tokens, two), jnp.bfloat16), pltpu.VMEM((tokens, 2 * size), jnp.bfloat16)],
        name="fast_gradient",
    )(keys, values, rates, packed, gain.reshape(pairs, 1, 2 * size), bias.reshape(pairs, 1, 2 * size))

def output(queries, packed, gain, bias, size, chunk=128, kind=jnp.float32):
    tokens = queries.shape[0]
    rows, two = packed.shape
    pairs = rows // (2 * size)
    col = pl.BlockSpec((tokens, 2 * size), lambda i: (0, i))
    vec = pl.BlockSpec((1, 1, 2 * size), lambda i: (i, 0, 0))
    mat = pl.BlockSpec((2 * size, two), lambda i: (i, 0))
    return pl.pallas_call(
        functools.partial(apply_kernel, size, chunk, kind),
        out_shape=jax.ShapeDtypeStruct((tokens, rows), jnp.bfloat16),
        grid=(pairs,),
        in_specs=[col, mat, vec, vec],
        out_specs=col,
        name="fast_output",
    )(queries, packed, gain.reshape(pairs, 1, 2 * size), bias.reshape(pairs, 1, 2 * size))


def fetch(fast):
    inner = lax.all_gather(fast.astype(jnp.bfloat16), "gy", axis=0, tiled=True)
    return lax.all_gather(inner, "gx", axis=0, tiled=True)


def collect(part):
    outer = lax.psum_scatter(part, "gx", scatter_dimension=0, tiled=True)
    return lax.psum_scatter(outer, "gy", scatter_dimension=0, tiled=True).astype(jnp.float32)


def per_device(
    key_rows, value_rows, query_rows, token_rates, fast_weights, momentum, norm_gain, norm_bias
):
    total = key_rows.shape[0] * lax.axis_size("gx") * lax.axis_size("gy")
    size = norm_gain.shape[1]
    rates = jnp.repeat(token_rates.astype(jnp.bfloat16), size, axis=1)
    fast, moment = (fast_weights, momentum)
    for step in range(STEPS):
        part = gradient(key_rows, value_rows, rates, fetch(fast), norm_gain, norm_bias, total, size, kind=KIND)
        grad = collect(part)
        moment = momentum_keep * moment + grad
        fast = fast - inner_rate * moment
    mixed = output(query_rows, fetch(fast), norm_gain, norm_bias, size, kind=KIND)
    return (mixed, fast, moment)


def solution(mesh):
    rows = P(("gx", "gy"), None)
    return jax.shard_map(
        per_device,
        mesh=mesh,
        in_specs=(rows,) * 6 + (P(), P()),
        out_specs=(rows,) * 3,
        check_vma=False,
    )
```

time: 824 us -> 476 us (0.58)
  matrix products: 217 us -> 0 us
  other arithmetic: 189 us -> 4.48 us
  Pallas kernels: 0 us -> 178 us
  local copies, waits for them, and re-layouts: 139 us -> 6.12 us
  waiting for transfers between devices: 221 us -> 241 us
    dot_general x216 -> x0, matrix products: 217 us -> none  [the longest x96 154 us: predict(): first = jnp.einsum('tgd,gdf->tgf', inputs, packed[:, :, :width])]
    pallas_call x0 -> x3, Pallas kernels: none -> 178 us  [the longest x2 141 us: gradient(): pl.pallas_call(functools.partial(grad_kernel, size, chunk, total, kind),...]
    reduce_sum x168 -> x0, other arithmetic: 113 us -> none  [the longest x48 55.6 us: normalize(): centre = hidden - jnp.mean(hidden, axis=-1, keepdims=True)]
    squeeze x72 -> x0, local copies, waits for them, and re-layouts: 65.7 us -> none  [shard_gradient(): grads = lax.map(per_group, (inputs, targets, rates, packed, gains, biases))]
    dynamic_update_slice x72 -> x0, other arithmetic: 52 us -> none  [the longest x48 32.5 us: shard_gradient(): grads = lax.map(per_group, (inputs, targets, rates, packed, gains, biases))]
    mul x72 -> x0, local copies, waits for them, and re-layouts: 50.7 us -> none  [normalize(): return centre * lax.rsqrt(spread + 1e-06) * gain + bias]
    all_gather x3, waiting for transfers between devices: 88.7 us -> 108 us  [fetch(): return lax.all_gather(inner, 'gx', axis=0, tiled=True)]
    transpose x2 -> x0, local copies, waits for them, and re-layouts: 11.1 us -> none  [grouped(): return jnp.moveaxis(array.reshape(array.shape[0], heads // 2, 2, -1), 1, 0)]
  transfers between devices with their start and end apart: 7 -> 7, of which waited for: 7 -> 7; matrix products, arithmetic and copies ran while one was open for 3% -> 1% of each run, Pallas kernels for 0% -> 0%
where the time goes in v1:
time: 476 us
  waiting for transfers between devices  241 us (51%)
  Pallas kernels  178 us (37%)
  blocking collectives  31.9 us (7%)
  between operations  14.1 us (3%)
  local copies, waits for them, and re-layouts  6.12 us (1%)
    pallas_call x2, Pallas kernels, gradient(): pl.pallas_call(functools.partial(grad_kernel, size, chunk, total, kind),...  141 us
    all_gather x3, waiting for transfers between devices, fetch(): return lax.all_gather(inner, 'gx', axis=0, tiled=True)  108 us
    reduce_scatter x2, waiting for transfers between devices, collect(): outer = lax.psum_scatter(part, 'gx', scatter_dimension=0, tiled=True)  78.8 us
    reduce_scatter x2, waiting for transfers between devices, collect(): lax.psum_scatter(outer, 'gy', scatter_dimension=0, tiled=True)  53.5 us
    pallas_call x1, Pallas kernels, output(): pl.pallas_call(functools.partial(apply_kernel, size, chunk, kind), out_sh...  36.8 us
    all_gather x3, blocking collectives, fetch(): inner = lax.all_gather(fast.astype(jnp.bfloat16), 'gy', axis=0, tiled=True)  31.9 us
  transfers between devices with their start and end apart: 7, of which 7 were waited for; matrix products, arithmetic and copies ran while one was open for 1% of the time, Pallas kernels for 0%

profile of v1, /device:TPU:0, one launch (start us, length us, event | category | flops | bytes accessed | tf_op | source)
XLA Modules:
  0.0 475.6 jit_solution(2952285323499966251)
XLA Ops:
  7.2 0.9 convert_element_type.19
  8.2 11.7 %all_gather.18 = bf16[384,512]{1,0:T(8,128)(2,1)} all-gather(bf16[96,512]{1,0:T(8,128)(2,1)S(1)} %convert_element_type.19), channel_id=1, replica_groups=mesh['gx'=8,'gy'=4] {'gy'}, dimensions={0}, use_global_device_ids=true | all-gather | bytes 491520 | tf_op jit(solution)/shard_map/all_gather | solution.py:140
  19.9 0.0 reduce-scatter.5.cloned.1.call-start
  19.9 1.4 reshape.20.gain_ref
  21.4 1.4 reshape.21.bias_ref
  22.8 0.9 convert_element_type.18
  23.7 0.3 broadcast_in_dim.3
  23.9 3.0 copy.12.rate_ref
  27.0 31.6 %all-gather.4.cloned.1.call-done.packed_ref = bf16[3072,512]{1,0:T(8,128)(2,1)} async-done(((bf16[384,512]{1,0:T(8,128)(2,1)}), bf16[3072,512]{1,0:T(8,128)(2,1)}) %all-gather.4.cloned.1.call-update) | async-done | bytes 3145744 | tf_op jit(solution)/shard_map/all_gather | solution.py:141
  58.5 70.6 %fast_gradient.2 = bf16[3072,512]{1,0:T(8,128)(2,1)} custom-call(bf16[512,3072]{1,0:T(8,128)(2,1)} %key_ref.3, bf16[512,3072]{1,0:T(8,128)(2,1)} %value_ref.3, bf16[512,3072]{1,0:T(8,128)(2,1)} %copy.12.rate_ref, bf16[3072,512]{1,0:T(8,128)(2,1)} %all-gather.4.cloned.1.call-done.packed_ref, f32[24,1,128]{2,1,0:T(1,128)} %reshape.20.gain_ref, ...), custom_call_target="tpu_custom_call" | custom-call | tf_op jit(solution)/shard_map/fast_gradient/pallas_call | solution.py:112
  129.2 0.0 reduce-scatter.7.cloned.1.call-start
  129.2 39.4 %reduce-scatter.5.cloned.1.call-done = bf16[384,512]{1,0:T(8,128)(2,1)} async-done(((bf16[3072,512]{1,0:T(8,128)(2,1)}), bf16[384,512]{1,0:T(8,128)(2,1)}) %reduce-scatter.5.cloned.1.call-update) | async-done | bytes 393232 | tf_op jit(solution)/shard_map/reduce_scatter | solution.py:145
  168.7 26.9 %reduce-scatter.7.cloned.1.call-done = bf16[96,512]{1,0:T(8,128)(2,1)} async-done(((bf16[384,512]{1,0:T(8,128)(2,1)}), bf16[96,512]{1,0:T(8,128)(2,1)}) %reduce-scatter.7.cloned.1.call-update) | async-done | bytes 98320 | tf_op jit(solution)/shard_map/reduce_scatter | solution.py:146
  195.6 0.9 fusion
  196.5 10.1 %all_gather.20 = bf16[384,512]{1,0:T(8,128)(2,1)} all-gather(bf16[96,512]{1,0:T(8,128)(2,1)S(1)} %fusion), channel_id=1, replica_groups=mesh['gx'=8,'gy'=4] {'gy'}, dimensions={0}, use_global_device_ids=true | all-gather | bytes 491520 | tf_op jit(solution)/shard_map/all_gather | solution.py:140
  206.6 0.0 reduce-scatter.9.cloned.1.call-start
  206.7 38.3 %all-gather.6.cloned.1.call-done.packed_ref = bf16[3072,512]{1,0:T(8,128)(2,1)} async-done(((bf16[384,512]{1,0:T(8,128)(2,1)}), bf16[3072,512]{1,0:T(8,128)(2,1)}) %all-gather.6.cloned.1.call-update) | async-done | bytes 3145744 | tf_op jit(solution)/shard_map/all_gather | solution.py:141
  245.0 70.6 %fast_gradient.3 = bf16[3072,512]{1,0:T(8,128)(2,1)} custom-call(bf16[512,3072]{1,0:T(8,128)(2,1)} %key_ref.3, bf16[512,3072]{1,0:T(8,128)(2,1)} %value_ref.3, bf16[512,3072]{1,0:T(8,128)(2,1)} %copy.12.rate_ref, bf16[3072,512]{1,0:T(8,128)(2,1)} %all-gather.6.cloned.1.call-done.packed_ref, f32[24,1,128]{2,1,0:T(1,128)} %reshape.20.gain_ref, ...), custom_call_target="tpu_custom_call" | custom-call | tf_op jit(solution)/shard_map/fast_gradient/pallas_call | solution.py:112
  315.7 39.4 %reduce-scatter.9.cloned.1.call-done = bf16[384,512]{1,0:T(8,128)(2,1)} async-done(((bf16[3072,512]{1,0:T(8,128)(2,1)}), bf16[384,512]{1,0:T(8,128)(2,1)}) %reduce-scatter.9.cloned.1.call-update) | async-done | bytes 393232 | tf_op jit(solution)/shard_map/reduce_scatter | solution.py:145
  355.2 26.6 %reduce-scatter.11.cloned.1.call-done = bf16[96,512]{1,0:T(8,128)(2,1)} async-done(((bf16[384,512]{1,0:T(8,128)(2,1)}), bf16[96,512]{1,0:T(8,128)(2,1)}) %reduce-scatter.11.cloned.1.call-update) | async-done | bytes 98320 | tf_op jit(solution)/shard_map/reduce_scatter | solution.py:146
  381.8 1.7 fusion.1
  383.5 10.1 %all_gather.22 = bf16[384,512]{1,0:T(8,128)(2,1)} all-gather(bf16[96,512]{1,0:T(8,128)(2,1)S(1)} %get-tuple-element.3), channel_id=1, replica_groups=mesh['gx'=8,'gy'=4] {'gy'}, dimensions={0}, use_global_device_ids=true | all-gather | bytes 491520 | tf_op jit(solution)/shard_map/all_gather | solution.py:140
  393.6 38.4 %all-gather.8.cloned.1.call-done.packed_ref = bf16[3072,512]{1,0:T(8,128)(2,1)} async-done(((bf16[384,512]{1,0:T(8,128)(2,1)}), bf16[3072,512]{1,0:T(8,128)(2,1)}) %all-gather.8.cloned.1.call-update) | async-done | bytes 3145744 | tf_op jit(solution)/shard_map/all_gather | solution.py:141
  432.0 36.8 %fast_output.1 = bf16[512,3072]{1,0:T(8,128)(2,1)} custom-call(bf16[512,3072]{1,0:T(8,128)(2,1)} %query_ref.1, bf16[3072,512]{1,0:T(8,128)(2,1)} %all-gather.8.cloned.1.call-done.packed_ref, f32[24,1,128]{2,1,0:T(1,128)} %reshape.20.gain_ref, f32[24,1,128]{2,1,0:T(1,128)} %reshape.21.bias_ref), custom_call_target="tpu_custom_call" | custom-call | tf_op jit(solution)/shard_map/fast_output/pallas_call | solution.py:129
  (17 shorter events, 0.3 us)
Async XLA Ops:
  7.2 51.4 %all-gather.4.cloned.1.call-start = ((), (), s32[]{:S(2)}) async-start(), calls=%async_computation.4 | async-start | bytes 3538944 | tf_op jit(solution)/shard_map/all_gather | solution.py:141
  19.9 148.7 %reduce-scatter.5.cloned.1.call-start = ((), (), s32[]{:S(2)}) async-start(), calls=%async_computation.5 | async-start | bytes 3538944 | tf_op jit(solution)/shard_map/reduce_scatter | solution.py:145
  129.2 66.4 %copy-start = (f32[96,512]{1,0:T(8,128)S(1)}, f32[96,512]{1,0:T(8,128)}, u32[]{:S(2)}) copy-start(f32[96,512]{1,0:T(8,128)} %param.12) | copy-start | bytes 589828
  129.2 66.4 %copy-start.1 = (f32[96,512]{1,0:T(8,128)S(1)}, f32[96,512]{1,0:T(8,128)}, u32[]{:S(2)}) copy-start(f32[96,512]{1,0:T(8,128)} %param.13) | copy-start | bytes 589828
  129.2 66.4 %reduce-scatter.7.cloned.1.call-start = ((), (), s32[]{:S(2)}) async-start(), calls=%async_computation.6 | async-start | bytes 491520 | tf_op jit(solution)/shard_map/reduce_scatter | solution.py:146
  168.7 76.3 %all-gather.6.cloned.1.call-start = ((), (), s32[]{:S(2)}) async-start(), calls=%async_computation.7 | async-start | bytes 3538944 | tf_op jit(solution)/shard_map/all_gather | solution.py:141
  206.6 148.5 %reduce-scatter.9.cloned.1.call-start = ((), (), s32[]{:S(2)}) async-start(), calls=%async_computation.8 | async-start | bytes 3538944 | tf_op jit(solution)/shard_map/reduce_scatter | solution.py:145
  315.6 66.2 %copy-start.2 = (bf16[96,512]{1,0:T(8,128)(2,1)S(1)}, bf16[96,512]{1,0:T(8,128)(2,1)}, u32[]{:S(2)}) copy-start(bf16[96,512]{1,0:T(8,128)(2,1)} %reduce-scatter.7.cloned.1.call-done) | copy-start | bytes 294916
  315.7 66.2 %reduce-scatter.11.cloned.1.call-start = ((), (), s32[]{:S(2)}) async-start(), calls=%async_computation.9 | async-start | bytes 491520 | tf_op jit(solution)/shard_map/reduce_scatter | solution.py:146
  355.1 76.9 %all-gather.8.cloned.1.call-start = ((), (), s32[]{:S(2)}) async-start(), calls=%async_computation.10 | async-start | bytes 3538944 | tf_op jit(solution)/shard_map/all_gather | solution.py:141
Sparse Core Ops, SparseCore 0:
  20.0 38.4 all-gather.3
  129.3 39.2 reduce-scatter.4
  171.4 24.0 reduce-scatter.6
  206.8 38.1 all-gather.5
  315.8 39.2 reduce-scatter.8
  357.7 24.0 reduce-scatter.10
  393.8 38.2 all-gather.7

commit v2 on v1

v2 whole, which is shorter than its diff:
```python
import functools

import jax
import jax.numpy as jnp
from jax import lax
from jax.experimental import pallas as pl
from jax.experimental.pallas import tpu as pltpu
from jax.sharding import PartitionSpec as P

STEPS = 2

momentum_keep = 0.9
inner_rate = 0.5

GELU_SCALE = 0.7978845608028654
GELU_CUBIC = 0.044715
NT = (((1,), (1,)), ((), ()))
NN = (((1,), (0,)), ((), ()))
BF = jnp.bfloat16
F32 = jnp.float32


def dot(a, b, dims=NN):
    return lax.dot_general(a, b, dims, preferred_element_type=F32)


def blocks(packed, size):
    width = packed.shape[1] // 2
    top, low = packed[:size], packed[size:]

    def diagonal(a, b):
        a = jnp.concatenate([a, jnp.zeros_like(a)], axis=1)
        b = jnp.concatenate([jnp.zeros_like(b), b], axis=1)
        return jnp.concatenate([a, b], axis=0).astype(BF)

    def centred(a):
        a = a[:, width:].astype(F32)
        return a - jnp.mean(a, axis=0, keepdims=True)

    return diagonal(top[:, :width], low[:, :width]), diagonal(centred(top), centred(low))


def pair_mean(size):
    row = lax.broadcasted_iota(jnp.int32, (2 * size, 2 * size), 0) // size
    col = lax.broadcasted_iota(jnp.int32, (2 * size, 2 * size), 1) // size
    return jnp.where(row == col, 1.0 / size, 0.0).astype(BF)


def activate(first, kind, slope_too):
    const = lambda x: jnp.asarray(x, kind)
    first = first.astype(kind)
    square = first * first
    inner = first * (square * const(GELU_SCALE * GELU_CUBIC) + const(GELU_SCALE))
    half = jnp.tanh(inner) * const(0.5) + const(0.5)
    active = first * half
    if not slope_too:
        return active.astype(BF)
    poly = square * const(6 * GELU_SCALE * GELU_CUBIC) + const(2 * GELU_SCALE)
    slope = half + (active - active * half) * poly
    return active.astype(BF), slope.astype(BF)


def grad_kernel(cfg, place_ref, *refs):
    (size, chunk, skew, kind, total) = cfg
    key_own, value_own, rate_own, key_far, value_far, rate_far = refs[:6]
    members = (len(refs) - 14) // 2
    weight_refs = refs[6 : 6 + members]
    gain_ref, bias_ref = refs[6 + members : 8 + members]
    out_refs = refs[8 + members : 8 + 2 * members]
    whole_ref, sums_ref, active_ref, dfirst_ref, dsecond_ref, slope_ref = refs[-6:]
    step = pl.program_id(0)
    mine = place_ref[2]
    groups, rows_own, two = weight_refs[0].shape
    width = two // 2
    span = members * rows_own

    @pl.when(step == 0)
    def _():
        for rel, w in enumerate(weight_refs):
            at = pl.multiple_of((mine ^ rel) * rows_own, rows_own)
            for g in range(groups):
                whole_ref[pl.ds(g * span + at, rows_own), :] = w[g]

    base = pl.multiple_of(step * 2 * size, 2 * size)
    first_w, second_w = blocks(whole_ref[pl.ds(base, 2 * size), :], size)
    mean = pair_mean(size)
    gain = gain_ref[0]
    bias = bias_ref[0]
    scaled = gain * (1.0 / total)
    tokens = key_own.shape[0]
    pieces = [(src, at) for src in ((key_own, value_own, rate_own, 0), (key_far, value_far, rate_far, tokens)) for at in range(0, tokens, chunk)]
    state = {}

    def s0(i):
        (key, value, rate, off), at = pieces[i]
        state[i, "first"] = dot(key[pl.ds(at, chunk), :], first_w)

    def s1(i):
        (key, value, rate, off), at = pieces[i]
        rows = pl.ds(off + at, chunk)
        active, slope = activate(state.pop((i, "first")), kind, True)
        active_ref[rows, :] = active
        slope_ref[rows, :] = slope
        state[i, "centre"] = dot(active, second_w, NT)

    def s2(i):
        centre = state[i, "centre"]
        state[i, "spread"] = dot((centre * centre).astype(BF), mean)

    def s3(i):
        (key, value, rate, off), at = pieces[i]
        rows = pl.ds(at, chunk)
        inverse = lax.rsqrt(state.pop((i, "spread")) + 1e-06)
        unit = state.pop((i, "centre")) * inverse
        target = value[rows, :].astype(F32) - key[rows, :].astype(F32)
        error = unit * gain + (bias - target)
        dunit = error * (rate[rows, :].astype(F32) * scaled)
        state[i, "along"] = dot((dunit * unit).astype(BF), mean)
        state[i, "rest"] = (inverse, unit, dunit)

    def s4(i):
        (key, value, rate, off), at = pieces[i]
        inverse, unit, dunit = state.pop((i, "rest"))
        dsecond = (inverse * (dunit - unit * state.pop((i, "along")))).astype(BF)
        dsecond_ref[pl.ds(off + at, chunk), :] = dsecond
        state[i, "dactive"] = dot(dsecond, second_w)

    def s5(i):
        (key, value, rate, off), at = pieces[i]
        rows = pl.ds(off + at, chunk)
        dfirst_ref[rows, :] = state.pop((i, "dactive")).astype(BF) * slope_ref[rows, :]

    stages = (s0, s1, s2, s3, s4, s5)
    n = len(pieces)
    if skew is None:
        for i in range(n):
            for s in stages: s(i)
    else:
        for t in range(n + max(skew)):
            for s, lag in list(zip(stages, skew))[::-1]:
                if 0 <= t - lag < n:
                    s(t - lag)
    dsecond_t = dsecond_ref[...].T
    key_t = [key_own[...].T, key_far[...].T]
    for head in range(2):
        part = slice(head * size, (head + 1) * size)
        cols = slice(head * width, (head + 1) * width)
        first = dot(key_t[0][part], dfirst_ref[:tokens, cols]) + dot(key_t[1][part], dfirst_ref[tokens:, cols])
        second = dot(dsecond_t[part], active_ref[:, cols])
        second = second - jnp.mean(second, axis=0, keepdims=True)
        sums_ref[pl.ds(base + head * size, size), :width] = first.astype(BF)
        sums_ref[pl.ds(base + head * size, size), width:] = second.astype(BF)

    @pl.when(step == pl.num_programs(0) - 1)
    def _():
        for rel, o in enumerate(out_refs):
            at = pl.multiple_of((mine ^ rel) * rows_own, rows_own)
            for g in range(groups):
                o[g] = sums_ref[pl.ds(g * span + at, rows_own), :]


def gradient(place, own, far, weights, gain, bias, total, size, lag, chunk=128, skew=None, kind=BF, flags=None):
    tokens = own[0].shape[0]
    groups, rows_own, two = weights[0].shape
    members = len(weights)
    per = members * rows_own // (2 * size)
    zof = lambda i, place: place[0] ^ (i // per + lag)
    own_spec = pl.BlockSpec((tokens, 2 * size), lambda i, place: (0, (zof(i, place) * 2 + place[1]) * per + i % per))
    far_spec = pl.BlockSpec((tokens, 2 * size), lambda i, place: (0, zof(i, place) * per + i % per))
    vec = pl.BlockSpec((1, 1, 2 * size), lambda i, place: ((zof(i, place) * 2 + place[1]) * per + i % per, 0, 0))
    mat = pl.BlockSpec((groups, rows_own, two), lambda i, place: (0, 0, 0))
    out = jax.ShapeDtypeStruct((groups, rows_own, two), BF)
    cfg = (size, chunk, skew, kind, total)
    rows = groups * members * rows_own
    pairs = gain.size // (2 * size)
    return pl.pallas_call(
        functools.partial(grad_kernel, cfg),
        out_shape=[out] * members,
        grid_spec=pltpu.PrefetchScalarGridSpec(
            num_scalar_prefetch=1,
            grid=(groups * per,),
            in_specs=[own_spec] * 3 + [far_spec] * 2 + [own_spec] + [mat] * members + [vec, vec],
            out_specs=[mat] * members,
            scratch_shapes=[
                pltpu.VMEM((rows, two), BF),
                pltpu.VMEM((rows, two), BF),
                pltpu.VMEM((2 * tokens, two), BF),
                pltpu.VMEM((2 * tokens, two), BF),
                pltpu.VMEM((2 * tokens, 2 * size), BF),
                pltpu.VMEM((2 * tokens, two), BF),
            ],
        ),
        compiler_params=pltpu.CompilerParams(flags=flags) if flags else None,
        name="fast_gradient",
    )(place, *own, *far, *weights, gain.reshape(pairs, 1, 2 * size), bias.reshape(pairs, 1, 2 * size))


def output_kernel(size, chunk, kind, place_ref, query_ref, weight_ref, gain_ref, bias_ref, *refs):
    out_ref, whole_ref = refs[-2:]
    step = pl.program_id(0)
    mine = place_ref[2]
    members, groups, rows_own, _ = weight_ref.shape

    @pl.when(step == 0)
    def _():
        for rel in range(members):
            at = pl.multiple_of((mine ^ rel) * rows_own, rows_own)
            for g in range(groups):
                whole_ref[pl.ds(g * members * rows_own + at, rows_own), :] = weight_ref[rel, g]

    base = pl.multiple_of(step * 2 * size, 2 * size)
    first_w, second_w = blocks(whole_ref[pl.ds(base, 2 * size), :], size)
    mean = pair_mean(size)
    gain = gain_ref[0]
    bias = bias_ref[0]
    for at in range(0, query_ref.shape[0], chunk):
        rows = pl.ds(at, chunk)
        queries = query_ref[rows, :]
        active = activate(dot(queries, first_w), kind, False)
        centre = dot(active, second_w, NT)
        spread = dot((centre * centre).astype(BF), mean)
        unit = centre * lax.rsqrt(spread + 1e-06)
        out_ref[rows, :] = (queries.astype(F32) + unit * gain + bias).astype(BF)


def output(place, queries, weights, gain, bias, before, size, lag, flip, chunk=512, kind=BF):
    tokens, model = queries.shape
    members, groups, rows_own, two = weights.shape
    per = members * rows_own // (2 * size)
    pairs = gain.size // (2 * size)
    column = lambda i, place: ((place[0] ^ (i // per + lag)) * 2 + (place[1] ^ flip)) * per + i % per
    col = pl.BlockSpec((tokens, 2 * size), lambda i, place: (0, column(i, place)))
    vec = pl.BlockSpec((1, 1, 2 * size), lambda i, place: (column(i, place), 0, 0))
    mat = pl.BlockSpec((members, groups, rows_own, two), lambda i, place: (0, 0, 0, 0))
    more = [] if before is None else [before]
    return pl.pallas_call(
        functools.partial(output_kernel, size, chunk, kind),
        out_shape=jax.ShapeDtypeStruct((tokens, model), BF),
        grid_spec=pltpu.PrefetchScalarGridSpec(
            num_scalar_prefetch=1,
            grid=(groups * per,),
            in_specs=[col, mat, vec, vec] + [pl.BlockSpec(memory_space=pl.ANY)] * len(more),
            out_specs=col,
            scratch_shapes=[pltpu.VMEM((groups * members * rows_own, two), BF)],
        ),
        input_output_aliases={5: 0} if more else {},
        name="fast_output",
    )(place, queries, weights, gain.reshape(pairs, 1, 2 * size), bias.reshape(pairs, 1, 2 * size), *more)


def pick_kernel(place_ref, *refs):
    half = len(refs) // 2
    for source, target in zip(refs[:half], refs[half:]):
        target[...] = source[...]


def pick(place, arrays, groups, flip):
    tokens, model = arrays[0].shape
    wide = model // (2 * groups)
    return pl.pallas_call(
        pick_kernel,
        out_shape=[jax.ShapeDtypeStruct((tokens, groups * wide), a.dtype) for a in arrays],
        grid_spec=pltpu.PrefetchScalarGridSpec(
            num_scalar_prefetch=1,
            grid=(groups,),
            in_specs=[pl.BlockSpec((tokens, wide), lambda i, place: (0, 2 * i + (place[1] ^ flip)))] * len(arrays),
            out_specs=[pl.BlockSpec((tokens, wide), lambda i, place: (0, i))] * len(arrays),
        ),
        name="pick",
    )(place, *arrays)


def core_swap(x):
    n = lax.axis_size("gx")
    return lax.ppermute(x, "gx", [(i, i ^ 1) for i in range(n)])


def z_shift(x, s):
    n = lax.axis_size("gx")
    return lax.ppermute(x, "gx", [(i, i ^ (2 * s)) for i in range(n)])


def plane_shift(x, s):
    n = lax.axis_size("gy")
    return lax.ppermute(x, "gy", [(i, i ^ s) for i in range(n)])


def fetch(fast, groups, members, chunks):
    narrow = fast.astype(BF)
    held = [narrow] + [z_shift(narrow, s) for s in range(1, groups)]
    return [(lambda mine: [mine] + [plane_shift(mine, s) for s in range(1, members)])(jnp.stack(held[at : at + count])) for at, count in chunks]


def collect(parts, groups, members, chunks):
    sums = []
    for part, (at, count) in zip(parts, chunks):
        arrived = [plane_shift(part[s], s) for s in range(1, members)]
        for g in range(count):
            sums.append(sum([a[g].astype(F32) for a in [part[0]] + arrived]))
    total = sums[0]
    for s in range(1, groups):
        total = total + z_shift(sums[s].astype(BF), s).astype(F32)
    return total


def per_device(
    key_rows, value_rows, query_rows, token_rates, fast_weights, momentum, norm_gain, norm_bias
):
    size = norm_gain.shape[1]
    groups, members = lax.axis_size("gx") // 2, lax.axis_size("gy")
    total = key_rows.shape[0] * 2 * groups * members
    gx = lax.axis_index("gx")
    place = jnp.stack([gx // 2, gx % 2, lax.axis_index("gy")]).astype(jnp.int32)
    chunks = [(0, groups // 2), (groups // 2, groups - groups // 2)]
    fast, moment = (fast_weights, momentum)
    spread = lambda rates: jnp.repeat(rates.astype(BF), size, axis=1)
    weights = fetch(fast, groups, members, chunks)
    key_send, value_send = pick(place, (key_rows, value_rows), groups, 1)
    far = (core_swap(key_send), core_swap(value_send), spread(core_swap(token_rates)))
    own = (key_rows, value_rows, spread(token_rates))
    for step in range(STEPS):
        parts = [
            gradient(place, own, far, w, norm_gain, norm_bias, total, size, at, chunk=512)
            for w, (at, count) in zip(weights, chunks)
        ]
        grad = collect(parts, groups, members, chunks)
        moment = momentum_keep * moment + grad
        fast = fast - inner_rate * moment
        weights = fetch(fast, groups, members, chunks)
    mixed = None
    whole = [jnp.stack(w) for w in weights]
    twin = [core_swap(w) for w in whole]
    for flip, ws in enumerate((whole, twin)):
        for w, (at, count) in zip(ws, chunks):
            mixed = output(place, query_rows, w, norm_gain, norm_bias, mixed, size, at, flip)
    return (mixed, fast, moment)


def plain_grad_kernel(size, chunk, total, kind, key_ref, value_ref, rate_ref, packed_ref, gain_ref, bias_ref, out_ref,
                active_ref, dfirst_ref, dsecond_ref):
    tokens = key_ref.shape[0]
    width = packed_ref.shape[1] // 2
    first_w, second_w = blocks(packed_ref[...], size)
    mean = pair_mean(size)
    gain = gain_ref[0]
    bias = bias_ref[0]
    scaled = gain * (1.0 / total)
    for at in range(0, tokens, chunk):
        rows = pl.ds(at, chunk)
        keys = key_ref[rows, :]
        first = dot(keys, first_w)
        active, slope = activate(first, kind, True)
        active_ref[rows, :] = active
        centre = dot(active, second_w, NT)
        spread = dot((centre * centre).astype(jnp.bfloat16), mean)
        inverse = lax.rsqrt(spread + 1e-06)
        unit = centre * inverse
        target = value_ref[rows, :].astype(jnp.float32) - keys.astype(jnp.float32)
        error = unit * gain + (bias - target)
        dunit = error * (rate_ref[rows, :].astype(jnp.float32) * scaled)
        along = dot((dunit * unit).astype(jnp.bfloat16), mean)
        dsecond = (inverse * (dunit - unit * along)).astype(jnp.bfloat16)
        dsecond_ref[rows, :] = dsecond
        dactive = dot(dsecond, second_w)
        dfirst_ref[rows, :] = (dactive * slope.astype(F32)).astype(jnp.bfloat16)
    keys_t = key_ref[...].T
    dsecond_t = dsecond_ref[...].T
    for head in range(2):
        mine = slice(head * size, (head + 1) * size)
        cols = slice(head * width, (head + 1) * width)
        out_ref[mine, :width] = dot(keys_t[mine], dfirst_ref[:, cols]).astype(out_ref.dtype)
        second = dot(dsecond_t[mine], active_ref[:, cols])
        out_ref[mine, width:] = (second - jnp.mean(second, axis=0, keepdims=True)).astype(out_ref.dtype)

def plain_apply_kernel(size, chunk, kind, query_ref, packed_ref, gain_ref, bias_ref, out_ref):
    tokens = query_ref.shape[0]
    first_w, second_w = blocks(packed_ref[...], size)
    mean = pair_mean(size)
    gain = gain_ref[0]
    bias = bias_ref[0]
    for at in range(0, tokens, chunk):
        rows = pl.ds(at, chunk)
        queries = query_ref[rows, :]
        first = dot(queries, first_w)
        active = activate(first, kind, False)
        centre = dot(active, second_w, NT)
        spread = dot((centre * centre).astype(jnp.bfloat16), mean)
        unit = centre * lax.rsqrt(spread + 1e-06)
        out_ref[rows, :] = (queries.astype(jnp.float32) + unit * gain + bias).astype(out_ref.dtype)

def plain_gradient(keys, values, rates, packed, gain, bias, total, size, chunk=128, kind=jnp.float32):
    tokens = keys.shape[0]
    rows, two = packed.shape
    pairs = rows // (2 * size)
    col = pl.BlockSpec((tokens, 2 * size), lambda i: (0, i))
    vec = pl.BlockSpec((1, 1, 2 * size), lambda i: (i, 0, 0))
    mat = pl.BlockSpec((2 * size, two), lambda i: (i, 0))
    return pl.pallas_call(
        functools.partial(plain_grad_kernel, size, chunk, total, kind),
        out_shape=jax.ShapeDtypeStruct((rows, two), jnp.bfloat16),
        grid=(pairs,),
        in_specs=[col, col, col, mat, vec, vec],
        out_specs=mat,
        scratch_shapes=[pltpu.VMEM((tokens, two), jnp.bfloat16), pltpu.VMEM((tokens, two), jnp.bfloat16), pltpu.VMEM((tokens, 2 * size), jnp.bfloat16)],
        name="plain_gradient",
    )(keys, values, rates, packed, gain.reshape(pairs, 1, 2 * size), bias.reshape(pairs, 1, 2 * size))

def plain_output(queries, packed, gain, bias, size, chunk=128, kind=jnp.float32):
    tokens = queries.shape[0]
    rows, two = packed.shape
    pairs = rows // (2 * size)
    col = pl.BlockSpec((tokens, 2 * size), lambda i: (0, i))
    vec = pl.BlockSpec((1, 1, 2 * size), lambda i: (i, 0, 0))
    mat = pl.BlockSpec((2 * size, two), lambda i: (i, 0))
    return pl.pallas_call(
        functools.partial(plain_apply_kernel, size, chunk, kind),
        out_shape=jax.ShapeDtypeStruct((tokens, rows), jnp.bfloat16),
        grid=(pairs,),
        in_specs=[col, mat, vec, vec],
        out_specs=col,
        name="plain_output",
    )(queries, packed, gain.reshape(pairs, 1, 2 * size), bias.reshape(pairs, 1, 2 * size))


def plain_device(
    key_rows, value_rows, query_rows, token_rates, fast_weights, momentum, norm_gain, norm_bias
):
    size = norm_gain.shape[1]
    total = key_rows.shape[0] * lax.axis_size("gx") * lax.axis_size("gy")
    place = jnp.zeros((3,), jnp.int32)
    rates = jnp.repeat(token_rates.astype(BF), size, axis=1)
    fast, moment = (fast_weights, momentum)

    def whole(fast):
        inner = lax.all_gather(fast.astype(BF), "gy", axis=0, tiled=True)
        return lax.all_gather(inner, "gx", axis=0, tiled=True)

    for step in range(STEPS):
        part = plain_gradient(key_rows, value_rows, rates, whole(fast), norm_gain, norm_bias, total, size)
        outer = lax.psum_scatter(part, "gx", scatter_dimension=0, tiled=True)
        grad = lax.psum_scatter(outer, "gy", scatter_dimension=0, tiled=True).astype(F32)
        moment = momentum_keep * moment + grad
        fast = fast - inner_rate * moment
    mixed = plain_output(query_rows, whole(fast), norm_gain, norm_bias, size)
    return (mixed, fast, moment)


def power_of_two(n):
    return n > 0 and n & (n - 1) == 0


def solution(mesh):
    rows = P(("gx", "gy"), None)

    def run(*args):
        rows_own = args[0].shape[1] // mesh.size
        size = args[6].shape[1]
        gx, gy = mesh.shape["gx"], mesh.shape["gy"]
        paired = gx % 4 == 0 and power_of_two(gx) and power_of_two(gy)
        even = rows_own % 32 == 0 and (rows_own * gy) % (2 * size) == 0
        body = per_device if paired and even else plain_device
        return jax.shard_map(
            body,
            mesh=mesh,
            in_specs=(rows,) * 6 + (P(), P()),
            out_specs=(rows,) * 3,
            check_vma=False,
        )(*args)

    return run
```

time: 476 us -> 235 us (0.49)
  waiting for transfers between devices: 241 us -> 45 us
  Pallas kernels: 178 us -> 103 us
  starting transfers between devices: 0.28 us -> 55.8 us
  blocking collectives: 31.9 us -> 0 us
  local copies, waits for them, and re-layouts: 6.12 us -> 23.1 us
  between operations: 14.1 us -> 0.93 us
    reduce_scatter x4 -> x0, waiting for transfers between devices: 132 us -> none  [the longest x2 78.8 us: collect(): outer = lax.psum_scatter(part, 'gx', scatter_dimension=0, tiled=True)]
    all_gather x3 -> x0, waiting for transfers between devices: 108 us -> none  [fetch(): return lax.all_gather(inner, 'gx', axis=0, tiled=True)]
    pallas_call x3 -> x9, Pallas kernels: 178 us -> 103 us  [the longest x4 68 us: gradient(): pl.pallas_call(functools.partial(grad_kernel, cfg), out_shape=[out] * mem...]
    ppermute x0 -> x50, starting transfers between devices: none -> 55.8 us  [the longest x30 36.5 us: plane_shift(): return lax.ppermute(x, 'gy', [(i, i ^ s) for i in range(n)])]
    ppermute x0 -> x50, waiting for transfers between devices: none -> 45 us  [the longest x15 26 us: z_shift(): return lax.ppermute(x, 'gx', [(i, i ^ 2 * s) for i in range(n)])]
    all_gather x3 -> x0, blocking collectives: 31.9 us -> none  [fetch(): inner = lax.all_gather(fast.astype(jnp.bfloat16), 'gy', axis=0, tiled=True)]
    reshape x1 -> x2, local copies, waits for them, and re-layouts: 3.03 us -> 9.33 us  [per_device(): spread = lambda rates: jnp.repeat(rates.astype(BF), size, axis=1)]
    unnamed x6 -> x42, local copies, waits for them, and re-layouts: 0.01 us -> 6.3 us
  transfers between devices with their start and end apart: 7 -> 50, of which waited for: 7 -> 24; matrix products, arithmetic and copies ran while one was open for 1% -> 9% of each run, Pallas kernels for 0% -> 39%
where the time goes in v2:
time: 235 us; the launch traced here: 234 us
  Pallas kernels  103 us (44%)
  starting transfers between devices  55.8 us (24%)
  waiting for transfers between devices  45 us (19%)
  local copies, waits for them, and re-layouts  23.1 us (10%)
  other arithmetic  6.55 us (3%)
    pallas_call x4, Pallas kernels, gradient(): pl.pallas_call(functools.partial(grad_kernel, cfg), out_shape=[out] * mem...  68 us
    ppermute x30, starting transfers between devices, plane_shift(): return lax.ppermute(x, 'gy', [(i, i ^ s) for i in range(n)])  36.5 us
    pallas_call x4, Pallas kernels, output(): pl.pallas_call(functools.partial(output_kernel, size, chunk, kind), out_s...  29.6 us
    ppermute x15, waiting for transfers between devices, z_shift(): return lax.ppermute(x, 'gx', [(i, i ^ 2 * s) for i in range(n)])  26 us
    ppermute x30, waiting for transfers between devices, plane_shift(): return lax.ppermute(x, 'gy', [(i, i ^ s) for i in range(n)])  19 us
    ppermute x15, starting transfers between devices, z_shift(): return lax.ppermute(x, 'gx', [(i, i ^ 2 * s) for i in range(n)])  18.7 us
    reshape x2, local copies, waits for them, and re-layouts, per_device(): spread = lambda rates: jnp.repeat(rates.astype(BF), size, axis=1)  9.33 us
    unnamed x42, local copies, waits for them, and re-layouts  6.3 us
  transfers between devices with their start and end apart: 50, of which 24 were waited for; matrix products, arithmetic and copies ran while one was open for 9% of the time, Pallas kernels for 39%

profile of v2, /device:TPU:0, one launch (start us, length us, event | category | flops | bytes accessed | tf_op | source)
XLA Modules:
  0.0 234.2 jit_solution(16587659174148251092)
XLA Ops:
  1.3 5.1 %pick.1 = (bf16[512,1536]{1,0:T(8,128)(2,1)}, bf16[512,1536]{1,0:T(8,128)(2,1)}) custom-call(s32[3]{0:T(128)} %pad_add_fusion.place_ref, bf16[512,3072]{1,0:T(8,128)(2,1)} %refs_0_.9, bf16[512,3072]{1,0:T(8,128)(2,1)} %refs_1_.9), custom_call_target="tpu_custom_call" | custom-call | tf_op jit(solution)/shard_map/pick/pallas_call | solution.py:260
  6.9 5.1 %collective-permute-start.12 = (bf16[96,512]{1,0:T(8,128)(2,1)S(1)}, bf16[96,512]{1,0:T(8,128)(2,1)S(1)}, u32[]{:S(2)}, u32[]{:S(2)}) collective-permute-start(bf16[96,512]{1,0:T(8,128)(2,1)S(1)} %convert_element_type.169), channel_id=1, source_target_pairs={{0,24},{4,28},{8,16},{12,20},{16,8},{20,12},{24,0},{28,4},{1,25},{... | collective-permute-start | bytes 294920 | tf_op jit(solution)/shard_map/ppermute | solution.py:280
  12.7 3.1 %collective-permute-done.12 = bf16[96,512]{1,0:T(8,128)(2,1)S(1)} collective-permute-done((bf16[96,512]{1,0:T(8,128)(2,1)S(1)}, bf16[96,512]{1,0:T(8,128)(2,1)S(1)}, u32[]{:S(2)}, u32[]{:S(2)}) %collective-permute-start.12) | collective-permute-done | bytes 98336 | tf_op jit(solution)/shard_map/ppermute | solution.py:280
  15.8 4.7 %collective-permute-done.11 = bf16[96,512]{1,0:T(8,128)(2,1)S(1)} collective-permute-done((bf16[96,512]{1,0:T(8,128)(2,1)S(1)}, bf16[96,512]{1,0:T(8,128)(2,1)S(1)}, u32[]{:S(2)}, u32[]{:S(2)}) %collective-permute-start.11) | collective-permute-done | bytes 98336 | tf_op jit(solution)/shard_map/ppermute | solution.py:280
  24.8 4.4 %collective-permute-done.13.refs_7_ = bf16[2,96,512]{2,1,0:T(8,128)(2,1)} collective-permute-done((bf16[2,96,512]{2,1,0:T(8,128)(2,1)}, bf16[2,96,512]{2,1,0:T(8,128)(2,1)}, u32[]{:S(2)}, u32[]{:S(2)}) %collective-permute-start.13) | collective-permute-done | bytes 196640 | tf_op jit(solution)/shard_map/ppermute | solution.py:285
  32.7 4.7 %copy.16.refs_2_ = bf16[512,3072]{1,0:T(8,128)(2,1)} copy(bf16[512,3072]{0,1:T(8,128)(2,1)} %bitcast.58) | data formatting | bytes 6291456 | tf_op jit(solution)/shard_map/reshape | solution.py:316
  40.2 2.7 %broadcast_in_dim.7 = bf16[512,48,64]{0,2,1:T(8,128)(2,1)} broadcast(bf16[512,48]{0,1:T(8,128)(2,1)} %copy-done.20), dimensions={0,1} | broadcast | bytes 3194880 | tf_op jit(solution)/shard_map/broadcast_in_dim | solution.py:316
  43.0 4.6 %copy.17.refs_5_ = bf16[512,3072]{1,0:T(8,128)(2,1)} copy(bf16[512,3072]{0,1:T(8,128)(2,1)} %bitcast.59) | data formatting | bytes 6291456 | tf_op jit(solution)/shard_map/reshape | solution.py:316
  51.9 16.9 %fast_gradient.5 = (bf16[2,96,512]{2,1,0:T(8,128)(2,1)}, bf16[2,96,512]{2,1,0:T(8,128)(2,1)}, bf16[2,96,512]{2,1,0:T(8,128)(2,1)}, bf16[2,96,512]{2,1,0:T(8,128)(2,1)}) custom-call(s32[3]{0:T(128)} %pad_add_fusion.place_ref, bf16[512,3072]{1,0:T(8,128)(2,1)} %refs_0_.9, bf16[512,3072]{1,0:T(8,128)(2,1)} %refs_1_.9, bf16[512,3072]{1,0:T(8,128)(2,1)} %copy.16.refs_2_, ...), custom_call_target="tpu_custom_call" | custom-call | tf_op jit(solution)/shard_map/fast_gradient/pallas_call | solution.py:176
  68.8 2.6 %collective-permute-start.18 = (bf16[2,96,512]{2,1,0:T(8,128)(2,1)}, bf16[2,96,512]{2,1,0:T(8,128)(2,1)S(1)}, u32[]{:S(2)}, u32[]{:S(2)}) collective-permute-start(bf16[2,96,512]{2,1,0:T(8,128)(2,1)} %get-tuple-element.30), channel_id=1, source_target_pairs={{0,3},{1,2},{2,1},{3,0},{4,7},{5,6},{6,5},{7,4},{8,11},{9,10},{10,... | collective-permute-start | bytes 589832 | tf_op jit(solution)/shard_map/ppermute | solution.py:285
  72.4 16.9 %fast_gradient.4 = (bf16[2,96,512]{2,1,0:T(8,128)(2,1)}, bf16[2,96,512]{2,1,0:T(8,128)(2,1)}, bf16[2,96,512]{2,1,0:T(8,128)(2,1)}, bf16[2,96,512]{2,1,0:T(8,128)(2,1)}) custom-call(s32[3]{0:T(128)} %pad_add_fusion.place_ref, bf16[512,3072]{1,0:T(8,128)(2,1)} %refs_0_.9, bf16[512,3072]{1,0:T(8,128)(2,1)} %refs_1_.9, bf16[512,3072]{1,0:T(8,128)(2,1)} %copy.16.refs_2_, ...), custom_call_target="tpu_custom_call" | custom-call | tf_op jit(solution)/shard_map/fast_gradient/pallas_call | solution.py:176
  89.4 2.6 %collective-permute-start.9 = (bf16[2,96,512]{2,1,0:T(8,128)(2,1)}, bf16[2,96,512]{2,1,0:T(8,128)(2,1)S(1)}, u32[]{:S(2)}, u32[]{:S(2)}) collective-permute-start(bf16[2,96,512]{2,1,0:T(8,128)(2,1)} %get-tuple-element.26), channel_id=1, source_target_pairs={{0,3},{1,2},{2,1},{3,0},{4,7},{5,6},{6,5},{7,4},{8,11},{9,10},{10,... | collective-permute-start | bytes 589832 | tf_op jit(solution)/shard_map/ppermute | solution.py:285
  93.0 2.5 %collective-permute-start.20 = (bf16[96,512]{1,0:T(8,128)(2,1)S(1)}, bf16[96,512]{1,0:T(8,128)(2,1)S(1)}, u32[]{:S(2)}, u32[]{:S(2)}) collective-permute-start(bf16[96,512]{1,0:T(8,128)(2,1)S(1)} %get-tuple-element.47), channel_id=1, source_target_pairs={{0,24},{4,28},{8,16},{12,20},{16,8},{20,12},{24,0},{28,4},{1,25},{... | collective-permute-start | bytes 294920 | tf_op jit(solution)/shard_map/ppermute | solution.py:280
  101.9 3.1 %collective-permute-done.10 = bf16[96,512]{1,0:T(8,128)(2,1)S(1)} collective-permute-done((bf16[96,512]{1,0:T(8,128)(2,1)S(1)}, bf16[96,512]{1,0:T(8,128)(2,1)S(1)}, u32[]{:S(2)}, u32[]{:S(2)}) %collective-permute-start.10) | collective-permute-done | bytes 98336 | tf_op jit(solution)/shard_map/ppermute | solution.py:280
  107.6 3.0 %collective-permute-start.21 = (bf16[96,512]{1,0:T(8,128)(2,1)S(1)}, bf16[96,512]{1,0:T(8,128)(2,1)S(1)}, u32[]{:S(2)}, u32[]{:S(2)}) collective-permute-start(bf16[96,512]{1,0:T(8,128)(2,1)S(1)} %get-tuple-element.42), channel_id=1, source_target_pairs={{0,8},{4,12},{8,0},{12,4},{16,24},{20,28},{24,16},{28,20},{1,9},{5... | collective-permute-start | bytes 294920 | tf_op jit(solution)/shard_map/ppermute | solution.py:280
  126.8 17.0 %fast_gradient.7 = (bf16[2,96,512]{2,1,0:T(8,128)(2,1)}, bf16[2,96,512]{2,1,0:T(8,128)(2,1)}, bf16[2,96,512]{2,1,0:T(8,128)(2,1)}, bf16[2,96,512]{2,1,0:T(8,128)(2,1)}) custom-call(s32[3]{0:T(128)} %pad_add_fusion.place_ref, bf16[512,3072]{1,0:T(8,128)(2,1)} %refs_0_.9, bf16[512,3072]{1,0:T(8,128)(2,1)} %refs_1_.9, bf16[512,3072]{1,0:T(8,128)(2,1)} %copy.16.refs_2_, ...), custom_call_target="tpu_custom_call" | custom-call | tf_op jit(solution)/shard_map/fast_gradient/pallas_call | solution.py:176
  143.8 2.3 collective-permute-start.36
  148.7 17.1 %fast_gradient.6 = (bf16[2,96,512]{2,1,0:T(8,128)(2,1)}, bf16[2,96,512]{2,1,0:T(8,128)(2,1)}, bf16[2,96,512]{2,1,0:T(8,128)(2,1)}, bf16[2,96,512]{2,1,0:T(8,128)(2,1)}) custom-call(s32[3]{0:T(128)} %pad_add_fusion.place_ref, bf16[512,3072]{1,0:T(8,128)(2,1)} %refs_0_.9, bf16[512,3072]{1,0:T(8,128)(2,1)} %refs_1_.9, bf16[512,3072]{1,0:T(8,128)(2,1)} %copy.16.refs_2_, ...), custom_call_target="tpu_custom_call" | custom-call | tf_op jit(solution)/shard_map/fast_gradient/pallas_call | solution.py:176
  176.7 4.8 %collective-permute-done.37 = bf16[96,512]{1,0:T(8,128)(2,1)S(1)} collective-permute-done((bf16[96,512]{1,0:T(8,128)(2,1)S(1)}, bf16[96,512]{1,0:T(8,128)(2,1)S(1)}, u32[]{:S(2)}, u32[]{:S(2)}) %collective-permute-start.37) | collective-permute-done | bytes 98336 | tf_op jit(solution)/shard_map/ppermute | solution.py:280
  198.0 2.4 %collective-permute-done.43 = bf16[2,96,512]{2,1,0:T(8,128)(2,1)S(1)} collective-permute-done((bf16[2,96,512]{2,1,0:T(8,128)(2,1)S(1)}, bf16[2,96,512]{2,1,0:T(8,128)(2,1)S(1)}, u32[]{:S(2)}, u32[]{:S(2)}) %collective-permute-start.43) | collective-permute-done | bytes 196640 | tf_op jit(solution)/shard_map/ppermute | solution.py:285
  202.7 7.4 %fast_output.4.refs_0_ = bf16[512,3072]{1,0:T(8,128)(2,1)} custom-call(s32[3]{0:T(128)} %pad_add_fusion.place_ref, bf16[512,3072]{1,0:T(8,128)(2,1)} %query_ref.7, bf16[4,2,96,512]{3,2,1,0:T(8,128)(2,1)} %copy-done.4, f32[24,1,128]{2,1,0:T(1,128)} %reshape.96.refs_10_.gain_ref, f32[24,1,128]{2,1,0:T(1,128)} %reshape.97.refs_11_.bias_ref), custom_call_target="tpu_custom_call" | custom-call | tf_op jit(solution)/shard_map/fast_output/pallas_call | solution.py:236
  210.1 7.5 %fast_output.5.refs_0_ = bf16[512,3072]{1,0:T(8,128)(2,1)} custom-call(s32[3]{0:T(128)} %pad_add_fusion.place_ref, bf16[512,3072]{1,0:T(8,128)(2,1)} %query_ref.7, bf16[4,2,96,512]{3,2,1,0:T(8,128)(2,1)} %copy-done.2, f32[24,1,128]{2,1,0:T(1,128)} %reshape.96.refs_10_.gain_ref, ...), custom_call_target="tpu_custom_call", output_to_operand_aliasing={{}: (5, {})} | custom-call | tf_op jit(solution)/shard_map/fast_output/pallas_call | solution.py:236
  218.5 7.4 %fast_output.6.refs_0_ = bf16[512,3072]{1,0:T(8,128)(2,1)} custom-call(s32[3]{0:T(128)} %pad_add_fusion.place_ref, bf16[512,3072]{1,0:T(8,128)(2,1)} %query_ref.7, bf16[4,2,96,512]{3,2,1,0:T(8,128)(2,1)} %copy-done.5, f32[24,1,128]{2,1,0:T(1,128)} %reshape.96.refs_10_.gain_ref, ...), custom_call_target="tpu_custom_call", output_to_operand_aliasing={{}: (5, {})} | custom-call | tf_op jit(solution)/shard_map/fast_output/pallas_call | solution.py:236
  226.8 7.4 %fast_output.7 = bf16[512,3072]{1,0:T(8,128)(2,1)} custom-call(s32[3]{0:T(128)} %pad_add_fusion.place_ref, bf16[512,3072]{1,0:T(8,128)(2,1)} %query_ref.7, bf16[4,2,96,512]{3,2,1,0:T(8,128)(2,1)} %copy-done.6, f32[24,1,128]{2,1,0:T(1,128)} %reshape.96.refs_10_.gain_ref, f32[24,1,128]{2,1,0:T(1,128)} %reshape.97.refs_11_.bias_ref, ...), custom_call_target="tpu_custom_call", output_to_operand_aliasing={{}: (5, {})} | custom-call | tf_op jit(solution)/shard_map/fast_output/pallas_call | solution.py:236
  (151 shorter events, 77.7 us)
Async XLA Ops:
  6.4 43.1 %collective-permute-start = (bf16[512,1536]{1,0:T(8,128)(2,1)}, bf16[512,1536]{1,0:T(8,128)(2,1)S(1)}, u32[]{:S(2)}, u32[]{:S(2)}) collective-permute-start(bf16[512,1536]{1,0:T(8,128)(2,1)} %get-tuple-element.21), channel_id=1, source_target_pairs={{0,4},{4,0},{8,12},{12,8},{16,20},{20,16},{24,28},{28,24},{1,5},{5... | collective-permute-start | bytes 4718600 | tf_op jit(solution)/shard_map/ppermute | solution.py:275
  6.9 42.6 %collective-permute-start.1 = (bf16[512,1536]{1,0:T(8,128)(2,1)}, bf16[512,1536]{1,0:T(8,128)(2,1)S(1)}, u32[]{:S(2)}, u32[]{:S(2)}) collective-permute-start(bf16[512,1536]{1,0:T(8,128)(2,1)} %get-tuple-element.22), channel_id=1, source_target_pairs={{0,4},{4,0},{8,12},{12,8},{16,20},{20,16},{24,28},{28,24},{1,5},{5... | collective-permute-start | bytes 4718600 | tf_op jit(solution)/shard_map/ppermute | solution.py:275
  6.9 8.9 %collective-permute-start.12 = (bf16[96,512]{1,0:T(8,128)(2,1)S(1)}, bf16[96,512]{1,0:T(8,128)(2,1)S(1)}, u32[]{:S(2)}, u32[]{:S(2)}) collective-permute-start(bf16[96,512]{1,0:T(8,128)(2,1)S(1)} %convert_element_type.169), channel_id=1, source_target_pairs={{0,24},{4,28},{8,16},{12,20},{16,8},{20,12},{24,0},{28,4},{1,25},{... | collective-permute-start | bytes 294920 | tf_op jit(solution)/shard_map/ppermute | solution.py:280
  12.1 12.2 %collective-permute-start.3 = (bf16[96,512]{1,0:T(8,128)(2,1)S(1)}, bf16[96,512]{1,0:T(8,128)(2,1)S(1)}, u32[]{:S(2)}, u32[]{:S(2)}) collective-permute-start(bf16[96,512]{1,0:T(8,128)(2,1)S(1)} %convert_element_type.169), channel_id=1, source_target_pairs={{0,8},{4,12},{8,0},{12,4},{16,24},{20,28},{24,16},{28,20},{1,9},{5... | collective-permute-start | bytes 294920 | tf_op jit(solution)/shard_map/ppermute | solution.py:280
  22.7 24.9 %collective-permute-start.14 = (bf16[2,96,512]{2,1,0:T(8,128)(2,1)}, bf16[2,96,512]{2,1,0:T(8,128)(2,1)}, u32[]{:S(2)}, u32[]{:S(2)}) collective-permute-start(bf16[2,96,512]{2,1,0:T(8,128)(2,1)} %pad_maximum_fusion.3.refs_6_), channel_id=1, source_target_pairs={{0,2},{1,3},{2,0},{3,1},{4,6},{5,7},{6,4},{7,5},{8,10},{9,11},{10,... | collective-permute-start | bytes 589832 | tf_op jit(solution)/shard_map/ppermute | solution.py:285
  24.3 24.8 %collective-permute-start.15 = (bf16[2,96,512]{2,1,0:T(8,128)(2,1)}, bf16[2,96,512]{2,1,0:T(8,128)(2,1)}, u32[]{:S(2)}, u32[]{:S(2)}) collective-permute-start(bf16[2,96,512]{2,1,0:T(8,128)(2,1)} %pad_maximum_fusion.3.refs_6_), channel_id=1, source_target_pairs={{0,3},{1,2},{2,1},{3,0},{4,7},{5,6},{6,5},{7,4},{8,11},{9,10},{10,... | collective-permute-start | bytes 589832 | tf_op jit(solution)/shard_map/ppermute | solution.py:285
  29.2 42.8 %collective-permute-start.4 = (bf16[2,96,512]{2,1,0:T(8,128)(2,1)S(1)}, bf16[2,96,512]{2,1,0:T(8,128)(2,1)}, u32[]{:S(2)}, u32[]{:S(2)}) collective-permute-start(bf16[2,96,512]{2,1,0:T(8,128)(2,1)S(1)} %pad_maximum_fusion.2.refs_6_), channel_id=1, source_target_pairs={{0,1},{1,0},{2,3},{3,2},{4,5},{5,4},{6,7},{7,6},{8,9},{9,8},{10,11... | collective-permute-start | bytes 589832 | tf_op jit(solution)/shard_map/ppermute | solution.py:285
  47.6 24.8 %collective-permute-start.5 = (bf16[2,96,512]{2,1,0:T(8,128)(2,1)S(1)}, bf16[2,96,512]{2,1,0:T(8,128)(2,1)}, u32[]{:S(2)}, u32[]{:S(2)}) collective-permute-start(bf16[2,96,512]{2,1,0:T(8,128)(2,1)S(1)} %pad_maximum_fusion.2.refs_6_), channel_id=1, source_target_pairs={{0,2},{1,3},{2,0},{3,1},{4,6},{5,7},{6,4},{7,5},{8,10},{9,11},{10,... | collective-permute-start | bytes 589832 | tf_op jit(solution)/shard_map/ppermute | solution.py:285
  49.1 23.3 %collective-permute-start.6 = (bf16[2,96,512]{2,1,0:T(8,128)(2,1)S(1)}, bf16[2,96,512]{2,1,0:T(8,128)(2,1)}, u32[]{:S(2)}, u32[]{:S(2)}) collective-permute-start(bf16[2,96,512]{2,1,0:T(8,128)(2,1)S(1)} %pad_maximum_fusion.2.refs_6_), channel_id=1, source_target_pairs={{0,3},{1,2},{2,1},{3,0},{4,7},{5,6},{6,5},{7,4},{8,11},{9,10},{10,... | collective-permute-start | bytes 589832 | tf_op jit(solution)/shard_map/ppermute | solution.py:285
  68.8 23.6 %collective-permute-start.18 = (bf16[2,96,512]{2,1,0:T(8,128)(2,1)}, bf16[2,96,512]{2,1,0:T(8,128)(2,1)S(1)}, u32[]{:S(2)}, u32[]{:S(2)}) collective-permute-start(bf16[2,96,512]{2,1,0:T(8,128)(2,1)} %get-tuple-element.30), channel_id=1, source_target_pairs={{0,3},{1,2},{2,1},{3,0},{4,7},{5,6},{6,5},{7,4},{8,11},{9,10},{10,... | collective-permute-start | bytes 589832 | tf_op jit(solution)/shard_map/ppermute | solution.py:285
  71.4 21.5 %collective-permute-start.17 = (bf16[2,96,512]{2,1,0:T(8,128)(2,1)}, bf16[2,96,512]{2,1,0:T(8,128)(2,1)S(1)}, u32[]{:S(2)}, u32[]{:S(2)}) collective-permute-start(bf16[2,96,512]{2,1,0:T(8,128)(2,1)} %get-tuple-element.29), channel_id=1, source_target_pairs={{0,2},{1,3},{2,0},{3,1},{4,6},{5,7},{6,4},{7,5},{8,10},{9,11},{10,... | collective-permute-start | bytes 589832 | tf_op jit(solution)/shard_map/ppermute | solution.py:285
  72.0 20.9 %collective-permute-start.16 = (bf16[2,96,512]{2,1,0:T(8,128)(2,1)}, bf16[2,96,512]{2,1,0:T(8,128)(2,1)S(1)}, u32[]{:S(2)}, u32[]{:S(2)}) collective-permute-start(bf16[2,96,512]{2,1,0:T(8,128)(2,1)} %get-tuple-element.28), channel_id=1, source_target_pairs={{0,1},{1,0},{2,3},{3,2},{4,5},{5,4},{6,7},{7,6},{8,9},{9,8},{10,11... | collective-permute-start | bytes 589832 | tf_op jit(solution)/shard_map/ppermute | solution.py:285
  107.6 10.7 %collective-permute-start.21 = (bf16[96,512]{1,0:T(8,128)(2,1)S(1)}, bf16[96,512]{1,0:T(8,128)(2,1)S(1)}, u32[]{:S(2)}, u32[]{:S(2)}) collective-permute-start(bf16[96,512]{1,0:T(8,128)(2,1)S(1)} %get-tuple-element.42), channel_id=1, source_target_pairs={{0,8},{4,12},{8,0},{12,4},{16,24},{20,28},{24,16},{28,20},{1,9},{5... | collective-permute-start | bytes 294920 | tf_op jit(solution)/shard_map/ppermute | solution.py:280
  115.3 9.4 %collective-permute-start.32 = (bf16[2,96,512]{2,1,0:T(8,128)(2,1)S(1)}, bf16[2,96,512]{2,1,0:T(8,128)(2,1)S(1)}, u32[]{:S(2)}, u32[]{:S(2)}) collective-permute-start(bf16[2,96,512]{2,1,0:T(8,128)(2,1)S(1)} %pad_maximum_fusion.5.refs_6_), channel_id=1, source_target_pairs={{0,2},{1,3},{2,0},{3,1},{4,6},{5,7},{6,4},{7,5},{8,10},{9,11},{10,... | collective-permute-start | bytes 589832 | tf_op jit(solution)/shard_map/ppermute | solution.py:285
  117.3 8.8 %collective-permute-start.33 = (bf16[2,96,512]{2,1,0:T(8,128)(2,1)S(1)}, bf16[2,96,512]{2,1,0:T(8,128)(2,1)S(1)}, u32[]{:S(2)}, u32[]{:S(2)}) collective-permute-start(bf16[2,96,512]{2,1,0:T(8,128)(2,1)S(1)} %pad_maximum_fusion.5.refs_6_), channel_id=1, source_target_pairs={{0,3},{1,2},{2,1},{3,0},{4,7},{5,6},{6,5},{7,4},{8,11},{9,10},{10,... | collective-permute-start | bytes 589832 | tf_op jit(solution)/shard_map/ppermute | solution.py:285
  118.3 27.9 %collective-permute-start.22 = (bf16[2,96,512]{2,1,0:T(8,128)(2,1)S(1)}, bf16[2,96,512]{2,1,0:T(8,128)(2,1)S(1)}, u32[]{:S(2)}, u32[]{:S(2)}) collective-permute-start(bf16[2,96,512]{2,1,0:T(8,128)(2,1)S(1)} %pad_maximum_fusion.4.refs_6_), channel_id=1, source_target_pairs={{0,1},{1,0},{2,3},{3,2},{4,5},{5,4},{6,7},{7,6},{8,9},{9,8},{10,11... | collective-permute-start | bytes 589832 | tf_op jit(solution)/shard_map/ppermute | solution.py:285
  118.9 28.4 %collective-permute-start.23 = (bf16[2,96,512]{2,1,0:T(8,128)(2,1)S(1)}, bf16[2,96,512]{2,1,0:T(8,128)(2,1)S(1)}, u32[]{:S(2)}, u32[]{:S(2)}) collective-permute-start(bf16[2,96,512]{2,1,0:T(8,128)(2,1)S(1)} %pad_maximum_fusion.4.refs_6_), channel_id=1, source_target_pairs={{0,2},{1,3},{2,0},{3,1},{4,6},{5,7},{6,4},{7,5},{8,10},{9,11},{10,... | collective-permute-start | bytes 589832 | tf_op jit(solution)/shard_map/ppermute | solution.py:285
  122.5 24.8 %collective-permute-start.24 = (bf16[2,96,512]{2,1,0:T(8,128)(2,1)S(1)}, bf16[2,96,512]{2,1,0:T(8,128)(2,1)S(1)}, u32[]{:S(2)}, u32[]{:S(2)}) collective-permute-start(bf16[2,96,512]{2,1,0:T(8,128)(2,1)S(1)} %pad_maximum_fusion.4.refs_6_), channel_id=1, source_target_pairs={{0,3},{1,2},{2,1},{3,0},{4,7},{5,6},{6,5},{7,4},{8,11},{9,10},{10,... | collective-permute-start | bytes 589832 | tf_op jit(solution)/shard_map/ppermute | solution.py:285
  143.8 24.5 %collective-permute-start.36 = (bf16[2,96,512]{2,1,0:T(8,128)(2,1)}, bf16[2,96,512]{2,1,0:T(8,128)(2,1)S(1)}, u32[]{:S(2)}, u32[]{:S(2)}) collective-permute-start(bf16[2,96,512]{2,1,0:T(8,128)(2,1)} %get-tuple-element.38), channel_id=1, source_target_pairs={{0,3},{1,2},{2,1},{3,0},{4,7},{5,6},{6,5},{7,4},{8,11},{9,10},{10,... | collective-permute-start | bytes 589832 | tf_op jit(solution)/shard_map/ppermute | solution.py:285
  146.2 23.3 %collective-permute-start.35 = (bf16[2,96,512]{2,1,0:T(8,128)(2,1)}, bf16[2,96,512]{2,1,0:T(8,128)(2,1)S(1)}, u32[]{:S(2)}, u32[]{:S(2)}) collective-permute-start(bf16[2,96,512]{2,1,0:T(8,128)(2,1)} %get-tuple-element.37), channel_id=1, source_target_pairs={{0,2},{1,3},{2,0},{3,1},{4,6},{5,7},{6,4},{7,5},{8,10},{9,11},{10,... | collective-permute-start | bytes 589832 | tf_op jit(solution)/shard_map/ppermute | solution.py:285
  146.2 23.3 %collective-permute-start.34 = (bf16[2,96,512]{2,1,0:T(8,128)(2,1)}, bf16[2,96,512]{2,1,0:T(8,128)(2,1)S(1)}, u32[]{:S(2)}, u32[]{:S(2)}) collective-permute-start(bf16[2,96,512]{2,1,0:T(8,128)(2,1)} %get-tuple-element.36), channel_id=1, source_target_pairs={{0,1},{1,0},{2,3},{3,2},{4,5},{5,4},{6,7},{7,6},{8,9},{9,8},{10,11... | collective-permute-start | bytes 589832 | tf_op jit(solution)/shard_map/ppermute | solution.py:285
  171.6 10.0 %collective-permute-start.37 = (bf16[96,512]{1,0:T(8,128)(2,1)S(1)}, bf16[96,512]{1,0:T(8,128)(2,1)S(1)}, u32[]{:S(2)}, u32[]{:S(2)}) collective-permute-start(bf16[96,512]{1,0:T(8,128)(2,1)S(1)} %get-tuple-element.44), channel_id=1, source_target_pairs={{0,16},{4,20},{8,24},{12,28},{16,0},{20,4},{24,8},{28,12},{1,17},{... | collective-permute-start | bytes 294920 | tf_op jit(solution)/shard_map/ppermute | solution.py:280
  198.0 19.6 %collective-permute-start.49 = (bf16[4,2,96,512]{3,2,1,0:T(8,128)(2,1)S(1)}, bf16[4,2,96,512]{3,2,1,0:T(8,128)(2,1)S(1)}, u32[]{:S(2)}, u32[]{:S(2)}) collective-permute-start(bf16[4,2,96,512]{3,2,1,0:T(8,128)(2,1)S(1)} %pad_maximum_fusion.1.weight_ref), channel_id=1, source_target_pairs={{0,4},{4,0},{8,12},{12,8},{16,20},{20,16},{24,28},{28,24},{1,5},{5... | collective-permute-start | bytes 2359304 | tf_op jit(solution)/shard_map/ppermute | solution.py:275
  202.6 23.3 %collective-permute-start.44 = (bf16[4,2,96,512]{3,2,1,0:T(8,128)(2,1)S(1)}, bf16[4,2,96,512]{3,2,1,0:T(8,128)(2,1)S(1)}, u32[]{:S(2)}, u32[]{:S(2)}) collective-permute-start(bf16[4,2,96,512]{3,2,1,0:T(8,128)(2,1)S(1)} %pad_maximum_fusion.weight_ref), channel_id=1, source_target_pairs={{0,4},{4,0},{8,12},{12,8},{16,20},{20,16},{24,28},{28,24},{1,5},{5... | collective-permute-start | bytes 2359304 | tf_op jit(solution)/shard_map/ppermute | solution.py:275
  (47 other events, 359.4 us)

commit v3 on v2

--- a/solution.py
+++ b/solution.py
@@ -40,10 +40,34 @@
     return diagonal(top[:, :width], low[:, :width]), diagonal(centred(top), centred(low))
 
 
-def pair_mean(size):
-    row = lax.broadcasted_iota(jnp.int32, (2 * size, 2 * size), 0) // size
-    col = lax.broadcasted_iota(jnp.int32, (2 * size, 2 * size), 1) // size
+def head_mean(size, heads):
+    row = lax.broadcasted_iota(jnp.int32, (heads * size, heads * size), 0) // size
+    col = lax.broadcasted_iota(jnp.int32, (heads * size, heads * size), 1) // size
     return jnp.where(row == col, 1.0 / size, 0.0).astype(BF)
+
+
+def averaged(x, mean):
+    half, wide = x.shape[0] // 2, x.shape[1]
+    both = dot(jnp.concatenate([x[:half], x[half:]], axis=1), mean)
+    return jnp.concatenate([both[:, :wide], both[:, wide:]], axis=0)
+
+
+def pair_row(ref, pair):
+    return jnp.concatenate([ref[pl.ds(2 * pair, 1), :], ref[pl.ds(2 * pair + 1, 1), :]], axis=1)
+
+
+def fill(whole_ref, parts, mine, rows_own):
+    for rel, part in enumerate(parts):
+        at = pl.multiple_of((mine ^ rel) * rows_own, rows_own)
+        for g in range(part.shape[0]):
+            whole_ref[pl.ds(g * len(parts) * rows_own + at, rows_own), :] = part[g]
+
+
+def staggered(stages, lags, n):
+    for t in range(n + max(lags)):
+        for stage, lag in sorted(zip(stages, lags), key=lambda item: -item[1]):
+            if 0 <= t - lag < n:
+                stage(t - lag)
 
 
 def activate(first, kind, slope_too):
@@ -60,192 +84,208 @@
     return active.astype(BF), slope.astype(BF)
 
 
-def grad_kernel(cfg, place_ref, *refs):
-    (size, chunk, skew, kind, total) = cfg
-    key_own, value_own, rate_own, key_far, value_far, rate_far = refs[:6]
-    members = (len(refs) - 14) // 2
+def grad_kernel(size, lags, pairs, per, lag, total, place_ref, *refs):
+    key_own, value_own, key_far, value_far, rate_own, rate_far = refs[:6]
+    members = (len(refs) - 15) // 2
     weight_refs = refs[6 : 6 + members]
     gain_ref, bias_ref = refs[6 + members : 8 + members]
     out_refs = refs[8 + members : 8 + 2 * members]
-    whole_ref, sums_ref, active_ref, dfirst_ref, dsecond_ref, slope_ref = refs[-6:]
+    whole_ref, sums_ref, active_ref, dfirst_ref, dsecond_ref, slope_ref, rate_ref = refs[-7:]
     step = pl.program_id(0)
     mine = place_ref[2]
     groups, rows_own, two = weight_refs[0].shape
     width = two // 2
-    span = members * rows_own
+    tokens = key_own.shape[0]
+    heads = rate_own.shape[0]
 
     @pl.when(step == 0)
     def _():
-        for rel, w in enumerate(weight_refs):
+        fill(whole_ref, weight_refs, mine, rows_own)
+        rate_ref[:tokens, :] = rate_own[...].T.astype(BF)
+        rate_ref[tokens:, :] = rate_far[...].T.astype(BF)
+
+    mean = head_mean(size, 4)
+    head_row = lax.broadcasted_iota(jnp.int32, (heads, 2 * size), 0)
+    head_col = lax.broadcasted_iota(jnp.int32, (heads, 2 * size), 1) // size
+    zof = place_ref[0] ^ (step * pairs // per + lag)
+    first_pair = (zof * 2 + place_ref[1]) * per + (step * pairs) % per
+    const, state = [], {}
+    for j in range(pairs):
+        base = pl.multiple_of((step * pairs + j) * 2 * size, 2 * size)
+        gain = pair_row(gain_ref, first_pair + j)
+        pick = jnp.where(head_row == 2 * (first_pair + j) + head_col, 1.0, 0.0).astype(BF)
+        const.append((base, blocks(whole_ref[pl.ds(base, 2 * size), :], size), gain, pair_row(bias_ref, first_pair + j), gain * (1.0 / total), pick))
+    sources = ((key_own, value_own), (key_far, value_far))
+
+    def at(i):
+        j, far = divmod(i, 2)
+        return j, sources[far], slice(2 * size * j, 2 * size * (j + 1)), pl.ds(far * tokens, tokens), pl.ds(i * tokens, tokens)
+
+    def enter(i):
+        j, (key, value), cols, rows, own = at(i)
+        state[i, "first"] = dot(key[:, cols], const[j][1][0]).astype(BF)
+
+    def bend(i):
+        j, (key, value), cols, rows, own = at(i)
+        active, slope = activate(state.pop((i, "first")), BF, True)
+        active_ref[own, :] = active
+        slope_ref[own, :] = slope
+        state[i, "centre"] = dot(active, const[j][1][1], NT)
+
+    def measure(i):
+        centre = state[i, "centre"]
+        state[i, "spread"] = averaged((centre * centre).astype(BF), mean)
+        state[i, "rate"] = dot(rate_ref[at(i)[3], :], const[at(i)[0]][5])
+
+    def compare(i):
+        j, (key, value), cols, rows, own = at(i)
+        base, mats, gain, bias, scaled, pick = const[j]
+        inverse = lax.rsqrt(state.pop((i, "spread")) + 1e-06)
+        unit = state.pop((i, "centre")) * inverse
+        target = value[:, cols].astype(F32) - key[:, cols].astype(F32)
+        error = unit * gain + (bias - target)
+        dunit = error * (state.pop((i, "rate")) * scaled)
+        state[i, "along"] = averaged((dunit * unit).astype(BF), mean)
+        state[i, "rest"] = (inverse, unit, dunit)
+
+    def back(i):
+        j, (key, value), cols, rows, own = at(i)
+        inverse, unit, dunit = state.pop((i, "rest"))
+        dsecond = (inverse * (dunit - unit * state.pop((i, "along")))).astype(BF)
+        dsecond_ref[own, :] = dsecond
+        state[i, "dactive"] = dot(dsecond, const[j][1][1]).astype(BF)
+
+    def leave(i):
+        j, (key, value), cols, rows, own = at(i)
+        dfirst_ref[own, :] = state.pop((i, "dactive")) * slope_ref[own, :]
+
+    def gather(i):
+        j, (key, value), cols, rows, own = at(i)
+        if i % 2 == 0:
+            return
+        base = const[j][0]
+        both = pl.ds((i - 1) * tokens, 2 * tokens)
+        key_t = [source[0][:, cols].T for source in sources]
+        dsecond_t = dsecond_ref[both, :].T
+        for head in range(2):
+            part = slice(head * size, (head + 1) * size)
+            lane = slice(head * width, (head + 1) * width)
+            halves = [dfirst_ref[pl.ds(k * tokens, tokens), lane] for k in (i - 1, i)]
+            first = dot(key_t[0][part], halves[0]) + dot(key_t[1][part], halves[1])
+            second = dot(dsecond_t[part], active_ref[both, lane])
+            second = second - jnp.mean(second, axis=0, keepdims=True)
+            sums_ref[pl.ds(base + head * size, size), :width] = first.astype(BF)
+            sums_ref[pl.ds(base + head * size, size), width:] = second.astype(BF)
+
+    staggered((enter, bend, measure, compare, back, leave, gather), lags, 2 * pairs)
+
+    @pl.when(step == pl.num_programs(0) - 1)
+    def _():
+        for rel, out in enumerate(out_refs):
             at = pl.multiple_of((mine ^ rel) * rows_own, rows_own)
             for g in range(groups):
-                whole_ref[pl.ds(g * span + at, rows_own), :] = w[g]
-
-    base = pl.multiple_of(step * 2 * size, 2 * size)
-    first_w, second_w = blocks(whole_ref[pl.ds(base, 2 * size), :], size)
-    mean = pair_mean(size)
-    gain = gain_ref[0]
-    bias = bias_ref[0]
-    scaled = gain * (1.0 / total)
-    tokens = key_own.shape[0]
-    pieces = [(src, at) for src in ((key_own, value_own, rate_own, 0), (key_far, value_far, rate_far, tokens)) for at in range(0, tokens, chunk)]
-    state = {}
-
-    def s0(i):
-        (key, value, rate, off), at = pieces[i]
-        state[i, "first"] = dot(key[pl.ds(at, chunk), :], first_w)
-
-    def s1(i):
-        (key, value, rate, off), at = pieces[i]
-        rows = pl.ds(off + at, chunk)
-        active, slope = activate(state.pop((i, "first")), kind, True)
-        active_ref[rows, :] = active
-        slope_ref[rows, :] = slope
-        state[i, "centre"] = dot(active, second_w, NT)
-
-    def s2(i):
-        centre = state[i, "centre"]
-        state[i, "spread"] = dot((centre * centre).astype(BF), mean)
-
-    def s3(i):
-        (key, value, rate, off), at = pieces[i]
-        rows = pl.ds(at, chunk)
-        inverse = lax.rsqrt(state.pop((i, "spread")) + 1e-06)
-        unit = state.pop((i, "centre")) * inverse
-        target = value[rows, :].astype(F32) - key[rows, :].astype(F32)
-        error = unit * gain + (bias - target)
-        dunit = error * (rate[rows, :].astype(F32) * scaled)
-        state[i, "along"] = dot((dunit * unit).astype(BF), mean)
-        state[i, "rest"] = (inverse, unit, dunit)
-
-    def s4(i):
-        (key, value, rate, off), at = pieces[i]
-        inverse, unit, dunit = state.pop((i, "rest"))
-        dsecond = (inverse * (dunit - unit * state.pop((i, "along")))).astype(BF)
-        dsecond_ref[pl.ds(off + at, chunk), :] = dsecond
-        state[i, "dactive"] = dot(dsecond, second_w)
-
-    def s5(i):
-        (key, value, rate, off), at = pieces[i]
-        rows = pl.ds(off + at, chunk)
-        dfirst_ref[rows, :] = state.pop((i, "dactive")).astype(BF) * slope_ref[rows, :]
-
-    stages = (s0, s1, s2, s3, s4, s5)
-    n = len(pieces)
-    if skew is None:
-        for i in range(n):
-            for s in stages: s(i)
-    else:
-        for t in range(n + max(skew)):
-            for s, lag in list(zip(stages, skew))[::-1]:
-                if 0 <= t - lag < n:
-                    s(t - lag)
-    dsecond_t = dsecond_ref[...].T
-    key_t = [key_own[...].T, key_far[...].T]
-    for head in range(2):
-        part = slice(head * size, (head + 1) * size)
-        cols = slice(head * width, (head + 1) * width)
-        first = dot(key_t[0][part], dfirst_ref[:tokens, cols]) + dot(key_t[1][part], dfirst_ref[tokens:, cols])
-        second = dot(dsecond_t[part], active_ref[:, cols])
-        second = second - jnp.mean(second, axis=0, keepdims=True)
-        sums_ref[pl.ds(base + head * size, size), :width] = first.astype(BF)
-        sums_ref[pl.ds(base + head * size, size), width:] = second.astype(BF)
-
-    @pl.when(step == pl.num_programs(0) - 1)
-    def _():
-        for rel, o in enumerate(out_refs):
-            at = pl.multiple_of((mine ^ rel) * rows_own, rows_own)
-            for g in range(groups):
-                o[g] = sums_ref[pl.ds(g * span + at, rows_own), :]
-
-
-def gradient(place, own, far, weights, gain, bias, total, size, lag, chunk=128, skew=None, kind=BF, flags=None):
+                out[g] = sums_ref[pl.ds(g * members * rows_own + at, rows_own), :]
+
+
+def gradient(place, own, far, rates, weights, gain, bias, total, lag, pairs=1, lags=(0, 1, 2, 3, 4, 5, 6)):
     tokens = own[0].shape[0]
+    heads, size = gain.shape
+    members = len(weights)
     groups, rows_own, two = weights[0].shape
-    members = len(weights)
     per = members * rows_own // (2 * size)
-    zof = lambda i, place: place[0] ^ (i // per + lag)
-    own_spec = pl.BlockSpec((tokens, 2 * size), lambda i, place: (0, (zof(i, place) * 2 + place[1]) * per + i % per))
-    far_spec = pl.BlockSpec((tokens, 2 * size), lambda i, place: (0, zof(i, place) * per + i % per))
-    vec = pl.BlockSpec((1, 1, 2 * size), lambda i, place: ((zof(i, place) * 2 + place[1]) * per + i % per, 0, 0))
-    mat = pl.BlockSpec((groups, rows_own, two), lambda i, place: (0, 0, 0))
-    out = jax.ShapeDtypeStruct((groups, rows_own, two), BF)
-    cfg = (size, chunk, skew, kind, total)
+    zof = lambda i, place: place[0] ^ (i * pairs // per + lag)
+    wide = pairs * 2 * size
+    own_spec = pl.BlockSpec((tokens, wide), lambda i, place: (0, ((zof(i, place) * 2 + place[1]) * per + i * pairs % per) // pairs))
+    far_spec = pl.BlockSpec((tokens, wide), lambda i, place: (0, (zof(i, place) * per + i * pairs % per) // pairs))
+    whole = lambda shape: pl.BlockSpec(shape, lambda i, place: (0,) * len(shape))
+    mat = whole((groups, rows_own, two))
     rows = groups * members * rows_own
-    pairs = gain.size // (2 * size)
     return pl.pallas_call(
-        functools.partial(grad_kernel, cfg),
-        out_shape=[out] * members,
+        functools.partial(grad_kernel, size, lags, pairs, per, lag, total),
+        out_shape=[jax.ShapeDtypeStruct((groups, rows_own, two), BF)] * members,
         grid_spec=pltpu.PrefetchScalarGridSpec(
             num_scalar_prefetch=1,
-            grid=(groups * per,),
-            in_specs=[own_spec] * 3 + [far_spec] * 2 + [own_spec] + [mat] * members + [vec, vec],
+            grid=(groups * per // pairs,),
+            in_specs=[own_spec] * 2 + [far_spec] * 2 + [whole((heads, tokens))] * 2 + [mat] * members + [whole((heads, size))] * 2,
             out_specs=[mat] * members,
             scratch_shapes=[
                 pltpu.VMEM((rows, two), BF),
                 pltpu.VMEM((rows, two), BF),
-                pltpu.VMEM((2 * tokens, two), BF),
-                pltpu.VMEM((2 * tokens, two), BF),
-                pltpu.VMEM((2 * tokens, 2 * size), BF),
-                pltpu.VMEM((2 * tokens, two), BF),
+                pltpu.VMEM((2 * pairs * tokens, two), BF),
+                pltpu.VMEM((2 * pairs * tokens, two), BF),
+                pltpu.VMEM((2 * pairs * tokens, 2 * size), BF),
+                pltpu.VMEM((2 * pairs * tokens, two), BF),
+                pltpu.VMEM((2 * tokens, heads), BF),
             ],
         ),
-        compiler_params=pltpu.CompilerParams(flags=flags) if flags else None,
         name="fast_gradient",
-    )(place, *own, *far, *weights, gain.reshape(pairs, 1, 2 * size), bias.reshape(pairs, 1, 2 * size))
-
-
-def output_kernel(size, chunk, kind, place_ref, query_ref, weight_ref, gain_ref, bias_ref, *refs):
+    )(place, *own, *far, *rates, *weights, gain, bias)
+
+
+def output_kernel(size, chunk, lags, pairs, per, lag, flip, place_ref, query_ref, weight_ref, gain_ref, bias_ref, *refs):
     out_ref, whole_ref = refs[-2:]
     step = pl.program_id(0)
-    mine = place_ref[2]
-    members, groups, rows_own, _ = weight_ref.shape
+    members, groups, rows_own, two = weight_ref.shape
 
     @pl.when(step == 0)
     def _():
-        for rel in range(members):
-            at = pl.multiple_of((mine ^ rel) * rows_own, rows_own)
-            for g in range(groups):
-                whole_ref[pl.ds(g * members * rows_own + at, rows_own), :] = weight_ref[rel, g]
-
-    base = pl.multiple_of(step * 2 * size, 2 * size)
-    first_w, second_w = blocks(whole_ref[pl.ds(base, 2 * size), :], size)
-    mean = pair_mean(size)
-    gain = gain_ref[0]
-    bias = bias_ref[0]
-    for at in range(0, query_ref.shape[0], chunk):
-        rows = pl.ds(at, chunk)
-        queries = query_ref[rows, :]
-        active = activate(dot(queries, first_w), kind, False)
-        centre = dot(active, second_w, NT)
-        spread = dot((centre * centre).astype(BF), mean)
-        unit = centre * lax.rsqrt(spread + 1e-06)
-        out_ref[rows, :] = (queries.astype(F32) + unit * gain + bias).astype(BF)
-
-
-def output(place, queries, weights, gain, bias, before, size, lag, flip, chunk=512, kind=BF):
+        fill(whole_ref, [weight_ref.at[rel] for rel in range(members)], place_ref[2], rows_own)
+
+    mean = head_mean(size, 4)
+    zof = place_ref[0] ^ (step * pairs // per + lag)
+    first_pair = (zof * 2 + (place_ref[1] ^ flip)) * per + (step * pairs) % per
+    const, state = [], {}
+    for j in range(pairs):
+        base = pl.multiple_of((step * pairs + j) * 2 * size, 2 * size)
+        const.append((blocks(whole_ref[pl.ds(base, 2 * size), :], size), pair_row(gain_ref, first_pair + j), pair_row(bias_ref, first_pair + j)))
+    count = query_ref.shape[0] // chunk
+
+    def at(i):
+        j, k = divmod(i, count)
+        return const[j], (pl.ds(k * chunk, chunk), slice(2 * size * j, 2 * size * (j + 1)))
+
+    def enter(i):
+        (mats, gain, bias), where = at(i)
+        state[i, "first"] = dot(query_ref[where], mats[0]).astype(BF)
+
+    def bend(i):
+        (mats, gain, bias), where = at(i)
+        state[i, "centre"] = dot(activate(state.pop((i, "first")), BF, False), mats[1], NT)
+
+    def measure(i):
+        centre = state[i, "centre"]
+        state[i, "spread"] = averaged((centre * centre).astype(BF), mean)
+
+    def leave(i):
+        (mats, gain, bias), where = at(i)
+        unit = state.pop((i, "centre")) * lax.rsqrt(state.pop((i, "spread")) + 1e-06)
+        out_ref[where] = (query_ref[where].astype(F32) + unit * gain + bias).astype(BF)
+
+    staggered((enter, bend, measure, leave), lags, pairs * count)
+
+
+def output(place, queries, weights, gain, bias, before, lag, flip, pairs=1, chunk=256, lags=(0, 1, 2, 3)):
     tokens, model = queries.shape
     members, groups, rows_own, two = weights.shape
+    heads, size = gain.shape
     per = members * rows_own // (2 * size)
-    pairs = gain.size // (2 * size)
-    column = lambda i, place: ((place[0] ^ (i // per + lag)) * 2 + (place[1] ^ flip)) * per + i % per
-    col = pl.BlockSpec((tokens, 2 * size), lambda i, place: (0, column(i, place)))
-    vec = pl.BlockSpec((1, 1, 2 * size), lambda i, place: (column(i, place), 0, 0))
-    mat = pl.BlockSpec((members, groups, rows_own, two), lambda i, place: (0, 0, 0, 0))
+    column = lambda i, place: (((place[0] ^ (i * pairs // per + lag)) * 2 + (place[1] ^ flip)) * per + i * pairs % per) // pairs
+    col = pl.BlockSpec((tokens, pairs * 2 * size), lambda i, place: (0, column(i, place)))
+    whole = lambda shape: pl.BlockSpec(shape, lambda i, place: (0,) * len(shape))
     more = [] if before is None else [before]
     return pl.pallas_call(
-        functools.partial(output_kernel, size, chunk, kind),
+        functools.partial(output_kernel, size, chunk, lags, pairs, per, lag, flip),
         out_shape=jax.ShapeDtypeStruct((tokens, model), BF),
         grid_spec=pltpu.PrefetchScalarGridSpec(
             num_scalar_prefetch=1,
-            grid=(groups * per,),
-            in_specs=[col, mat, vec, vec] + [pl.BlockSpec(memory_space=pl.ANY)] * len(more),
+            grid=(groups * per // pairs,),
+            in_specs=[col, whole(weights.shape)] + [whole((heads, size))] * 2 + [pl.BlockSpec(memory_space=pl.ANY)] * len(more),
             out_specs=col,
             scratch_shapes=[pltpu.VMEM((groups * members * rows_own, two), BF)],
         ),
         input_output_aliases={5: 0} if more else {},
         name="fast_output",
-    )(place, queries, weights, gain.reshape(pairs, 1, 2 * size), bias.reshape(pairs, 1, 2 * size), *more)
+    )(place, queries, weights, gain, bias, *more)
 
 
 def pick_kernel(place_ref, *refs):
@@ -313,14 +353,16 @@
     place = jnp.stack([gx // 2, gx % 2, lax.axis_index("gy")]).astype(jnp.int32)
     chunks = [(0, groups // 2), (groups // 2, groups - groups // 2)]
     fast, moment = (fast_weights, momentum)
-    spread = lambda rates: jnp.repeat(rates.astype(BF), size, axis=1)
     weights = fetch(fast, groups, members, chunks)
     key_send, value_send = pick(place, (key_rows, value_rows), groups, 1)
-    far = (core_swap(key_send), core_swap(value_send), spread(core_swap(token_rates)))
-    own = (key_rows, value_rows, spread(token_rates))
+    far = (core_swap(key_send), core_swap(value_send))
+    own = (key_rows, value_rows)
+    rates = (token_rates.T, core_swap(token_rates).T)
+    pairs = members * fast.shape[0] // (2 * size)
+    pairs = pairs if pairs <= 3 else 1
     for step in range(STEPS):
         parts = [
-            gradient(place, own, far, w, norm_gain, norm_bias, total, size, at, chunk=512)
+            gradient(place, own, far, rates, w, norm_gain, norm_bias, total, at, pairs)
             for w, (at, count) in zip(weights, chunks)
         ]
         grad = collect(parts, groups, members, chunks)
@@ -332,7 +374,7 @@
     twin = [core_swap(w) for w in whole]
     for flip, ws in enumerate((whole, twin)):
         for w, (at, count) in zip(ws, chunks):
-            mixed = output(place, query_rows, w, norm_gain, norm_bias, mixed, size, at, flip)
+            mixed = output(place, query_rows, w, norm_gain, norm_bias, mixed, at, flip, pairs, min(512, query_rows.shape[0]))
     return (mixed, fast, moment)
 
 
@@ -341,7 +383,7 @@
     tokens = key_ref.shape[0]
     width = packed_ref.shape[1] // 2
     first_w, second_w = blocks(packed_ref[...], size)
-    mean = pair_mean(size)
+    mean = head_mean(size, 2)
     gain = gain_ref[0]
     bias = bias_ref[0]
     scaled = gain * (1.0 / total)
@@ -375,7 +417,7 @@
 def plain_apply_kernel(size, chunk, kind, query_ref, packed_ref, gain_ref, bias_ref, out_ref):
     tokens = query_ref.shape[0]
     first_w, second_w = blocks(packed_ref[...], size)
-    mean = pair_mean(size)
+    mean = head_mean(size, 2)
     gain = gain_ref[0]
     bias = bias_ref[0]
     for at in range(0, tokens, chunk):

time: 235 us -> 198 us (0.84)
  Pallas kernels: 103 us -> 80.4 us
  local copies, waits for them, and re-layouts: 23.1 us -> 6.13 us
  starting transfers between devices: 55.8 us -> 70.6 us
  waiting for transfers between devices: 45 us -> 34.1 us
    pallas_call x8, Pallas kernels: 97.7 us -> 75.3 us  [the longest x4 52.8 us: gradient(): pl.pallas_call(functools.partial(grad_kernel, size, lags, pairs, per, lag...]
    ppermute x15, starting transfers between devices: 18.7 us -> 32.5 us  [z_shift(): return lax.ppermute(x, 'gx', [(i, i ^ 2 * s) for i in range(n)])]
    reshape x4 -> x0, local copies, waits for them, and re-layouts: 12.2 us -> none  [the longest x2 9.33 us: per_device(): spread = lambda rates: jnp.repeat(rates.astype(BF), size, axis=1)]
    ppermute x15, waiting for transfers between devices: 26 us -> 17.4 us  [z_shift(): return lax.ppermute(x, 'gx', [(i, i ^ 2 * s) for i in range(n)])]
    broadcast_in_dim x2 -> x0, local copies, waits for them, and re-layouts: 4.65 us -> none  [per_device(): spread = lambda rates: jnp.repeat(rates.astype(BF), size, axis=1)]
    ppermute x30, waiting for transfers between devices: 19 us -> 15.5 us  [plane_shift(): return lax.ppermute(x, 'gy', [(i, i ^ s) for i in range(n)])]
    unnamed x42 -> x48, local copies, waits for them, and re-layouts: 6.3 us -> 6.13 us
  transfers between devices with their start and end apart: 50 -> 50, of which waited for: 24 -> 18; matrix products, arithmetic and copies ran while one was open for 9% -> 2% of each run, Pallas kernels for 39% -> 35%
where the time goes in v3:
time: 198 us; the launch traced here: 197 us
  Pallas kernels  80.4 us (41%)
  starting transfers between devices  70.6 us (36%)
  waiting for transfers between devices  34.1 us (17%)
  local copies, waits for them, and re-layouts  6.13 us (3%)
  other arithmetic  4.83 us (2%)
    pallas_call x4, Pallas kernels, gradient(): pl.pallas_call(functools.partial(grad_kernel, size, lags, pairs, per, lag...  52.8 us
    ppermute x30, starting transfers between devices, plane_shift(): return lax.ppermute(x, 'gy', [(i, i ^ s) for i in range(n)])  37.4 us
    ppermute x15, starting transfers between devices, z_shift(): return lax.ppermute(x, 'gx', [(i, i ^ 2 * s) for i in range(n)])  32.5 us
    pallas_call x4, Pallas kernels, output(): pl.pallas_call(functools.partial(output_kernel, size, chunk, lags, pairs,...  22.6 us
    ppermute x15, waiting for transfers between devices, z_shift(): return lax.ppermute(x, 'gx', [(i, i ^ 2 * s) for i in range(n)])  17.4 us
    ppermute x30, waiting for transfers between devices, plane_shift(): return lax.ppermute(x, 'gy', [(i, i ^ s) for i in range(n)])  15.5 us
    unnamed x48, local copies, waits for them, and re-layouts  6.13 us
    pallas_call x1, Pallas kernels, pick(): pl.pallas_call(pick_kernel, out_shape=[jax.ShapeDtypeStruct((tokens, grou...  5.08 us
  transfers between devices with their start and end apart: 50, of which 18 were waited for; matrix products, arithmetic and copies ran while one was open for 2% of the time, Pallas kernels for 35%

profile of v3, /device:TPU:0, one launch (start us, length us, event | category | flops | bytes accessed | tf_op | source)
XLA Modules:
  0.0 197.0 jit_solution(1869020344607130177)
XLA Ops:
  1.2 5.1 %pick.1 = (bf16[512,1536]{1,0:T(8,128)(2,1)}, bf16[512,1536]{1,0:T(8,128)(2,1)}) custom-call(s32[3]{0:T(128)} %pad_add_fusion.place_ref, bf16[512,3072]{1,0:T(8,128)(2,1)} %refs_0_.9, bf16[512,3072]{1,0:T(8,128)(2,1)} %refs_1_.9), custom_call_target="tpu_custom_call" | custom-call | tf_op jit(solution)/shard_map/pick/pallas_call | solution.py:300
  6.8 3.1 %collective-permute-start.3 = (bf16[96,512]{1,0:T(8,128)(2,1)S(1)}, bf16[96,512]{1,0:T(8,128)(2,1)S(1)}, u32[]{:S(2)}, u32[]{:S(2)}) collective-permute-start(bf16[96,512]{1,0:T(8,128)(2,1)S(1)} %convert_element_type.161), channel_id=1, source_target_pairs={{0,8},{4,12},{8,0},{12,4},{16,24},{20,28},{24,16},{28,20},{1,9},{5... | collective-permute-start | bytes 294920 | tf_op jit(solution)/shard_map/ppermute | solution.py:320
  10.0 2.5 %collective-permute-start.12 = (bf16[96,512]{1,0:T(8,128)(2,1)S(1)}, bf16[96,512]{1,0:T(8,128)(2,1)S(1)}, u32[]{:S(2)}, u32[]{:S(2)}) collective-permute-start(bf16[96,512]{1,0:T(8,128)(2,1)S(1)} %convert_element_type.161), channel_id=1, source_target_pairs={{0,24},{4,28},{8,16},{12,20},{16,8},{20,12},{24,0},{28,4},{1,25},{... | collective-permute-start | bytes 294920 | tf_op jit(solution)/shard_map/ppermute | solution.py:320
  25.8 4.5 %collective-permute-done.6.refs_9_ = bf16[2,96,512]{2,1,0:T(8,128)(2,1)S(1)} collective-permute-done((bf16[2,96,512]{2,1,0:T(8,128)(2,1)S(1)}, bf16[2,96,512]{2,1,0:T(8,128)(2,1)S(1)}, u32[]{:S(2)}, u32[]{:S(2)}) %collective-permute-start.6) | collective-permute-done | bytes 196640 | tf_op jit(solution)/shard_map/ppermute | solution.py:325
  34.3 13.2 %fast_gradient.4 = (bf16[2,96,512]{2,1,0:T(8,128)(2,1)}, bf16[2,96,512]{2,1,0:T(8,128)(2,1)}, bf16[2,96,512]{2,1,0:T(8,128)(2,1)}, bf16[2,96,512]{2,1,0:T(8,128)(2,1)}) custom-call(s32[3]{0:T(128)} %pad_add_fusion.place_ref, bf16[512,3072]{1,0:T(8,128)(2,1)} %refs_0_.9, bf16[512,3072]{1,0:T(8,128)(2,1)} %refs_1_.9, bf16[512,1536]{1,0:T(8,128)(2,1)} %copy-done, ...), custom_call_target="tpu_custom_call" | custom-call | tf_op jit(solution)/shard_map/fast_gradient/pallas_call | solution.py:203
  48.6 2.5 %collective-permute-start.9 = (bf16[2,96,512]{2,1,0:T(8,128)(2,1)}, bf16[2,96,512]{2,1,0:T(8,128)(2,1)S(1)}, u32[]{:S(2)}, u32[]{:S(2)}) collective-permute-start(bf16[2,96,512]{2,1,0:T(8,128)(2,1)} %get-tuple-element.26), channel_id=1, source_target_pairs={{0,3},{1,2},{2,1},{3,0},{4,7},{5,6},{6,5},{7,4},{8,11},{9,10},{10,... | collective-permute-start | bytes 589832 | tf_op jit(solution)/shard_map/ppermute | solution.py:325
  51.1 13.2 %fast_gradient.5 = (bf16[2,96,512]{2,1,0:T(8,128)(2,1)}, bf16[2,96,512]{2,1,0:T(8,128)(2,1)}, bf16[2,96,512]{2,1,0:T(8,128)(2,1)}, bf16[2,96,512]{2,1,0:T(8,128)(2,1)}) custom-call(s32[3]{0:T(128)} %pad_add_fusion.place_ref, bf16[512,3072]{1,0:T(8,128)(2,1)} %refs_0_.9, bf16[512,3072]{1,0:T(8,128)(2,1)} %refs_1_.9, bf16[512,1536]{1,0:T(8,128)(2,1)} %copy-done, ...), custom_call_target="tpu_custom_call" | custom-call | tf_op jit(solution)/shard_map/fast_gradient/pallas_call | solution.py:203
  67.9 4.4 %collective-permute-start.10 = (bf16[96,512]{1,0:T(8,128)(2,1)S(1)}, bf16[96,512]{1,0:T(8,128)(2,1)S(1)}, u32[]{:S(2)}, u32[]{:S(2)}) collective-permute-start(bf16[96,512]{1,0:T(8,128)(2,1)S(1)} %fusion.6), channel_id=1, source_target_pairs={{0,8},{4,12},{8,0},{12,4},{16,24},{20,28},{24,16},{28,20},{1,9},{5... | collective-permute-start | bytes 294920 | tf_op jit(solution)/shard_map/ppermute | solution.py:320
  73.9 3.0 %collective-permute-start.19 = (bf16[96,512]{1,0:T(8,128)(2,1)S(1)}, bf16[96,512]{1,0:T(8,128)(2,1)S(1)}, u32[]{:S(2)}, u32[]{:S(2)}) collective-permute-start(bf16[96,512]{1,0:T(8,128)(2,1)S(1)} %get-tuple-element.46), channel_id=1, source_target_pairs={{0,16},{4,20},{8,24},{12,28},{16,0},{20,4},{24,8},{28,12},{1,17},{... | collective-permute-start | bytes 294920 | tf_op jit(solution)/shard_map/ppermute | solution.py:320
  76.8 3.9 %collective-permute-start.20 = (bf16[96,512]{1,0:T(8,128)(2,1)S(1)}, bf16[96,512]{1,0:T(8,128)(2,1)S(1)}, u32[]{:S(2)}, u32[]{:S(2)}) collective-permute-start(bf16[96,512]{1,0:T(8,128)(2,1)S(1)} %get-tuple-element.47), channel_id=1, source_target_pairs={{0,24},{4,28},{8,16},{12,20},{16,8},{20,12},{24,0},{28,4},{1,25},{... | collective-permute-start | bytes 294920 | tf_op jit(solution)/shard_map/ppermute | solution.py:320
  80.8 4.2 %collective-permute-done.20 = bf16[96,512]{1,0:T(8,128)(2,1)S(1)} collective-permute-done((bf16[96,512]{1,0:T(8,128)(2,1)S(1)}, bf16[96,512]{1,0:T(8,128)(2,1)S(1)}, u32[]{:S(2)}, u32[]{:S(2)}) %collective-permute-start.20) | collective-permute-done | bytes 98336 | tf_op jit(solution)/shard_map/ppermute | solution.py:320
  85.1 2.8 %collective-permute-start.21 = (bf16[96,512]{1,0:T(8,128)(2,1)S(1)}, bf16[96,512]{1,0:T(8,128)(2,1)S(1)}, u32[]{:S(2)}, u32[]{:S(2)}) collective-permute-start(bf16[96,512]{1,0:T(8,128)(2,1)S(1)} %get-tuple-element.42), channel_id=1, source_target_pairs={{0,8},{4,12},{8,0},{12,4},{16,24},{20,28},{24,16},{28,20},{1,9},{5... | collective-permute-start | bytes 294920 | tf_op jit(solution)/shard_map/ppermute | solution.py:320
  101.7 13.2 %fast_gradient.6 = (bf16[2,96,512]{2,1,0:T(8,128)(2,1)}, bf16[2,96,512]{2,1,0:T(8,128)(2,1)}, bf16[2,96,512]{2,1,0:T(8,128)(2,1)}, bf16[2,96,512]{2,1,0:T(8,128)(2,1)}) custom-call(s32[3]{0:T(128)} %pad_add_fusion.place_ref, bf16[512,3072]{1,0:T(8,128)(2,1)} %refs_0_.9, bf16[512,3072]{1,0:T(8,128)(2,1)} %refs_1_.9, bf16[512,1536]{1,0:T(8,128)(2,1)} %copy-done, ...), custom_call_target="tpu_custom_call" | custom-call | tf_op jit(solution)/shard_map/fast_gradient/pallas_call | solution.py:203
  119.9 13.2 %fast_gradient.7 = (bf16[2,96,512]{2,1,0:T(8,128)(2,1)}, bf16[2,96,512]{2,1,0:T(8,128)(2,1)}, bf16[2,96,512]{2,1,0:T(8,128)(2,1)}, bf16[2,96,512]{2,1,0:T(8,128)(2,1)}) custom-call(s32[3]{0:T(128)} %pad_add_fusion.place_ref, bf16[512,3072]{1,0:T(8,128)(2,1)} %refs_0_.9, bf16[512,3072]{1,0:T(8,128)(2,1)} %refs_1_.9, bf16[512,1536]{1,0:T(8,128)(2,1)} %copy-done, ...), custom_call_target="tpu_custom_call" | custom-call | tf_op jit(solution)/shard_map/fast_gradient/pallas_call | solution.py:203
  139.0 2.9 %collective-permute-done.35 = bf16[2,96,512]{2,1,0:T(8,128)(2,1)S(1)} collective-permute-done((bf16[2,96,512]{2,1,0:T(8,128)(2,1)}, bf16[2,96,512]{2,1,0:T(8,128)(2,1)S(1)}, u32[]{:S(2)}, u32[]{:S(2)}) %collective-permute-start.35) | collective-permute-done | bytes 196640 | tf_op jit(solution)/shard_map/ppermute | solution.py:325
  143.0 3.2 %collective-permute-start.37 = (bf16[96,512]{1,0:T(8,128)(2,1)S(1)}, bf16[96,512]{1,0:T(8,128)(2,1)S(1)}, u32[]{:S(2)}, u32[]{:S(2)}) collective-permute-start(bf16[96,512]{1,0:T(8,128)(2,1)S(1)} %get-tuple-element.44), channel_id=1, source_target_pairs={{0,16},{4,20},{8,24},{12,28},{16,0},{20,4},{24,8},{28,12},{1,17},{... | collective-permute-start | bytes 294920 | tf_op jit(solution)/shard_map/ppermute | solution.py:320
  146.6 3.2 %collective-permute-done.37 = bf16[96,512]{1,0:T(8,128)(2,1)S(1)} collective-permute-done((bf16[96,512]{1,0:T(8,128)(2,1)S(1)}, bf16[96,512]{1,0:T(8,128)(2,1)S(1)}, u32[]{:S(2)}, u32[]{:S(2)}) %collective-permute-start.37) | collective-permute-done | bytes 98336 | tf_op jit(solution)/shard_map/ppermute | solution.py:320
  149.8 2.8 %collective-permute-done.38 = bf16[96,512]{1,0:T(8,128)(2,1)S(1)} collective-permute-done((bf16[96,512]{1,0:T(8,128)(2,1)S(1)}, bf16[96,512]{1,0:T(8,128)(2,1)S(1)}, u32[]{:S(2)}, u32[]{:S(2)}) %collective-permute-start.38) | collective-permute-done | bytes 98336 | tf_op jit(solution)/shard_map/ppermute | solution.py:320
  155.2 2.7 %collective-permute-start.40 = (bf16[96,512]{1,0:T(8,128)(2,1)S(1)}, bf16[96,512]{1,0:T(8,128)(2,1)S(1)}, u32[]{:S(2)}, u32[]{:S(2)}) collective-permute-start(bf16[96,512]{1,0:T(8,128)(2,1)S(1)} %get-tuple-element.39), channel_id=1, source_target_pairs={{0,24},{4,28},{8,16},{12,20},{16,8},{20,12},{24,0},{28,4},{1,25},{... | collective-permute-start | bytes 294920 | tf_op jit(solution)/shard_map/ppermute | solution.py:320
  169.7 2.7 %collective-permute-done.42 = bf16[2,96,512]{2,1,0:T(8,128)(2,1)S(1)} collective-permute-done((bf16[2,96,512]{2,1,0:T(8,128)(2,1)S(1)}, bf16[2,96,512]{2,1,0:T(8,128)(2,1)S(1)}, u32[]{:S(2)}, u32[]{:S(2)}) %collective-permute-start.42) | collective-permute-done | bytes 196640 | tf_op jit(solution)/shard_map/ppermute | solution.py:325
  172.6 5.7 %fast_output.4.refs_0_ = bf16[512,3072]{1,0:T(8,128)(2,1)} custom-call(s32[3]{0:T(128)} %pad_add_fusion.place_ref, bf16[512,3072]{1,0:T(8,128)(2,1)} %query_ref.7, bf16[4,2,96,512]{3,2,1,0:T(8,128)(2,1)} %copy-done.2, f32[48,64]{1,0:T(8,128)} %gain_ref.7, f32[48,64]{1,0:T(8,128)} %bias_ref.7), custom_call_target="tpu_custom_call" | custom-call | tf_op jit(solution)/shard_map/fast_output/pallas_call | solution.py:276
  178.3 5.6 %fast_output.5.refs_0_ = bf16[512,3072]{1,0:T(8,128)(2,1)} custom-call(s32[3]{0:T(128)} %pad_add_fusion.place_ref, bf16[512,3072]{1,0:T(8,128)(2,1)} %query_ref.7, bf16[4,2,96,512]{3,2,1,0:T(8,128)(2,1)} %copy-done.3, f32[48,64]{1,0:T(8,128)} %gain_ref.7, f32[48,64]{1,0:T(8,128)} %bias_ref.7, ...), custom_call_target="tpu_custom_call", output_to_operand_aliasing={{}: (5, {})} | custom-call | tf_op jit(solution)/shard_map/fast_output/pallas_call | solution.py:276
  184.8 5.7 %fast_output.6.refs_0_ = bf16[512,3072]{1,0:T(8,128)(2,1)} custom-call(s32[3]{0:T(128)} %pad_add_fusion.place_ref, bf16[512,3072]{1,0:T(8,128)(2,1)} %query_ref.7, bf16[4,2,96,512]{3,2,1,0:T(8,128)(2,1)} %copy-done.7, f32[48,64]{1,0:T(8,128)} %gain_ref.7, f32[48,64]{1,0:T(8,128)} %bias_ref.7, ...), custom_call_target="tpu_custom_call", output_to_operand_aliasing={{}: (5, {})} | custom-call | tf_op jit(solution)/shard_map/fast_output/pallas_call | solution.py:276
  191.4 5.6 %fast_output.7 = bf16[512,3072]{1,0:T(8,128)(2,1)} custom-call(s32[3]{0:T(128)} %pad_add_fusion.place_ref, bf16[512,3072]{1,0:T(8,128)(2,1)} %query_ref.7, bf16[4,2,96,512]{3,2,1,0:T(8,128)(2,1)} %copy-done.8, f32[48,64]{1,0:T(8,128)} %gain_ref.7, f32[48,64]{1,0:T(8,128)} %bias_ref.7, ...), custom_call_target="tpu_custom_call", output_to_operand_aliasing={{}: (5, {})} | custom-call | tf_op jit(solution)/shard_map/fast_output/pallas_call | solution.py:276
  (150 shorter events, 67.3 us)
Async XLA Ops:
  6.3 26.4 %collective-permute-start = (bf16[512,1536]{1,0:T(8,128)(2,1)}, bf16[512,1536]{1,0:T(8,128)(2,1)S(1)}, u32[]{:S(2)}, u32[]{:S(2)}) collective-permute-start(bf16[512,1536]{1,0:T(8,128)(2,1)} %get-tuple-element.21), channel_id=1, source_target_pairs={{0,4},{4,0},{8,12},{12,8},{16,20},{20,16},{24,28},{28,24},{1,5},{5... | collective-permute-start | bytes 4718600 | tf_op jit(solution)/shard_map/ppermute | solution.py:315
  6.8 25.9 %collective-permute-start.1 = (bf16[512,1536]{1,0:T(8,128)(2,1)}, bf16[512,1536]{1,0:T(8,128)(2,1)S(1)}, u32[]{:S(2)}, u32[]{:S(2)}) collective-permute-start(bf16[512,1536]{1,0:T(8,128)(2,1)} %get-tuple-element.22), channel_id=1, source_target_pairs={{0,4},{4,0},{8,12},{12,8},{16,20},{20,16},{24,28},{28,24},{1,5},{5... | collective-permute-start | bytes 4718600 | tf_op jit(solution)/shard_map/ppermute | solution.py:315
  10.0 8.3 %collective-permute-start.12 = (bf16[96,512]{1,0:T(8,128)(2,1)S(1)}, bf16[96,512]{1,0:T(8,128)(2,1)S(1)}, u32[]{:S(2)}, u32[]{:S(2)}) collective-permute-start(bf16[96,512]{1,0:T(8,128)(2,1)S(1)} %convert_element_type.161), channel_id=1, source_target_pairs={{0,24},{4,28},{8,16},{12,20},{16,8},{20,12},{24,0},{28,4},{1,25},{... | collective-permute-start | bytes 294920 | tf_op jit(solution)/shard_map/ppermute | solution.py:320
  12.4 9.1 %collective-permute-start.11 = (bf16[96,512]{1,0:T(8,128)(2,1)S(1)}, bf16[96,512]{1,0:T(8,128)(2,1)S(1)}, u32[]{:S(2)}, u32[]{:S(2)}) collective-permute-start(bf16[96,512]{1,0:T(8,128)(2,1)S(1)} %convert_element_type.161), channel_id=1, source_target_pairs={{0,16},{4,20},{8,24},{12,28},{16,0},{20,4},{24,8},{28,12},{1,17},{... | collective-permute-start | bytes 294920 | tf_op jit(solution)/shard_map/ppermute | solution.py:320
  14.2 10.5 %collective-permute-start.4 = (bf16[2,96,512]{2,1,0:T(8,128)(2,1)S(1)}, bf16[2,96,512]{2,1,0:T(8,128)(2,1)S(1)}, u32[]{:S(2)}, u32[]{:S(2)}) collective-permute-start(bf16[2,96,512]{2,1,0:T(8,128)(2,1)S(1)} %pad_maximum_fusion.2.refs_6_), channel_id=1, source_target_pairs={{0,1},{1,0},{2,3},{3,2},{4,5},{5,4},{6,7},{7,6},{8,9},{9,8},{10,11... | collective-permute-start | bytes 589832 | tf_op jit(solution)/shard_map/ppermute | solution.py:325
  21.6 8.7 %collective-permute-start.6 = (bf16[2,96,512]{2,1,0:T(8,128)(2,1)S(1)}, bf16[2,96,512]{2,1,0:T(8,128)(2,1)S(1)}, u32[]{:S(2)}, u32[]{:S(2)}) collective-permute-start(bf16[2,96,512]{2,1,0:T(8,128)(2,1)S(1)} %pad_maximum_fusion.2.refs_6_), channel_id=1, source_target_pairs={{0,3},{1,2},{2,1},{3,0},{4,7},{5,6},{6,5},{7,4},{8,11},{9,10},{10,... | collective-permute-start | bytes 589832 | tf_op jit(solution)/shard_map/ppermute | solution.py:325
  24.7 23.9 %collective-permute-start.13 = (bf16[2,96,512]{2,1,0:T(8,128)(2,1)}, bf16[2,96,512]{2,1,0:T(8,128)(2,1)}, u32[]{:S(2)}, u32[]{:S(2)}) collective-permute-start(bf16[2,96,512]{2,1,0:T(8,128)(2,1)} %pad_maximum_fusion.3.refs_6_), channel_id=1, source_target_pairs={{0,1},{1,0},{2,3},{3,2},{4,5},{5,4},{6,7},{7,6},{8,9},{9,8},{10,11... | collective-permute-start | bytes 589832 | tf_op jit(solution)/shard_map/ppermute | solution.py:325
  25.2 25.8 %collective-permute-start.14 = (bf16[2,96,512]{2,1,0:T(8,128)(2,1)}, bf16[2,96,512]{2,1,0:T(8,128)(2,1)}, u32[]{:S(2)}, u32[]{:S(2)}) collective-permute-start(bf16[2,96,512]{2,1,0:T(8,128)(2,1)} %pad_maximum_fusion.3.refs_6_), channel_id=1, source_target_pairs={{0,2},{1,3},{2,0},{3,1},{4,6},{5,7},{6,4},{7,5},{8,10},{9,11},{10,... | collective-permute-start | bytes 589832 | tf_op jit(solution)/shard_map/ppermute | solution.py:325
  30.2 20.8 %collective-permute-start.15 = (bf16[2,96,512]{2,1,0:T(8,128)(2,1)}, bf16[2,96,512]{2,1,0:T(8,128)(2,1)}, u32[]{:S(2)}, u32[]{:S(2)}) collective-permute-start(bf16[2,96,512]{2,1,0:T(8,128)(2,1)} %pad_maximum_fusion.3.refs_6_), channel_id=1, source_target_pairs={{0,3},{1,2},{2,1},{3,0},{4,7},{5,6},{6,5},{7,4},{8,11},{9,10},{10,... | collective-permute-start | bytes 589832 | tf_op jit(solution)/shard_map/ppermute | solution.py:325
  47.5 17.8 %collective-permute-start.7 = (bf16[2,96,512]{2,1,0:T(8,128)(2,1)}, bf16[2,96,512]{2,1,0:T(8,128)(2,1)S(1)}, u32[]{:S(2)}, u32[]{:S(2)}) collective-permute-start(bf16[2,96,512]{2,1,0:T(8,128)(2,1)} %get-tuple-element.24), channel_id=1, source_target_pairs={{0,1},{1,0},{2,3},{3,2},{4,5},{5,4},{6,7},{7,6},{8,9},{9,8},{10,11... | collective-permute-start | bytes 589832 | tf_op jit(solution)/shard_map/ppermute | solution.py:325
  48.1 19.7 %collective-permute-start.8 = (bf16[2,96,512]{2,1,0:T(8,128)(2,1)}, bf16[2,96,512]{2,1,0:T(8,128)(2,1)S(1)}, u32[]{:S(2)}, u32[]{:S(2)}) collective-permute-start(bf16[2,96,512]{2,1,0:T(8,128)(2,1)} %get-tuple-element.25), channel_id=1, source_target_pairs={{0,2},{1,3},{2,0},{3,1},{4,6},{5,7},{6,4},{7,5},{8,10},{9,11},{10,... | collective-permute-start | bytes 589832 | tf_op jit(solution)/shard_map/ppermute | solution.py:325
  48.6 19.2 %collective-permute-start.9 = (bf16[2,96,512]{2,1,0:T(8,128)(2,1)}, bf16[2,96,512]{2,1,0:T(8,128)(2,1)S(1)}, u32[]{:S(2)}, u32[]{:S(2)}) collective-permute-start(bf16[2,96,512]{2,1,0:T(8,128)(2,1)} %get-tuple-element.26), channel_id=1, source_target_pairs={{0,3},{1,2},{2,1},{3,0},{4,7},{5,6},{6,5},{7,4},{8,11},{9,10},{10,... | collective-permute-start | bytes 589832 | tf_op jit(solution)/shard_map/ppermute | solution.py:325
  67.9 12.9 %collective-permute-start.10 = (bf16[96,512]{1,0:T(8,128)(2,1)S(1)}, bf16[96,512]{1,0:T(8,128)(2,1)S(1)}, u32[]{:S(2)}, u32[]{:S(2)}) collective-permute-start(bf16[96,512]{1,0:T(8,128)(2,1)S(1)} %fusion.6), channel_id=1, source_target_pairs={{0,8},{4,12},{8,0},{12,4},{16,24},{20,28},{24,16},{28,20},{1,9},{5... | collective-permute-start | bytes 294920 | tf_op jit(solution)/shard_map/ppermute | solution.py:320
  96.4 20.5 %collective-permute-start.31 = (bf16[2,96,512]{2,1,0:T(8,128)(2,1)S(1)}, bf16[2,96,512]{2,1,0:T(8,128)(2,1)S(1)}, u32[]{:S(2)}, u32[]{:S(2)}) collective-permute-start(bf16[2,96,512]{2,1,0:T(8,128)(2,1)S(1)} %pad_maximum_fusion.5.refs_6_), channel_id=1, source_target_pairs={{0,1},{1,0},{2,3},{3,2},{4,5},{5,4},{6,7},{7,6},{8,9},{9,8},{10,11... | collective-permute-start | bytes 589832 | tf_op jit(solution)/shard_map/ppermute | solution.py:325
  97.6 20.9 %collective-permute-start.32 = (bf16[2,96,512]{2,1,0:T(8,128)(2,1)S(1)}, bf16[2,96,512]{2,1,0:T(8,128)(2,1)S(1)}, u32[]{:S(2)}, u32[]{:S(2)}) collective-permute-start(bf16[2,96,512]{2,1,0:T(8,128)(2,1)S(1)} %pad_maximum_fusion.5.refs_6_), channel_id=1, source_target_pairs={{0,2},{1,3},{2,0},{3,1},{4,6},{5,7},{6,4},{7,5},{8,10},{9,11},{10,... | collective-permute-start | bytes 589832 | tf_op jit(solution)/shard_map/ppermute | solution.py:325
  98.5 20.0 %collective-permute-start.33 = (bf16[2,96,512]{2,1,0:T(8,128)(2,1)S(1)}, bf16[2,96,512]{2,1,0:T(8,128)(2,1)S(1)}, u32[]{:S(2)}, u32[]{:S(2)}) collective-permute-start(bf16[2,96,512]{2,1,0:T(8,128)(2,1)S(1)} %pad_maximum_fusion.5.refs_6_), channel_id=1, source_target_pairs={{0,3},{1,2},{2,1},{3,0},{4,7},{5,6},{6,5},{7,4},{8,11},{9,10},{10,... | collective-permute-start | bytes 589832 | tf_op jit(solution)/shard_map/ppermute | solution.py:325
  114.9 20.0 %collective-permute-start.25 = (bf16[2,96,512]{2,1,0:T(8,128)(2,1)}, bf16[2,96,512]{2,1,0:T(8,128)(2,1)S(1)}, u32[]{:S(2)}, u32[]{:S(2)}) collective-permute-start(bf16[2,96,512]{2,1,0:T(8,128)(2,1)} %get-tuple-element.32), channel_id=1, source_target_pairs={{0,1},{1,0},{2,3},{3,2},{4,5},{5,4},{6,7},{7,6},{8,9},{9,8},{10,11... | collective-permute-start | bytes 589832 | tf_op jit(solution)/shard_map/ppermute | solution.py:325
  115.8 20.7 %collective-permute-start.26 = (bf16[2,96,512]{2,1,0:T(8,128)(2,1)}, bf16[2,96,512]{2,1,0:T(8,128)(2,1)S(1)}, u32[]{:S(2)}, u32[]{:S(2)}) collective-permute-start(bf16[2,96,512]{2,1,0:T(8,128)(2,1)} %get-tuple-element.33), channel_id=1, source_target_pairs={{0,2},{1,3},{2,0},{3,1},{4,6},{5,7},{6,4},{7,5},{8,10},{9,11},{10,... | collective-permute-start | bytes 589832 | tf_op jit(solution)/shard_map/ppermute | solution.py:325
  116.9 19.7 %collective-permute-start.27 = (bf16[2,96,512]{2,1,0:T(8,128)(2,1)}, bf16[2,96,512]{2,1,0:T(8,128)(2,1)S(1)}, u32[]{:S(2)}, u32[]{:S(2)}) collective-permute-start(bf16[2,96,512]{2,1,0:T(8,128)(2,1)} %get-tuple-element.34), channel_id=1, source_target_pairs={{0,3},{1,2},{2,1},{3,0},{4,7},{5,6},{6,5},{7,4},{8,11},{9,10},{10,... | collective-permute-start | bytes 589832 | tf_op jit(solution)/shard_map/ppermute | solution.py:325
  136.7 10.0 %collective-permute-start.28 = (bf16[96,512]{1,0:T(8,128)(2,1)S(1)}, bf16[96,512]{1,0:T(8,128)(2,1)S(1)}, u32[]{:S(2)}, u32[]{:S(2)}) collective-permute-start(bf16[96,512]{1,0:T(8,128)(2,1)S(1)} %fusion.9), channel_id=1, source_target_pairs={{0,8},{4,12},{8,0},{12,4},{16,24},{20,28},{24,16},{28,20},{1,9},{5... | collective-permute-start | bytes 294920 | tf_op jit(solution)/shard_map/ppermute | solution.py:320
  153.5 9.3 %collective-permute-start.39 = (bf16[96,512]{1,0:T(8,128)(2,1)S(1)}, bf16[96,512]{1,0:T(8,128)(2,1)S(1)}, u32[]{:S(2)}, u32[]{:S(2)}) collective-permute-start(bf16[96,512]{1,0:T(8,128)(2,1)S(1)} %get-tuple-element.39), channel_id=1, source_target_pairs={{0,16},{4,20},{8,24},{12,28},{16,0},{20,4},{24,8},{28,12},{1,17},{... | collective-permute-start | bytes 294920 | tf_op jit(solution)/shard_map/ppermute | solution.py:320
  164.0 8.4 %collective-permute-start.42 = (bf16[2,96,512]{2,1,0:T(8,128)(2,1)S(1)}, bf16[2,96,512]{2,1,0:T(8,128)(2,1)S(1)}, u32[]{:S(2)}, u32[]{:S(2)}) collective-permute-start(bf16[2,96,512]{2,1,0:T(8,128)(2,1)S(1)} %get-tuple-element.51), channel_id=1, source_target_pairs={{0,2},{1,3},{2,0},{3,1},{4,6},{5,7},{6,4},{7,5},{8,10},{9,11},{10,... | collective-permute-start | bytes 589832 | tf_op jit(solution)/shard_map/ppermute | solution.py:325
  168.3 15.6 %collective-permute-start.49 = (bf16[4,2,96,512]{3,2,1,0:T(8,128)(2,1)S(1)}, bf16[4,2,96,512]{3,2,1,0:T(8,128)(2,1)S(1)}, u32[]{:S(2)}, u32[]{:S(2)}) collective-permute-start(bf16[4,2,96,512]{3,2,1,0:T(8,128)(2,1)S(1)} %pad_maximum_fusion.1.weight_ref), channel_id=1, source_target_pairs={{0,4},{4,0},{8,12},{12,8},{16,20},{20,16},{24,28},{28,24},{1,5},{5... | collective-permute-start | bytes 2359304 | tf_op jit(solution)/shard_map/ppermute | solution.py:315
  172.5 17.9 %collective-permute-start.44 = (bf16[4,2,96,512]{3,2,1,0:T(8,128)(2,1)S(1)}, bf16[4,2,96,512]{3,2,1,0:T(8,128)(2,1)S(1)}, u32[]{:S(2)}, u32[]{:S(2)}) collective-permute-start(bf16[4,2,96,512]{3,2,1,0:T(8,128)(2,1)S(1)} %pad_maximum_fusion.weight_ref), channel_id=1, source_target_pairs={{0,4},{4,0},{8,12},{12,8},{16,20},{20,16},{24,28},{28,24},{1,5},{5... | collective-permute-start | bytes 2359304 | tf_op jit(solution)/shard_map/ppermute | solution.py:315
  (50 other events, 373.8 us)

commit v4 on v3

--- a/solution.py
+++ b/solution.py
@@ -6,6 +6,7 @@
 from jax.experimental import pallas as pl
 from jax.experimental.pallas import tpu as pltpu
 from jax.sharding import PartitionSpec as P
+
 
 STEPS = 2
 
@@ -139,7 +140,7 @@
 
     def compare(i):
         j, (key, value), cols, rows, own = at(i)
-        base, mats, gain, bias, scaled, pick = const[j]
+        _, _, gain, bias, scaled, _ = const[j]
         inverse = lax.rsqrt(state.pop((i, "spread")) + 1e-06)
         unit = state.pop((i, "centre")) * inverse
         target = value[:, cols].astype(F32) - key[:, cols].astype(F32)
@@ -187,6 +188,10 @@
                 out[g] = sums_ref[pl.ds(g * members * rows_own + at, rows_own), :]
 
 
+def vmem(x):
+    return pltpu.with_memory_space_constraint(x, pltpu.VMEM)
+
+
 def gradient(place, own, far, rates, weights, gain, bias, total, lag, pairs=1, lags=(0, 1, 2, 3, 4, 5, 6)):
     tokens = own[0].shape[0]
     heads, size = gain.shape
@@ -199,15 +204,16 @@
     far_spec = pl.BlockSpec((tokens, wide), lambda i, place: (0, (zof(i, place) * per + i * pairs % per) // pairs))
     whole = lambda shape: pl.BlockSpec(shape, lambda i, place: (0,) * len(shape))
     mat = whole((groups, rows_own, two))
+    held = pl.BlockSpec(memory_space=pltpu.VMEM)
     rows = groups * members * rows_own
     return pl.pallas_call(
         functools.partial(grad_kernel, size, lags, pairs, per, lag, total),
-        out_shape=[jax.ShapeDtypeStruct((groups, rows_own, two), BF)] * members,
+        out_shape=[pltpu.VMEM((groups, rows_own, two), BF)] * members,
         grid_spec=pltpu.PrefetchScalarGridSpec(
             num_scalar_prefetch=1,
             grid=(groups * per // pairs,),
-            in_specs=[own_spec] * 2 + [far_spec] * 2 + [whole((heads, tokens))] * 2 + [mat] * members + [whole((heads, size))] * 2,
-            out_specs=[mat] * members,
+            in_specs=[own_spec] * 2 + [far_spec] * 2 + [held] * (4 + members),
+            out_specs=[held] * members,
             scratch_shapes=[
                 pltpu.VMEM((rows, two), BF),
                 pltpu.VMEM((rows, two), BF),
@@ -218,14 +224,15 @@
                 pltpu.VMEM((2 * tokens, heads), BF),
             ],
         ),
+        compiler_params=pltpu.CompilerParams(vmem_limit_bytes=48 << 20),
         name="fast_gradient",
-    )(place, *own, *far, *rates, *weights, gain, bias)
+    )(place, *own, *far, *map(vmem, rates), *map(vmem, weights), vmem(gain), vmem(bias))
 
 
 def output_kernel(size, chunk, lags, pairs, per, lag, flip, place_ref, query_ref, weight_ref, gain_ref, bias_ref, *refs):
     out_ref, whole_ref = refs[-2:]
     step = pl.program_id(0)
-    members, groups, rows_own, two = weight_ref.shape
+    members, _, rows_own, _ = weight_ref.shape
 
     @pl.when(step == 0)
     def _():
@@ -267,11 +274,10 @@
 def output(place, queries, weights, gain, bias, before, lag, flip, pairs=1, chunk=256, lags=(0, 1, 2, 3)):
     tokens, model = queries.shape
     members, groups, rows_own, two = weights.shape
-    heads, size = gain.shape
+    _, size = gain.shape
     per = members * rows_own // (2 * size)
     column = lambda i, place: (((place[0] ^ (i * pairs // per + lag)) * 2 + (place[1] ^ flip)) * per + i * pairs % per) // pairs
     col = pl.BlockSpec((tokens, pairs * 2 * size), lambda i, place: (0, column(i, place)))
-    whole = lambda shape: pl.BlockSpec(shape, lambda i, place: (0,) * len(shape))
     more = [] if before is None else [before]
     return pl.pallas_call(
         functools.partial(output_kernel, size, chunk, lags, pairs, per, lag, flip),
@@ -279,13 +285,14 @@
         grid_spec=pltpu.PrefetchScalarGridSpec(
             num_scalar_prefetch=1,
             grid=(groups * per // pairs,),
-            in_specs=[col, whole(weights.shape)] + [whole((heads, size))] * 2 + [pl.BlockSpec(memory_space=pl.ANY)] * len(more),
+            in_specs=[col] + [pl.BlockSpec(memory_space=pltpu.VMEM)] * 3 + [pl.BlockSpec(memory_space=pl.ANY)] * len(more),
             out_specs=col,
             scratch_shapes=[pltpu.VMEM((groups * members * rows_own, two), BF)],
         ),
         input_output_aliases={5: 0} if more else {},
+        compiler_params=pltpu.CompilerParams(vmem_limit_bytes=48 << 20),
         name="fast_output",
-    )(place, queries, weights, gain, bias, *more)
+    )(place, queries, vmem(weights), vmem(gain), vmem(bias), *more)
 
 
 def pick_kernel(place_ref, *refs):
@@ -327,16 +334,26 @@
 
 def fetch(fast, groups, members, chunks):
     narrow = fast.astype(BF)
-    held = [narrow] + [z_shift(narrow, s) for s in range(1, groups)]
-    return [(lambda mine: [mine] + [plane_shift(mine, s) for s in range(1, members)])(jnp.stack(held[at : at + count])) for at, count in chunks]
+    held = [narrow]
+    for s in range(1, groups):
+        held.append(z_shift(narrow, s))
+    weights = []
+    for at, count in chunks:
+        mine = jnp.stack(held[at : at + count])
+        weights.append([mine])
+        for s in range(1, members):
+            weights[-1].append(plane_shift(mine, s))
+    return weights
 
 
 def collect(parts, groups, members, chunks):
-    sums = []
+    sums = {}
     for part, (at, count) in zip(parts, chunks):
-        arrived = [plane_shift(part[s], s) for s in range(1, members)]
+        arrived = [part[0]]
+        for s in range(1, members):
+            arrived.append(plane_shift(part[s], s))
         for g in range(count):
-            sums.append(sum([a[g].astype(F32) for a in [part[0]] + arrived]))
+            sums[at + g] = sum([a[g].astype(F32) for a in arrived])
     total = sums[0]
     for s in range(1, groups):
         total = total + z_shift(sums[s].astype(BF), s).astype(F32)
@@ -351,30 +368,37 @@
     total = key_rows.shape[0] * 2 * groups * members
     gx = lax.axis_index("gx")
     place = jnp.stack([gx // 2, gx % 2, lax.axis_index("gy")]).astype(jnp.int32)
-    chunks = [(0, groups // 2), (groups // 2, groups - groups // 2)]
+    half = groups // 2
+    near, remote = (0, half), (half, groups - half)
+    orders = [(near, remote)] * (STEPS + 1)
+    pairs = members * fast_weights.shape[0] // (2 * size)
+    pairs = pairs if pairs <= 3 else 1
     fast, moment = (fast_weights, momentum)
-    weights = fetch(fast, groups, members, chunks)
+    weights = fetch(fast, groups, members, orders[0])
     key_send, value_send = pick(place, (key_rows, value_rows), groups, 1)
-    far = (core_swap(key_send), core_swap(value_send))
+    far = (core_swap(key_send),)
+    far += (core_swap(value_send),)
     own = (key_rows, value_rows)
     rates = (token_rates.T, core_swap(token_rates).T)
-    pairs = members * fast.shape[0] // (2 * size)
-    pairs = pairs if pairs <= 3 else 1
     for step in range(STEPS):
-        parts = [
-            gradient(place, own, far, rates, w, norm_gain, norm_bias, total, at, pairs)
-            for w, (at, count) in zip(weights, chunks)
-        ]
-        grad = collect(parts, groups, members, chunks)
+        parts = []
+        for k, (w, (at, count)) in enumerate(zip(weights, orders[step])):
+            turn = place if k == 0 else lax.optimization_barrier((place, parts[-1][0]))[0]
+            parts.append(gradient(turn, own, far, rates, w, norm_gain, norm_bias, total, at, pairs))
+        grad = collect(parts, groups, members, orders[step])
         moment = momentum_keep * moment + grad
         fast = fast - inner_rate * moment
-        weights = fetch(fast, groups, members, chunks)
-    mixed = None
-    whole = [jnp.stack(w) for w in weights]
-    twin = [core_swap(w) for w in whole]
-    for flip, ws in enumerate((whole, twin)):
-        for w, (at, count) in zip(ws, chunks):
-            mixed = output(place, query_rows, w, norm_gain, norm_bias, mixed, at, flip, pairs, min(512, query_rows.shape[0]))
+        weights = fetch(fast, groups, members, orders[step + 1])
+    chunk = min(512, query_rows.shape[0])
+    mixed, twins = None, []
+    for w, (at, count) in zip(weights, orders[STEPS]):
+        if mixed is not None:
+            *w, mixed = lax.optimization_barrier((*w, mixed))
+        whole = jnp.stack(w)
+        twins.append(core_swap(whole))
+        mixed = output(place, query_rows, whole, norm_gain, norm_bias, mixed, at, 0, pairs, chunk)
+    for w, (at, count) in zip(twins, orders[STEPS]):
+        mixed = output(place, query_rows, w, norm_gain, norm_bias, mixed, at, 1, pairs, chunk)
     return (mixed, fast, moment)
 
 
@@ -414,6 +438,7 @@
         second = dot(dsecond_t[mine], active_ref[:, cols])
         out_ref[mine, width:] = (second - jnp.mean(second, axis=0, keepdims=True)).astype(out_ref.dtype)
 
+
 def plain_apply_kernel(size, chunk, kind, query_ref, packed_ref, gain_ref, bias_ref, out_ref):
     tokens = query_ref.shape[0]
     first_w, second_w = blocks(packed_ref[...], size)
@@ -429,6 +454,7 @@
         spread = dot((centre * centre).astype(jnp.bfloat16), mean)
         unit = centre * lax.rsqrt(spread + 1e-06)
         out_ref[rows, :] = (queries.astype(jnp.float32) + unit * gain + bias).astype(out_ref.dtype)
+
 
 def plain_gradient(keys, values, rates, packed, gain, bias, total, size, chunk=128, kind=jnp.float32):
     tokens = keys.shape[0]
@@ -447,6 +473,7 @@
         name="plain_gradient",
     )(keys, values, rates, packed, gain.reshape(pairs, 1, 2 * size), bias.reshape(pairs, 1, 2 * size))
 
+
 def plain_output(queries, packed, gain, bias, size, chunk=128, kind=jnp.float32):
     tokens = queries.shape[0]
     rows, two = packed.shape
@@ -477,7 +504,7 @@
         inner = lax.all_gather(fast.astype(BF), "gy", axis=0, tiled=True)
         return lax.all_gather(inner, "gx", axis=0, tiled=True)
 
-    for step in range(STEPS):
+    for _ in range(STEPS):
         part = plain_gradient(key_rows, value_rows, rates, whole(fast), norm_gain, norm_bias, total, size)
         outer = lax.psum_scatter(part, "gx", scatter_dimension=0, tiled=True)
         grad = lax.psum_scatter(outer, "gy", scatter_dimension=0, tiled=True).astype(F32)
@@ -493,14 +520,15 @@
 
 def solution(mesh):
     rows = P(("gx", "gy"), None)
+    gx, gy = mesh.shape["gx"], mesh.shape["gy"]
 
     def run(*args):
         rows_own = args[0].shape[1] // mesh.size
         size = args[6].shape[1]
-        gx, gy = mesh.shape["gx"], mesh.shape["gy"]
         paired = gx % 4 == 0 and power_of_two(gx) and power_of_two(gy)
         even = rows_own % 32 == 0 and (rows_own * gy) % (2 * size) == 0
         body = per_device if paired and even else plain_device
+
         return jax.shard_map(
             body,
             mesh=mesh,

time: 198 us -> 178 us (0.90)
  Pallas kernels: 80.4 us -> 69.6 us
  starting transfers between devices: 70.6 us -> 60.4 us
  waiting for transfers between devices: 34.1 us -> 44.1 us
  local copies, waits for them, and re-layouts: 6.13 us -> 0.03 us
  other arithmetic: 4.83 us -> 2.32 us
    ppermute x15, starting transfers between devices: 32.5 us -> 20.5 us  [z_shift(): return lax.ppermute(x, 'gx', [(i, i ^ 2 * s) for i in range(n)])]
    ppermute x30, waiting for transfers between devices: 15.5 us -> 24.6 us  [plane_shift(): return lax.ppermute(x, 'gy', [(i, i ^ s) for i in range(n)])]
    unnamed x48 -> x14, local copies, waits for them, and re-layouts: 6.13 us -> 0.03 us
    pallas_call x4, Pallas kernels: 52.8 us -> 47 us  [gradient(): pl.pallas_call(functools.partial(grad_kernel, size, lags, pairs, per, lag...]
    pallas_call x4, Pallas kernels: 22.6 us -> 17.5 us  [output(): pl.pallas_call(functools.partial(output_kernel, size, chunk, lags, pairs,...]
    ppermute x15, waiting for transfers between devices: 17.4 us -> 19.5 us  [z_shift(): return lax.ppermute(x, 'gx', [(i, i ^ 2 * s) for i in range(n)])]
  transfers between devices with their start and end apart: 50 -> 50, of which waited for: 18 -> 21; matrix products, arithmetic and copies ran while one was open for 2% -> 0% of each run, Pallas kernels for 35% -> 27%
where the time goes in v4:
time: 178 us; the launch traced here: 177 us
  Pallas kernels  69.6 us (39%)
  starting transfers between devices  60.4 us (34%)
  waiting for transfers between devices  44.1 us (25%)
  other arithmetic  2.32 us (1%)
    pallas_call x4, Pallas kernels, gradient(): pl.pallas_call(functools.partial(grad_kernel, size, lags, pairs, per, lag...  47 us
    ppermute x30, starting transfers between devices, plane_shift(): return lax.ppermute(x, 'gy', [(i, i ^ s) for i in range(n)])  39.1 us
    ppermute x30, waiting for transfers between devices, plane_shift(): return lax.ppermute(x, 'gy', [(i, i ^ s) for i in range(n)])  24.6 us
    ppermute x15, starting transfers between devices, z_shift(): return lax.ppermute(x, 'gx', [(i, i ^ 2 * s) for i in range(n)])  20.5 us
    ppermute x15, waiting for transfers between devices, z_shift(): return lax.ppermute(x, 'gx', [(i, i ^ 2 * s) for i in range(n)])  19.5 us
    pallas_call x4, Pallas kernels, output(): pl.pallas_call(functools.partial(output_kernel, size, chunk, lags, pairs,...  17.5 us
    pallas_call x1, Pallas kernels, pick(): pl.pallas_call(pick_kernel, out_shape=[jax.ShapeDtypeStruct((tokens, grou...  5.13 us
  transfers between devices with their start and end apart: 50, of which 21 were waited for; matrix products, arithmetic and copies ran while one was open for 0% of the time, Pallas kernels for 27%

profile of v4, /device:TPU:0, one launch (start us, length us, event | category | flops | bytes accessed | tf_op | source)
XLA Modules:
  0.0 177.3 jit_solution(7128323130894119951)
XLA Ops:
  1.3 5.1 %pick.1 = (bf16[512,1536]{1,0:T(8,128)(2,1)}, bf16[512,1536]{1,0:T(8,128)(2,1)}) custom-call(s32[3]{0:T(128)} %pad_add_fusion.place_ref, bf16[512,3072]{1,0:T(8,128)(2,1)} %refs_0_.9, bf16[512,3072]{1,0:T(8,128)(2,1)} %refs_1_.9), custom_call_target="tpu_custom_call" | custom-call | tf_op jit(solution)/shard_map/pick/pallas_call | solution.py:307
  7.0 4.1 %collective-permute-start.11 = (bf16[96,512]{1,0:T(8,128)(2,1)S(1)}, bf16[96,512]{1,0:T(8,128)(2,1)S(1)}, u32[]{:S(2)}, u32[]{:S(2)}) collective-permute-start(bf16[96,512]{1,0:T(8,128)(2,1)S(1)} %convert_element_type.161), channel_id=1, source_target_pairs={{0,16},{4,20},{8,24},{12,28},{16,0},{20,4},{24,8},{28,12},{1,17},{... | collective-permute-start | bytes 294920 | tf_op jit(solution)/shard_map/ppermute | solution.py:327
  12.7 3.5 %collective-permute-done.3 = bf16[96,512]{1,0:T(8,128)(2,1)S(1)} collective-permute-done((bf16[96,512]{1,0:T(8,128)(2,1)S(1)}, bf16[96,512]{1,0:T(8,128)(2,1)S(1)}, u32[]{:S(2)}, u32[]{:S(2)}) %collective-permute-start.3) | collective-permute-done | bytes 98336 | tf_op jit(solution)/shard_map/ppermute | solution.py:327
  17.2 2.9 %collective-permute-start.6 = (bf16[2,96,512]{2,1,0:T(8,128)(2,1)S(1)}, bf16[2,96,512]{2,1,0:T(8,128)(2,1)S(1)}, u32[]{:S(2)}, u32[]{:S(2)}) collective-permute-start(bf16[2,96,512]{2,1,0:T(8,128)(2,1)S(1)} %pad_maximum_fusion.2.refs_6_), channel_id=1, source_target_pairs={{0,3},{1,2},{2,1},{3,0},{4,7},{5,6},{6,5},{7,4},{8,11},{9,10},{10,... | collective-permute-start | bytes 589832 | tf_op jit(solution)/shard_map/ppermute | solution.py:332
  22.4 3.5 %collective-permute-done.6.refs_9_ = bf16[2,96,512]{2,1,0:T(8,128)(2,1)S(1)} collective-permute-done((bf16[2,96,512]{2,1,0:T(8,128)(2,1)S(1)}, bf16[2,96,512]{2,1,0:T(8,128)(2,1)S(1)}, u32[]{:S(2)}, u32[]{:S(2)}) %collective-permute-start.6) | collective-permute-done | bytes 196640 | tf_op jit(solution)/shard_map/ppermute | solution.py:332
  25.9 2.9 %collective-permute-start.15 = (bf16[2,96,512]{2,1,0:T(8,128)(2,1)S(1)}, bf16[2,96,512]{2,1,0:T(8,128)(2,1)S(1)}, u32[]{:S(2)}, u32[]{:S(2)}) collective-permute-start(bf16[2,96,512]{2,1,0:T(8,128)(2,1)S(1)} %pad_maximum_fusion.3.refs_6_), channel_id=1, source_target_pairs={{0,3},{1,2},{2,1},{3,0},{4,7},{5,6},{6,5},{7,4},{8,11},{9,10},{10,... | collective-permute-start | bytes 589832 | tf_op jit(solution)/shard_map/ppermute | solution.py:332
  33.6 11.6 %fast_gradient.4 = (bf16[2,96,512]{2,1,0:T(8,128)(2,1)S(1)}, bf16[2,96,512]{2,1,0:T(8,128)(2,1)S(1)}, bf16[2,96,512]{2,1,0:T(8,128)(2,1)S(1)}, bf16[2,96,512]{2,1,0:T(8,128)(2,1)S(1)}) custom-call(s32[3]{0:T(128)S(1)} %copy-done.4, bf16[512,3072]{1,0:T(8,128)(2,1)} %refs_0_.9, bf16[512,3072]{1,0:T(8,128)(2,1)} %refs_1_.9, ...), custom_call_target="tpu_custom_call" | custom-call | tf_op jit(solution)/shard_map/fast_gradient/pallas_call | solution.py:209
  45.3 11.8 %fast_gradient.5 = (bf16[2,96,512]{2,1,0:T(8,128)(2,1)S(1)}, bf16[2,96,512]{2,1,0:T(8,128)(2,1)S(1)}, bf16[2,96,512]{2,1,0:T(8,128)(2,1)S(1)}, bf16[2,96,512]{2,1,0:T(8,128)(2,1)S(1)}) custom-call(s32[3]{0:T(128)S(1)} %copy-done.4, bf16[512,3072]{1,0:T(8,128)(2,1)} %refs_0_.9, bf16[512,3072]{1,0:T(8,128)(2,1)} %refs_1_.9, ...), custom_call_target="tpu_custom_call" | custom-call | tf_op jit(solution)/shard_map/fast_gradient/pallas_call | solution.py:209
  57.8 2.9 %collective-permute-start.18 = (bf16[2,96,512]{2,1,0:T(8,128)(2,1)S(1)}, bf16[2,96,512]{2,1,0:T(8,128)(2,1)S(1)}, u32[]{:S(2)}, u32[]{:S(2)}) collective-permute-start(bf16[2,96,512]{2,1,0:T(8,128)(2,1)S(1)} %get-tuple-element.38), channel_id=1, source_target_pairs={{0,3},{1,2},{2,1},{3,0},{4,7},{5,6},{6,5},{7,4},{8,11},{9,10},{10,... | collective-permute-start | bytes 589832 | tf_op jit(solution)/shard_map/ppermute | solution.py:332
  61.3 3.7 %collective-permute-done.16 = bf16[2,96,512]{2,1,0:T(8,128)(2,1)S(1)} collective-permute-done((bf16[2,96,512]{2,1,0:T(8,128)(2,1)S(1)}, bf16[2,96,512]{2,1,0:T(8,128)(2,1)S(1)}, u32[]{:S(2)}, u32[]{:S(2)}) %collective-permute-start.16) | collective-permute-done | bytes 196640 | tf_op jit(solution)/shard_map/ppermute | solution.py:332
  65.0 4.6 %collective-permute-done.17 = bf16[2,96,512]{2,1,0:T(8,128)(2,1)S(1)} collective-permute-done((bf16[2,96,512]{2,1,0:T(8,128)(2,1)S(1)}, bf16[2,96,512]{2,1,0:T(8,128)(2,1)S(1)}, u32[]{:S(2)}, u32[]{:S(2)}) %collective-permute-start.17) | collective-permute-done | bytes 196640 | tf_op jit(solution)/shard_map/ppermute | solution.py:332
  73.4 2.8 %collective-permute-done.8 = bf16[2,96,512]{2,1,0:T(8,128)(2,1)S(1)} collective-permute-done((bf16[2,96,512]{2,1,0:T(8,128)(2,1)S(1)}, bf16[2,96,512]{2,1,0:T(8,128)(2,1)S(1)}, u32[]{:S(2)}, u32[]{:S(2)}) %collective-permute-start.8) | collective-permute-done | bytes 196640 | tf_op jit(solution)/shard_map/ppermute | solution.py:332
  78.0 3.0 %collective-permute-done.10 = bf16[96,512]{1,0:T(8,128)(2,1)S(1)} collective-permute-done((bf16[96,512]{1,0:T(8,128)(2,1)S(1)}, bf16[96,512]{1,0:T(8,128)(2,1)S(1)}, u32[]{:S(2)}, u32[]{:S(2)}) %collective-permute-start.10) | collective-permute-done | bytes 98336 | tf_op jit(solution)/shard_map/ppermute | solution.py:327
  87.4 2.1 %collective-permute-start.23 = (bf16[2,96,512]{2,1,0:T(8,128)(2,1)S(1)}, bf16[2,96,512]{2,1,0:T(8,128)(2,1)S(1)}, u32[]{:S(2)}, u32[]{:S(2)}) collective-permute-start(bf16[2,96,512]{2,1,0:T(8,128)(2,1)S(1)} %pad_maximum_fusion.4.refs_6_), channel_id=1, source_target_pairs={{0,2},{1,3},{2,0},{3,1},{4,6},{5,7},{6,4},{7,5},{8,10},{9,11},{10,... | collective-permute-start | bytes 589832 | tf_op jit(solution)/shard_map/ppermute | solution.py:332
  94.1 2.6 %collective-permute-start.31 = (bf16[2,96,512]{2,1,0:T(8,128)(2,1)S(1)}, bf16[2,96,512]{2,1,0:T(8,128)(2,1)S(1)}, u32[]{:S(2)}, u32[]{:S(2)}) collective-permute-start(bf16[2,96,512]{2,1,0:T(8,128)(2,1)S(1)} %pad_maximum_fusion.5.refs_6_), channel_id=1, source_target_pairs={{0,1},{1,0},{2,3},{3,2},{4,5},{5,4},{6,7},{7,6},{8,9},{9,8},{10,11... | collective-permute-start | bytes 589832 | tf_op jit(solution)/shard_map/ppermute | solution.py:332
  96.8 2.7 %collective-permute-done.23.refs_8_ = bf16[2,96,512]{2,1,0:T(8,128)(2,1)S(1)} collective-permute-done((bf16[2,96,512]{2,1,0:T(8,128)(2,1)S(1)}, bf16[2,96,512]{2,1,0:T(8,128)(2,1)S(1)}, u32[]{:S(2)}, u32[]{:S(2)}) %collective-permute-start.23) | collective-permute-done | bytes 196640 | tf_op jit(solution)/shard_map/ppermute | solution.py:332
  99.4 11.6 %fast_gradient.6 = (bf16[2,96,512]{2,1,0:T(8,128)(2,1)S(1)}, bf16[2,96,512]{2,1,0:T(8,128)(2,1)S(1)}, bf16[2,96,512]{2,1,0:T(8,128)(2,1)S(1)}, bf16[2,96,512]{2,1,0:T(8,128)(2,1)S(1)}) custom-call(s32[3]{0:T(128)S(1)} %copy-done.4, bf16[512,3072]{1,0:T(8,128)(2,1)} %refs_0_.9, bf16[512,3072]{1,0:T(8,128)(2,1)} %refs_1_.9, ...), custom_call_target="tpu_custom_call" | custom-call | tf_op jit(solution)/shard_map/fast_gradient/pallas_call | solution.py:209
  114.6 11.9 %fast_gradient.7 = (bf16[2,96,512]{2,1,0:T(8,128)(2,1)S(1)}, bf16[2,96,512]{2,1,0:T(8,128)(2,1)S(1)}, bf16[2,96,512]{2,1,0:T(8,128)(2,1)S(1)}, bf16[2,96,512]{2,1,0:T(8,128)(2,1)S(1)}) custom-call(s32[3]{0:T(128)S(1)} %copy-done.4, bf16[512,3072]{1,0:T(8,128)(2,1)} %refs_0_.9, bf16[512,3072]{1,0:T(8,128)(2,1)} %refs_1_.9, ...), custom_call_target="tpu_custom_call" | custom-call | tf_op jit(solution)/shard_map/fast_gradient/pallas_call | solution.py:209
  133.2 2.2 %collective-permute-done.36 = bf16[2,96,512]{2,1,0:T(8,128)(2,1)S(1)} collective-permute-done((bf16[2,96,512]{2,1,0:T(8,128)(2,1)S(1)}, bf16[2,96,512]{2,1,0:T(8,128)(2,1)S(1)}, u32[]{:S(2)}, u32[]{:S(2)}) %collective-permute-start.36) | collective-permute-done | bytes 196640 | tf_op jit(solution)/shard_map/ppermute | solution.py:332
  138.2 5.9 %collective-permute-done.37 = bf16[96,512]{1,0:T(8,128)(2,1)S(1)} collective-permute-done((bf16[96,512]{1,0:T(8,128)(2,1)S(1)}, bf16[96,512]{1,0:T(8,128)(2,1)S(1)}, u32[]{:S(2)}, u32[]{:S(2)}) %collective-permute-start.37) | collective-permute-done | bytes 98336 | tf_op jit(solution)/shard_map/ppermute | solution.py:327
  159.2 4.4 %fast_output.4.refs_0_ = bf16[512,3072]{1,0:T(8,128)(2,1)} custom-call(s32[3]{0:T(128)S(1)} %copy-done.4, bf16[512,3072]{1,0:T(8,128)(2,1)S(1)} %copy-done, bf16[4,2,96,512]{3,2,1,0:T(8,128)(2,1)S(1)} %pad_maximum_fusion.weight_ref, f32[48,64]{1,0:T(8,128)S(1)} %copy-done.2, f32[48,64]{1,0:T(8,128)S(1)} %copy-done.3), custom_call_target="tpu_custom_call" | custom-call | tf_op jit(solution)/shard_map/fast_output/pallas_call | solution.py:282
  164.2 4.4 %fast_output.5.refs_0_ = bf16[512,3072]{1,0:T(8,128)(2,1)} custom-call(s32[3]{0:T(128)S(1)} %copy-done.4, bf16[512,3072]{1,0:T(8,128)(2,1)S(1)} %copy-done, bf16[4,2,96,512]{3,2,1,0:T(8,128)(2,1)S(1)} %pad_maximum_fusion.1.weight_ref, f32[48,64]{1,0:T(8,128)S(1)} %copy-done.2, f32[48,64]{1,0:T(8,128)S(1)} %copy-done.3, ...), custom_call_target="tpu_custom_call", output_to_operand_aliasing={{}: (5, {})} | custom-call | tf_op jit(solution)/shard_map/fast_output/pallas_call | solution.py:282
  168.6 4.4 %fast_output.6.refs_0_ = bf16[512,3072]{1,0:T(8,128)(2,1)} custom-call(s32[3]{0:T(128)S(1)} %copy-done.4, bf16[512,3072]{1,0:T(8,128)(2,1)S(1)} %copy-done, bf16[4,2,96,512]{3,2,1,0:T(8,128)(2,1)S(1)} %collective-permute-done.49.weight_ref, f32[48,64]{1,0:T(8,128)S(1)} %copy-done.2, f32[48,64]{1,0:T(8,128)S(1)} %copy-done.3, ...), custom_call_target="tpu_custom_call", output_to_operand_aliasing={{}: (5, {})} | custom-call | tf_op jit(solution)/shard_map/fast_output/pallas_call | solution.py:282
  173.0 4.4 %fast_output.7 = bf16[512,3072]{1,0:T(8,128)(2,1)} custom-call(s32[3]{0:T(128)S(1)} %copy-done.4, bf16[512,3072]{1,0:T(8,128)(2,1)S(1)} %copy-done, bf16[4,2,96,512]{3,2,1,0:T(8,128)(2,1)S(1)} %collective-permute-done.48.weight_ref, f32[48,64]{1,0:T(8,128)S(1)} %copy-done.2, f32[48,64]{1,0:T(8,128)S(1)} %copy-done.3, ...), custom_call_target="tpu_custom_call", output_to_operand_aliasing={{}: (5, {})} | custom-call | tf_op jit(solution)/shard_map/fast_output/pallas_call | solution.py:282
  (116 shorter events, 57.5 us)
Async XLA Ops:
  6.5 27.1 %collective-permute-start = (bf16[512,1536]{1,0:T(8,128)(2,1)}, bf16[512,1536]{1,0:T(8,128)(2,1)S(1)}, u32[]{:S(2)}, u32[]{:S(2)}) collective-permute-start(bf16[512,1536]{1,0:T(8,128)(2,1)} %get-tuple-element.28), channel_id=1, source_target_pairs={{0,4},{4,0},{8,12},{12,8},{16,20},{20,16},{24,28},{28,24},{1,5},{5... | collective-permute-start | bytes 4718600 | tf_op jit(solution)/shard_map/ppermute | solution.py:322
  6.9 26.6 %collective-permute-start.1 = (bf16[512,1536]{1,0:T(8,128)(2,1)}, bf16[512,1536]{1,0:T(8,128)(2,1)S(1)}, u32[]{:S(2)}, u32[]{:S(2)}) collective-permute-start(bf16[512,1536]{1,0:T(8,128)(2,1)} %get-tuple-element.29), channel_id=1, source_target_pairs={{0,4},{4,0},{8,12},{12,8},{16,20},{20,16},{24,28},{28,24},{1,5},{5... | collective-permute-start | bytes 4718600 | tf_op jit(solution)/shard_map/ppermute | solution.py:322
  7.0 10.2 %collective-permute-start.11 = (bf16[96,512]{1,0:T(8,128)(2,1)S(1)}, bf16[96,512]{1,0:T(8,128)(2,1)S(1)}, u32[]{:S(2)}, u32[]{:S(2)}) collective-permute-start(bf16[96,512]{1,0:T(8,128)(2,1)S(1)} %convert_element_type.161), channel_id=1, source_target_pairs={{0,16},{4,20},{8,24},{12,28},{16,0},{20,4},{24,8},{28,12},{1,17},{... | collective-permute-start | bytes 294920 | tf_op jit(solution)/shard_map/ppermute | solution.py:327
  17.2 8.7 %collective-permute-start.6 = (bf16[2,96,512]{2,1,0:T(8,128)(2,1)S(1)}, bf16[2,96,512]{2,1,0:T(8,128)(2,1)S(1)}, u32[]{:S(2)}, u32[]{:S(2)}) collective-permute-start(bf16[2,96,512]{2,1,0:T(8,128)(2,1)S(1)} %pad_maximum_fusion.2.refs_6_), channel_id=1, source_target_pairs={{0,3},{1,2},{2,1},{3,0},{4,7},{5,6},{6,5},{7,4},{8,11},{9,10},{10,... | collective-permute-start | bytes 589832 | tf_op jit(solution)/shard_map/ppermute | solution.py:332
  20.1 10.0 %collective-permute-start.5 = (bf16[2,96,512]{2,1,0:T(8,128)(2,1)S(1)}, bf16[2,96,512]{2,1,0:T(8,128)(2,1)S(1)}, u32[]{:S(2)}, u32[]{:S(2)}) collective-permute-start(bf16[2,96,512]{2,1,0:T(8,128)(2,1)S(1)} %pad_maximum_fusion.2.refs_6_), channel_id=1, source_target_pairs={{0,2},{1,3},{2,0},{3,1},{4,6},{5,7},{6,4},{7,5},{8,10},{9,11},{10,... | collective-permute-start | bytes 589832 | tf_op jit(solution)/shard_map/ppermute | solution.py:332
  20.9 11.1 %collective-permute-start.4 = (bf16[2,96,512]{2,1,0:T(8,128)(2,1)S(1)}, bf16[2,96,512]{2,1,0:T(8,128)(2,1)S(1)}, u32[]{:S(2)}, u32[]{:S(2)}) collective-permute-start(bf16[2,96,512]{2,1,0:T(8,128)(2,1)S(1)} %pad_maximum_fusion.2.refs_6_), channel_id=1, source_target_pairs={{0,1},{1,0},{2,3},{3,2},{4,5},{5,4},{6,7},{7,6},{8,9},{9,8},{10,11... | collective-permute-start | bytes 589832 | tf_op jit(solution)/shard_map/ppermute | solution.py:332
  25.9 19.3 %collective-permute-start.15 = (bf16[2,96,512]{2,1,0:T(8,128)(2,1)S(1)}, bf16[2,96,512]{2,1,0:T(8,128)(2,1)S(1)}, u32[]{:S(2)}, u32[]{:S(2)}) collective-permute-start(bf16[2,96,512]{2,1,0:T(8,128)(2,1)S(1)} %pad_maximum_fusion.3.refs_6_), channel_id=1, source_target_pairs={{0,3},{1,2},{2,1},{3,0},{4,7},{5,6},{6,5},{7,4},{8,11},{9,10},{10,... | collective-permute-start | bytes 589832 | tf_op jit(solution)/shard_map/ppermute | solution.py:332
  30.1 15.2 %collective-permute-start.14 = (bf16[2,96,512]{2,1,0:T(8,128)(2,1)S(1)}, bf16[2,96,512]{2,1,0:T(8,128)(2,1)S(1)}, u32[]{:S(2)}, u32[]{:S(2)}) collective-permute-start(bf16[2,96,512]{2,1,0:T(8,128)(2,1)S(1)} %pad_maximum_fusion.3.refs_6_), channel_id=1, source_target_pairs={{0,2},{1,3},{2,0},{3,1},{4,6},{5,7},{6,4},{7,5},{8,10},{9,11},{10,... | collective-permute-start | bytes 589832 | tf_op jit(solution)/shard_map/ppermute | solution.py:332
  32.0 13.2 %collective-permute-start.13 = (bf16[2,96,512]{2,1,0:T(8,128)(2,1)S(1)}, bf16[2,96,512]{2,1,0:T(8,128)(2,1)S(1)}, u32[]{:S(2)}, u32[]{:S(2)}) collective-permute-start(bf16[2,96,512]{2,1,0:T(8,128)(2,1)S(1)} %pad_maximum_fusion.3.refs_6_), channel_id=1, source_target_pairs={{0,1},{1,0},{2,3},{3,2},{4,5},{5,4},{6,7},{7,6},{8,9},{9,8},{10,11... | collective-permute-start | bytes 589832 | tf_op jit(solution)/shard_map/ppermute | solution.py:332
  57.7 11.8 %collective-permute-start.17 = (bf16[2,96,512]{2,1,0:T(8,128)(2,1)S(1)}, bf16[2,96,512]{2,1,0:T(8,128)(2,1)S(1)}, u32[]{:S(2)}, u32[]{:S(2)}) collective-permute-start(bf16[2,96,512]{2,1,0:T(8,128)(2,1)S(1)} %get-tuple-element.37), channel_id=1, source_target_pairs={{0,2},{1,3},{2,0},{3,1},{4,6},{5,7},{6,4},{7,5},{8,10},{9,11},{10,... | collective-permute-start | bytes 589832 | tf_op jit(solution)/shard_map/ppermute | solution.py:332
  57.8 11.8 %collective-permute-start.18 = (bf16[2,96,512]{2,1,0:T(8,128)(2,1)S(1)}, bf16[2,96,512]{2,1,0:T(8,128)(2,1)S(1)}, u32[]{:S(2)}, u32[]{:S(2)}) collective-permute-start(bf16[2,96,512]{2,1,0:T(8,128)(2,1)S(1)} %get-tuple-element.38), channel_id=1, source_target_pairs={{0,3},{1,2},{2,1},{3,0},{4,7},{5,6},{6,5},{7,4},{8,11},{9,10},{10,... | collective-permute-start | bytes 589832 | tf_op jit(solution)/shard_map/ppermute | solution.py:332
  60.7 12.8 %collective-permute-start.7 = (bf16[2,96,512]{2,1,0:T(8,128)(2,1)S(1)}, bf16[2,96,512]{2,1,0:T(8,128)(2,1)S(1)}, u32[]{:S(2)}, u32[]{:S(2)}) collective-permute-start(bf16[2,96,512]{2,1,0:T(8,128)(2,1)S(1)} %get-tuple-element.31), channel_id=1, source_target_pairs={{0,1},{1,0},{2,3},{3,2},{4,5},{5,4},{6,7},{7,6},{8,9},{9,8},{10,11... | collective-permute-start | bytes 589832 | tf_op jit(solution)/shard_map/ppermute | solution.py:332
  61.2 15.0 %collective-permute-start.8 = (bf16[2,96,512]{2,1,0:T(8,128)(2,1)S(1)}, bf16[2,96,512]{2,1,0:T(8,128)(2,1)S(1)}, u32[]{:S(2)}, u32[]{:S(2)}) collective-permute-start(bf16[2,96,512]{2,1,0:T(8,128)(2,1)S(1)} %get-tuple-element.32), channel_id=1, source_target_pairs={{0,2},{1,3},{2,0},{3,1},{4,6},{5,7},{6,4},{7,5},{8,10},{9,11},{10,... | collective-permute-start | bytes 589832 | tf_op jit(solution)/shard_map/ppermute | solution.py:332
  65.0 11.3 %collective-permute-start.9 = (bf16[2,96,512]{2,1,0:T(8,128)(2,1)S(1)}, bf16[2,96,512]{2,1,0:T(8,128)(2,1)S(1)}, u32[]{:S(2)}, u32[]{:S(2)}) collective-permute-start(bf16[2,96,512]{2,1,0:T(8,128)(2,1)S(1)} %get-tuple-element.33), channel_id=1, source_target_pairs={{0,3},{1,2},{2,1},{3,0},{4,7},{5,6},{6,5},{7,4},{8,11},{9,10},{10,... | collective-permute-start | bytes 589832 | tf_op jit(solution)/shard_map/ppermute | solution.py:332
  87.4 12.1 %collective-permute-start.23 = (bf16[2,96,512]{2,1,0:T(8,128)(2,1)S(1)}, bf16[2,96,512]{2,1,0:T(8,128)(2,1)S(1)}, u32[]{:S(2)}, u32[]{:S(2)}) collective-permute-start(bf16[2,96,512]{2,1,0:T(8,128)(2,1)S(1)} %pad_maximum_fusion.4.refs_6_), channel_id=1, source_target_pairs={{0,2},{1,3},{2,0},{3,1},{4,6},{5,7},{6,4},{7,5},{8,10},{9,11},{10,... | collective-permute-start | bytes 589832 | tf_op jit(solution)/shard_map/ppermute | solution.py:332
  89.5 9.9 %collective-permute-start.22 = (bf16[2,96,512]{2,1,0:T(8,128)(2,1)S(1)}, bf16[2,96,512]{2,1,0:T(8,128)(2,1)S(1)}, u32[]{:S(2)}, u32[]{:S(2)}) collective-permute-start(bf16[2,96,512]{2,1,0:T(8,128)(2,1)S(1)} %pad_maximum_fusion.4.refs_6_), channel_id=1, source_target_pairs={{0,1},{1,0},{2,3},{3,2},{4,5},{5,4},{6,7},{7,6},{8,9},{9,8},{10,11... | collective-permute-start | bytes 589832 | tf_op jit(solution)/shard_map/ppermute | solution.py:332
  91.2 21.9 %collective-permute-start.33 = (bf16[2,96,512]{2,1,0:T(8,128)(2,1)S(1)}, bf16[2,96,512]{2,1,0:T(8,128)(2,1)S(1)}, u32[]{:S(2)}, u32[]{:S(2)}) collective-permute-start(bf16[2,96,512]{2,1,0:T(8,128)(2,1)S(1)} %pad_maximum_fusion.5.refs_6_), channel_id=1, source_target_pairs={{0,3},{1,2},{2,1},{3,0},{4,7},{5,6},{6,5},{7,4},{8,11},{9,10},{10,... | collective-permute-start | bytes 589832 | tf_op jit(solution)/shard_map/ppermute | solution.py:332
  92.7 21.9 %collective-permute-start.32 = (bf16[2,96,512]{2,1,0:T(8,128)(2,1)S(1)}, bf16[2,96,512]{2,1,0:T(8,128)(2,1)S(1)}, u32[]{:S(2)}, u32[]{:S(2)}) collective-permute-start(bf16[2,96,512]{2,1,0:T(8,128)(2,1)S(1)} %pad_maximum_fusion.5.refs_6_), channel_id=1, source_target_pairs={{0,2},{1,3},{2,0},{3,1},{4,6},{5,7},{6,4},{7,5},{8,10},{9,11},{10,... | collective-permute-start | bytes 589832 | tf_op jit(solution)/shard_map/ppermute | solution.py:332
  94.1 20.5 %collective-permute-start.31 = (bf16[2,96,512]{2,1,0:T(8,128)(2,1)S(1)}, bf16[2,96,512]{2,1,0:T(8,128)(2,1)S(1)}, u32[]{:S(2)}, u32[]{:S(2)}) collective-permute-start(bf16[2,96,512]{2,1,0:T(8,128)(2,1)S(1)} %pad_maximum_fusion.5.refs_6_), channel_id=1, source_target_pairs={{0,1},{1,0},{2,3},{3,2},{4,5},{5,4},{6,7},{7,6},{8,9},{9,8},{10,11... | collective-permute-start | bytes 589832 | tf_op jit(solution)/shard_map/ppermute | solution.py:332
  111.1 17.5 %collective-permute-start.25 = (bf16[2,96,512]{2,1,0:T(8,128)(2,1)S(1)}, bf16[2,96,512]{2,1,0:T(8,128)(2,1)S(1)}, u32[]{:S(2)}, u32[]{:S(2)}) collective-permute-start(bf16[2,96,512]{2,1,0:T(8,128)(2,1)S(1)} %get-tuple-element.40), channel_id=1, source_target_pairs={{0,1},{1,0},{2,3},{3,2},{4,5},{5,4},{6,7},{7,6},{8,9},{9,8},{10,11... | collective-permute-start | bytes 589832 | tf_op jit(solution)/shard_map/ppermute | solution.py:332
  112.1 18.0 %collective-permute-start.26 = (bf16[2,96,512]{2,1,0:T(8,128)(2,1)S(1)}, bf16[2,96,512]{2,1,0:T(8,128)(2,1)S(1)}, u32[]{:S(2)}, u32[]{:S(2)}) collective-permute-start(bf16[2,96,512]{2,1,0:T(8,128)(2,1)S(1)} %get-tuple-element.41), channel_id=1, source_target_pairs={{0,2},{1,3},{2,0},{3,1},{4,6},{5,7},{6,4},{7,5},{8,10},{9,11},{10,... | collective-permute-start | bytes 589832 | tf_op jit(solution)/shard_map/ppermute | solution.py:332
  113.1 17.0 %collective-permute-start.27 = (bf16[2,96,512]{2,1,0:T(8,128)(2,1)S(1)}, bf16[2,96,512]{2,1,0:T(8,128)(2,1)S(1)}, u32[]{:S(2)}, u32[]{:S(2)}) collective-permute-start(bf16[2,96,512]{2,1,0:T(8,128)(2,1)S(1)} %get-tuple-element.42), channel_id=1, source_target_pairs={{0,3},{1,2},{2,1},{3,0},{4,7},{5,6},{6,5},{7,4},{8,11},{9,10},{10,... | collective-permute-start | bytes 589832 | tf_op jit(solution)/shard_map/ppermute | solution.py:332
  159.1 9.5 %collective-permute-start.49 = (bf16[4,2,96,512]{3,2,1,0:T(8,128)(2,1)S(1)}, bf16[4,2,96,512]{3,2,1,0:T(8,128)(2,1)S(1)}, u32[]{:S(2)}, u32[]{:S(2)}) collective-permute-start(bf16[4,2,96,512]{3,2,1,0:T(8,128)(2,1)S(1)} %pad_maximum_fusion.weight_ref), channel_id=1, source_target_pairs={{0,4},{4,0},{8,12},{12,8},{16,20},{20,16},{24,28},{28,24},{1,5},{5... | collective-permute-start | bytes 2359304 | tf_op jit(solution)/shard_map/ppermute | solution.py:322
  164.0 8.9 %collective-permute-start.48 = (bf16[4,2,96,512]{3,2,1,0:T(8,128)(2,1)S(1)}, bf16[4,2,96,512]{3,2,1,0:T(8,128)(2,1)S(1)}, u32[]{:S(2)}, u32[]{:S(2)}) collective-permute-start(bf16[4,2,96,512]{3,2,1,0:T(8,128)(2,1)S(1)} %pad_maximum_fusion.1.weight_ref), channel_id=1, source_target_pairs={{0,4},{4,0},{8,12},{12,8},{16,20},{20,16},{24,28},{28,24},{1,5},{5... | collective-permute-start | bytes 2359304 | tf_op jit(solution)/shard_map/ppermute | solution.py:322
  (33 other events, 362.8 us)

commit v5 on v4

--- a/solution.py
+++ b/solution.py
@@ -117,10 +117,14 @@
         pick = jnp.where(head_row == 2 * (first_pair + j) + head_col, 1.0, 0.0).astype(BF)
         const.append((base, blocks(whole_ref[pl.ds(base, 2 * size), :], size), gain, pair_row(bias_ref, first_pair + j), gain * (1.0 / total), pick))
     sources = ((key_own, value_own), (key_far, value_far))
+    starts = (first_pair * 2 * size, (zof * per + (step * pairs) % per) * 2 * size)
+
+    def columns(far, j):
+        return pl.ds(pl.multiple_of(starts[far] + j * 2 * size, 2 * size), 2 * size)
 
     def at(i):
         j, far = divmod(i, 2)
-        return j, sources[far], slice(2 * size * j, 2 * size * (j + 1)), pl.ds(far * tokens, tokens), pl.ds(i * tokens, tokens)
+        return j, sources[far], columns(far, j), pl.ds(far * tokens, tokens), pl.ds(i * tokens, tokens)
 
     def enter(i):
         j, (key, value), cols, rows, own = at(i)
@@ -166,7 +170,7 @@
             return
         base = const[j][0]
         both = pl.ds((i - 1) * tokens, 2 * tokens)
-        key_t = [source[0][:, cols].T for source in sources]
+        key_t = [source[0][:, columns(far, j)].T for far, source in enumerate(sources)]
         dsecond_t = dsecond_ref[both, :].T
         for head in range(2):
             part = slice(head * size, (head + 1) * size)
@@ -198,12 +202,6 @@
     members = len(weights)
     groups, rows_own, two = weights[0].shape
     per = members * rows_own // (2 * size)
-    zof = lambda i, place: place[0] ^ (i * pairs // per + lag)
-    wide = pairs * 2 * size
-    own_spec = pl.BlockSpec((tokens, wide), lambda i, place: (0, ((zof(i, place) * 2 + place[1]) * per + i * pairs % per) // pairs))
-    far_spec = pl.BlockSpec((tokens, wide), lambda i, place: (0, (zof(i, place) * per + i * pairs % per) // pairs))
-    whole = lambda shape: pl.BlockSpec(shape, lambda i, place: (0,) * len(shape))
-    mat = whole((groups, rows_own, two))
     held = pl.BlockSpec(memory_space=pltpu.VMEM)
     rows = groups * members * rows_own
     return pl.pallas_call(
@@ -212,7 +210,7 @@
         grid_spec=pltpu.PrefetchScalarGridSpec(
             num_scalar_prefetch=1,
             grid=(groups * per // pairs,),
-            in_specs=[own_spec] * 2 + [far_spec] * 2 + [held] * (4 + members),
+            in_specs=[held] * (8 + members),
             out_specs=[held] * members,
             scratch_shapes=[
                 pltpu.VMEM((rows, two), BF),
@@ -224,9 +222,9 @@
                 pltpu.VMEM((2 * tokens, heads), BF),
             ],
         ),
-        compiler_params=pltpu.CompilerParams(vmem_limit_bytes=48 << 20),
+        compiler_params=pltpu.CompilerParams(vmem_limit_bytes=40 << 20),
         name="fast_gradient",
-    )(place, *own, *far, *map(vmem, rates), *map(vmem, weights), vmem(gain), vmem(bias))
+    )(place, *map(vmem, own), *map(vmem, far), *map(vmem, rates), *map(vmem, weights), vmem(gain), vmem(bias))
 
 
 def output_kernel(size, chunk, lags, pairs, per, lag, flip, place_ref, query_ref, weight_ref, gain_ref, bias_ref, *refs):
@@ -249,14 +247,16 @@
 
     def at(i):
         j, k = divmod(i, count)
-        return const[j], (pl.ds(k * chunk, chunk), slice(2 * size * j, 2 * size * (j + 1)))
+        start = pl.multiple_of((first_pair + j) * 2 * size, 2 * size)
+        rows = pl.ds(k * chunk, chunk)
+        return const[j], (rows, pl.ds(start, 2 * size)), (rows, slice(2 * size * j, 2 * size * (j + 1)))
 
     def enter(i):
-        (mats, gain, bias), where = at(i)
+        (mats, gain, bias), where, target = at(i)
         state[i, "first"] = dot(query_ref[where], mats[0]).astype(BF)
 
     def bend(i):
-        (mats, gain, bias), where = at(i)
+        (mats, gain, bias), where, target = at(i)
         state[i, "centre"] = dot(activate(state.pop((i, "first")), BF, False), mats[1], NT)
 
     def measure(i):
@@ -264,9 +264,9 @@
         state[i, "spread"] = averaged((centre * centre).astype(BF), mean)
 
     def leave(i):
-        (mats, gain, bias), where = at(i)
+        (mats, gain, bias), where, target = at(i)
         unit = state.pop((i, "centre")) * lax.rsqrt(state.pop((i, "spread")) + 1e-06)
-        out_ref[where] = (query_ref[where].astype(F32) + unit * gain + bias).astype(BF)
+        out_ref[target] = (query_ref[where].astype(F32) + unit * gain + bias).astype(BF)
 
     staggered((enter, bend, measure, leave), lags, pairs * count)
 
@@ -285,36 +285,40 @@
         grid_spec=pltpu.PrefetchScalarGridSpec(
             num_scalar_prefetch=1,
             grid=(groups * per // pairs,),
-            in_specs=[col] + [pl.BlockSpec(memory_space=pltpu.VMEM)] * 3 + [pl.BlockSpec(memory_space=pl.ANY)] * len(more),
+            in_specs=[pl.BlockSpec(memory_space=pltpu.VMEM)] * 4 + [pl.BlockSpec(memory_space=pl.ANY)] * len(more),
             out_specs=col,
             scratch_shapes=[pltpu.VMEM((groups * members * rows_own, two), BF)],
         ),
         input_output_aliases={5: 0} if more else {},
-        compiler_params=pltpu.CompilerParams(vmem_limit_bytes=48 << 20),
+        compiler_params=pltpu.CompilerParams(vmem_limit_bytes=40 << 20),
         name="fast_output",
-    )(place, queries, vmem(weights), vmem(gain), vmem(bias), *more)
-
-
-def pick_kernel(place_ref, *refs):
+    )(place, vmem(queries), vmem(weights), vmem(gain), vmem(bias), *more)
+
+
+def pick_kernel(groups, flip, place_ref, *refs):
     half = len(refs) // 2
+    wide = refs[-1].shape[1] // groups
     for source, target in zip(refs[:half], refs[half:]):
-        target[...] = source[...]
+        for g in range(groups):
+            start = pl.multiple_of((2 * g + (place_ref[1] ^ flip)) * wide, wide)
+            target[:, g * wide : (g + 1) * wide] = source[:, pl.ds(start, wide)]
 
 
 def pick(place, arrays, groups, flip):
     tokens, model = arrays[0].shape
-    wide = model // (2 * groups)
+    held = pl.BlockSpec(memory_space=pltpu.VMEM)
     return pl.pallas_call(
-        pick_kernel,
-        out_shape=[jax.ShapeDtypeStruct((tokens, groups * wide), a.dtype) for a in arrays],
+        functools.partial(pick_kernel, groups, flip),
+        out_shape=[pltpu.VMEM((tokens, model // 2), a.dtype) for a in arrays],
         grid_spec=pltpu.PrefetchScalarGridSpec(
             num_scalar_prefetch=1,
-            grid=(groups,),
-            in_specs=[pl.BlockSpec((tokens, wide), lambda i, place: (0, 2 * i + (place[1] ^ flip)))] * len(arrays),
-            out_specs=[pl.BlockSpec((tokens, wide), lambda i, place: (0, i))] * len(arrays),
+            grid=(1,),
+            in_specs=[held] * len(arrays),
+            out_specs=[held] * len(arrays),
         ),
+        compiler_params=pltpu.CompilerParams(vmem_limit_bytes=32 << 20),
         name="pick",
-    )(place, *arrays)
+    )(place, *map(vmem, arrays))
 
 
 def core_swap(x):

time: 178 us -> 175 us (0.983)
  Pallas kernels: 69.6 us -> 61.5 us
  local copies, waits for them, and re-layouts: 0.03 us -> 3.82 us
  waiting for transfers between devices: 44.1 us -> 41.6 us
  starting transfers between devices: 60.4 us -> 62.6 us
    pallas_call x1, Pallas kernels: 5.13 us -> 0.83 us  [pick(): pl.pallas_call(functools.partial(pick_kernel, groups, flip), out_shape=[p...]
    pallas_call x4, Pallas kernels: 47 us -> 43 us  [gradient(): pl.pallas_call(functools.partial(grad_kernel, size, lags, pairs, per, lag...]
    unnamed x14 -> x20, local copies, waits for them, and re-layouts: 0.03 us -> 3.82 us
    ppermute x15, starting transfers between devices: 20.5 us -> 23 us  [z_shift(): return lax.ppermute(x, 'gx', [(i, i ^ 2 * s) for i in range(n)])]
  transfers between devices with their start and end apart: 50 -> 50, of which waited for: 21 -> 19; matrix products, arithmetic and copies ran while one was open for 0% -> 2% of each run, Pallas kernels for 27% -> 26%
where the time goes in v5:
time: 175 us
  starting transfers between devices  62.6 us (36%)
  Pallas kernels  61.5 us (35%)
  waiting for transfers between devices  41.6 us (24%)
  other arithmetic  4.04 us (2%)
  local copies, waits for them, and re-layouts  3.82 us (2%)
    pallas_call x4, Pallas kernels, gradient(): pl.pallas_call(functools.partial(grad_kernel, size, lags, pairs, per, lag...  43 us
    ppermute x30, starting transfers between devices, plane_shift(): return lax.ppermute(x, 'gy', [(i, i ^ s) for i in range(n)])  38.5 us
    ppermute x30, waiting for transfers between devices, plane_shift(): return lax.ppermute(x, 'gy', [(i, i ^ s) for i in range(n)])  23.2 us
    ppermute x15, starting transfers between devices, z_shift(): return lax.ppermute(x, 'gx', [(i, i ^ 2 * s) for i in range(n)])  23 us
    ppermute x15, waiting for transfers between devices, z_shift(): return lax.ppermute(x, 'gx', [(i, i ^ 2 * s) for i in range(n)])  18.4 us
    pallas_call x4, Pallas kernels, output(): pl.pallas_call(functools.partial(output_kernel, size, chunk, lags, pairs,...  17.7 us
    unnamed x20, local copies, waits for them, and re-layouts  3.82 us
  transfers between devices with their start and end apart: 50, of which 19 were waited for; matrix products, arithmetic and copies ran while one was open for 2% of the time, Pallas kernels for 26%

profile of v5, /device:TPU:0, one launch (start us, length us, event | category | flops | bytes accessed | tf_op | source)
XLA Modules:
  0.0 174.5 jit_solution(8774536125778168198)
XLA Ops:
  7.4 4.1 %collective-permute-start.11 = (bf16[96,512]{1,0:T(8,128)(2,1)S(1)}, bf16[96,512]{1,0:T(8,128)(2,1)S(1)}, u32[]{:S(2)}, u32[]{:S(2)}) collective-permute-start(bf16[96,512]{1,0:T(8,128)(2,1)S(1)} %convert_element_type.161), channel_id=1, source_target_pairs={{0,16},{4,20},{8,24},{12,28},{16,0},{20,4},{24,8},{28,12},{1,17},{... | collective-permute-start | bytes 294920 | tf_op jit(solution)/shard_map/ppermute | solution.py:331
  14.0 2.6 %collective-permute-done.3 = bf16[96,512]{1,0:T(8,128)(2,1)S(1)} collective-permute-done((bf16[96,512]{1,0:T(8,128)(2,1)S(1)}, bf16[96,512]{1,0:T(8,128)(2,1)S(1)}, u32[]{:S(2)}, u32[]{:S(2)}) %collective-permute-start.3) | collective-permute-done | bytes 98336 | tf_op jit(solution)/shard_map/ppermute | solution.py:331
  17.5 2.6 %collective-permute-start.6 = (bf16[2,96,512]{2,1,0:T(8,128)(2,1)S(1)}, bf16[2,96,512]{2,1,0:T(8,128)(2,1)S(1)}, u32[]{:S(2)}, u32[]{:S(2)}) collective-permute-start(bf16[2,96,512]{2,1,0:T(8,128)(2,1)S(1)} %pad_maximum_fusion.2.refs_6_), channel_id=1, source_target_pairs={{0,3},{1,2},{2,1},{3,0},{4,7},{5,6},{6,5},{7,4},{8,11},{9,10},{10,... | collective-permute-start | bytes 589832 | tf_op jit(solution)/shard_map/ppermute | solution.py:336
  22.6 3.6 %collective-permute-done.6.refs_9_ = bf16[2,96,512]{2,1,0:T(8,128)(2,1)S(1)} collective-permute-done((bf16[2,96,512]{2,1,0:T(8,128)(2,1)S(1)}, bf16[2,96,512]{2,1,0:T(8,128)(2,1)S(1)}, u32[]{:S(2)}, u32[]{:S(2)}) %collective-permute-start.6) | collective-permute-done | bytes 196640 | tf_op jit(solution)/shard_map/ppermute | solution.py:336
  26.2 2.7 %collective-permute-start.15 = (bf16[2,96,512]{2,1,0:T(8,128)(2,1)S(1)}, bf16[2,96,512]{2,1,0:T(8,128)(2,1)S(1)}, u32[]{:S(2)}, u32[]{:S(2)}) collective-permute-start(bf16[2,96,512]{2,1,0:T(8,128)(2,1)S(1)} %pad_maximum_fusion.3.refs_6_), channel_id=1, source_target_pairs={{0,3},{1,2},{2,1},{3,0},{4,7},{5,6},{6,5},{7,4},{8,11},{9,10},{10,... | collective-permute-start | bytes 589832 | tf_op jit(solution)/shard_map/ppermute | solution.py:336
  33.6 10.7 %fast_gradient.4 = (bf16[2,96,512]{2,1,0:T(8,128)(2,1)S(1)}, bf16[2,96,512]{2,1,0:T(8,128)(2,1)S(1)}, bf16[2,96,512]{2,1,0:T(8,128)(2,1)S(1)}, bf16[2,96,512]{2,1,0:T(8,128)(2,1)S(1)}) custom-call(s32[3]{0:T(128)S(1)} %pad_add_fusion.place_ref, bf16[512,3072]{1,0:T(8,128)(2,1)S(1)} %copy-done.1, bf16[512,3072]{1,0:T(8,128)(2,1)S(1)} %copy-done.3, ...), custom_call_target="tpu_custom_call" | custom-call | tf_op jit(solution)/shard_map/fast_gradient/pallas_call | solution.py:207
  44.4 10.7 %fast_gradient.5 = (bf16[2,96,512]{2,1,0:T(8,128)(2,1)S(1)}, bf16[2,96,512]{2,1,0:T(8,128)(2,1)S(1)}, bf16[2,96,512]{2,1,0:T(8,128)(2,1)S(1)}, bf16[2,96,512]{2,1,0:T(8,128)(2,1)S(1)}) custom-call(s32[3]{0:T(128)S(1)} %pad_add_fusion.place_ref, bf16[512,3072]{1,0:T(8,128)(2,1)S(1)} %copy-done.1, bf16[512,3072]{1,0:T(8,128)(2,1)S(1)} %copy-done.3, ...), custom_call_target="tpu_custom_call" | custom-call | tf_op jit(solution)/shard_map/fast_gradient/pallas_call | solution.py:207
  56.1 2.6 %collective-permute-start.18 = (bf16[2,96,512]{2,1,0:T(8,128)(2,1)S(1)}, bf16[2,96,512]{2,1,0:T(8,128)(2,1)S(1)}, u32[]{:S(2)}, u32[]{:S(2)}) collective-permute-start(bf16[2,96,512]{2,1,0:T(8,128)(2,1)S(1)} %get-tuple-element.38), channel_id=1, source_target_pairs={{0,3},{1,2},{2,1},{3,0},{4,7},{5,6},{6,5},{7,4},{8,11},{9,10},{10,... | collective-permute-start | bytes 589832 | tf_op jit(solution)/shard_map/ppermute | solution.py:336
  59.6 3.4 %collective-permute-done.16 = bf16[2,96,512]{2,1,0:T(8,128)(2,1)S(1)} collective-permute-done((bf16[2,96,512]{2,1,0:T(8,128)(2,1)S(1)}, bf16[2,96,512]{2,1,0:T(8,128)(2,1)S(1)}, u32[]{:S(2)}, u32[]{:S(2)}) %collective-permute-start.16) | collective-permute-done | bytes 196640 | tf_op jit(solution)/shard_map/ppermute | solution.py:336
  63.3 4.3 %collective-permute-done.17 = bf16[2,96,512]{2,1,0:T(8,128)(2,1)S(1)} collective-permute-done((bf16[2,96,512]{2,1,0:T(8,128)(2,1)S(1)}, bf16[2,96,512]{2,1,0:T(8,128)(2,1)S(1)}, u32[]{:S(2)}, u32[]{:S(2)}) %collective-permute-start.17) | collective-permute-done | bytes 196640 | tf_op jit(solution)/shard_map/ppermute | solution.py:336
  69.5 2.5 %collective-permute-start.20 = (bf16[96,512]{1,0:T(8,128)(2,1)S(1)}, bf16[96,512]{1,0:T(8,128)(2,1)S(1)}, u32[]{:S(2)}, u32[]{:S(2)}) collective-permute-start(bf16[96,512]{1,0:T(8,128)(2,1)S(1)} %get-tuple-element.61), channel_id=1, source_target_pairs={{0,24},{4,28},{8,16},{12,20},{16,8},{20,12},{24,0},{28,4},{1,25},{... | collective-permute-start | bytes 294920 | tf_op jit(solution)/shard_map/ppermute | solution.py:331
  72.1 2.2 %collective-permute-done.8 = bf16[2,96,512]{2,1,0:T(8,128)(2,1)S(1)} collective-permute-done((bf16[2,96,512]{2,1,0:T(8,128)(2,1)S(1)}, bf16[2,96,512]{2,1,0:T(8,128)(2,1)S(1)}, u32[]{:S(2)}, u32[]{:S(2)}) %collective-permute-start.8) | collective-permute-done | bytes 196640 | tf_op jit(solution)/shard_map/ppermute | solution.py:336
  76.0 3.0 %collective-permute-done.10 = bf16[96,512]{1,0:T(8,128)(2,1)S(1)} collective-permute-done((bf16[96,512]{1,0:T(8,128)(2,1)S(1)}, bf16[96,512]{1,0:T(8,128)(2,1)S(1)}, u32[]{:S(2)}, u32[]{:S(2)}) %collective-permute-start.10) | collective-permute-done | bytes 98336 | tf_op jit(solution)/shard_map/ppermute | solution.py:331
  89.4 2.2 %collective-permute-start.33 = (bf16[2,96,512]{2,1,0:T(8,128)(2,1)S(1)}, bf16[2,96,512]{2,1,0:T(8,128)(2,1)S(1)}, u32[]{:S(2)}, u32[]{:S(2)}) collective-permute-start(bf16[2,96,512]{2,1,0:T(8,128)(2,1)S(1)} %pad_maximum_fusion.5.refs_6_), channel_id=1, source_target_pairs={{0,3},{1,2},{2,1},{3,0},{4,7},{5,6},{6,5},{7,4},{8,11},{9,10},{10,... | collective-permute-start | bytes 589832 | tf_op jit(solution)/shard_map/ppermute | solution.py:336
  94.4 2.8 %collective-permute-done.23.refs_8_ = bf16[2,96,512]{2,1,0:T(8,128)(2,1)S(1)} collective-permute-done((bf16[2,96,512]{2,1,0:T(8,128)(2,1)S(1)}, bf16[2,96,512]{2,1,0:T(8,128)(2,1)S(1)}, u32[]{:S(2)}, u32[]{:S(2)}) %collective-permute-start.23) | collective-permute-done | bytes 196640 | tf_op jit(solution)/shard_map/ppermute | solution.py:336
  97.3 10.9 %fast_gradient.6 = (bf16[2,96,512]{2,1,0:T(8,128)(2,1)S(1)}, bf16[2,96,512]{2,1,0:T(8,128)(2,1)S(1)}, bf16[2,96,512]{2,1,0:T(8,128)(2,1)S(1)}, bf16[2,96,512]{2,1,0:T(8,128)(2,1)S(1)}) custom-call(s32[3]{0:T(128)S(1)} %pad_add_fusion.place_ref, bf16[512,3072]{1,0:T(8,128)(2,1)S(1)} %copy-done.1, bf16[512,3072]{1,0:T(8,128)(2,1)S(1)} %copy-done.3, ...), custom_call_target="tpu_custom_call" | custom-call | tf_op jit(solution)/shard_map/fast_gradient/pallas_call | solution.py:207
  111.7 10.7 %fast_gradient.7 = (bf16[2,96,512]{2,1,0:T(8,128)(2,1)S(1)}, bf16[2,96,512]{2,1,0:T(8,128)(2,1)S(1)}, bf16[2,96,512]{2,1,0:T(8,128)(2,1)S(1)}, bf16[2,96,512]{2,1,0:T(8,128)(2,1)S(1)}) custom-call(s32[3]{0:T(128)S(1)} %pad_add_fusion.place_ref, bf16[512,3072]{1,0:T(8,128)(2,1)S(1)} %copy-done.1, bf16[512,3072]{1,0:T(8,128)(2,1)S(1)} %copy-done.3, ...), custom_call_target="tpu_custom_call" | custom-call | tf_op jit(solution)/shard_map/fast_gradient/pallas_call | solution.py:207
  128.2 3.3 %collective-permute-done.35 = bf16[2,96,512]{2,1,0:T(8,128)(2,1)S(1)} collective-permute-done((bf16[2,96,512]{2,1,0:T(8,128)(2,1)S(1)}, bf16[2,96,512]{2,1,0:T(8,128)(2,1)S(1)}, u32[]{:S(2)}, u32[]{:S(2)}) %collective-permute-start.35) | collective-permute-done | bytes 196640 | tf_op jit(solution)/shard_map/ppermute | solution.py:336
  134.7 6.4 %collective-permute-done.37 = bf16[96,512]{1,0:T(8,128)(2,1)S(1)} collective-permute-done((bf16[96,512]{1,0:T(8,128)(2,1)S(1)}, bf16[96,512]{1,0:T(8,128)(2,1)S(1)}, u32[]{:S(2)}, u32[]{:S(2)}) %collective-permute-start.37) | collective-permute-done | bytes 98336 | tf_op jit(solution)/shard_map/ppermute | solution.py:331
  143.6 2.1 %collective-permute-start.40 = (bf16[96,512]{1,0:T(8,128)(2,1)S(1)}, bf16[96,512]{1,0:T(8,128)(2,1)S(1)}, u32[]{:S(2)}, u32[]{:S(2)}) collective-permute-start(bf16[96,512]{1,0:T(8,128)(2,1)S(1)} %get-tuple-element.53), channel_id=1, source_target_pairs={{0,24},{4,28},{8,16},{12,20},{16,8},{20,12},{24,0},{28,4},{1,25},{... | collective-permute-start | bytes 294920 | tf_op jit(solution)/shard_map/ppermute | solution.py:331
  156.1 4.6 %fast_output.4.refs_0_ = bf16[512,3072]{1,0:T(8,128)(2,1)} custom-call(s32[3]{0:T(128)S(1)} %pad_add_fusion.place_ref, bf16[512,3072]{1,0:T(8,128)(2,1)S(1)} %copy-done.4, bf16[4,2,96,512]{3,2,1,0:T(8,128)(2,1)S(1)} %pad_maximum_fusion.weight_ref, f32[48,64]{1,0:T(8,128)S(1)} %copy-done.6, f32[48,64]{1,0:T(8,128)S(1)} %copy-done.7), custom_call_target="tpu_custom_call" | custom-call | tf_op jit(solution)/shard_map/fast_output/pallas_call | solution.py:282
  161.4 4.4 %fast_output.5.refs_0_ = bf16[512,3072]{1,0:T(8,128)(2,1)} custom-call(s32[3]{0:T(128)S(1)} %pad_add_fusion.place_ref, bf16[512,3072]{1,0:T(8,128)(2,1)S(1)} %copy-done.4, bf16[4,2,96,512]{3,2,1,0:T(8,128)(2,1)S(1)} %pad_maximum_fusion.1.weight_ref, f32[48,64]{1,0:T(8,128)S(1)} %copy-done.6, f32[48,64]{1,0:T(8,128)S(1)} %copy-done.7, ...), custom_call_target="tpu_custom_call", output_to_operand_aliasing={{}: (5, {})} | custom-call | tf_op jit(solution)/shard_map/fast_output/pallas_call | solution.py:282
  165.8 4.4 %fast_output.6.refs_0_ = bf16[512,3072]{1,0:T(8,128)(2,1)} custom-call(s32[3]{0:T(128)S(1)} %pad_add_fusion.place_ref, bf16[512,3072]{1,0:T(8,128)(2,1)S(1)} %copy-done.4, bf16[4,2,96,512]{3,2,1,0:T(8,128)(2,1)S(1)} %collective-permute-done.49.weight_ref, f32[48,64]{1,0:T(8,128)S(1)} %copy-done.6, ...), custom_call_target="tpu_custom_call", output_to_operand_aliasing={{}: (5, {})} | custom-call | tf_op jit(solution)/shard_map/fast_output/pallas_call | solution.py:282
  170.2 4.4 %fast_output.7 = bf16[512,3072]{1,0:T(8,128)(2,1)} custom-call(s32[3]{0:T(128)S(1)} %pad_add_fusion.place_ref, bf16[512,3072]{1,0:T(8,128)(2,1)S(1)} %copy-done.4, bf16[4,2,96,512]{3,2,1,0:T(8,128)(2,1)S(1)} %collective-permute-done.48.weight_ref, f32[48,64]{1,0:T(8,128)S(1)} %copy-done.6, f32[48,64]{1,0:T(8,128)S(1)} %copy-done.7, ...), custom_call_target="tpu_custom_call", output_to_operand_aliasing={{}: (5, {})} | custom-call | tf_op jit(solution)/shard_map/fast_output/pallas_call | solution.py:282
  (122 shorter events, 62.5 us)
Async XLA Ops:
  5.4 28.2 %collective-permute-start = (bf16[512,1536]{1,0:T(8,128)(2,1)S(1)}, bf16[512,1536]{1,0:T(8,128)(2,1)S(1)}, u32[]{:S(2)}, u32[]{:S(2)}) collective-permute-start(bf16[512,1536]{1,0:T(8,128)(2,1)S(1)} %get-tuple-element.28), channel_id=1, source_target_pairs={{0,4},{4,0},{8,12},{12,8},{16,20},{20,16},{24,28},{28,24},{1,5},{5... | collective-permute-start | bytes 4718600 | tf_op jit(solution)/shard_map/ppermute | solution.py:326
  5.9 27.7 %collective-permute-start.1 = (bf16[512,1536]{1,0:T(8,128)(2,1)S(1)}, bf16[512,1536]{1,0:T(8,128)(2,1)S(1)}, u32[]{:S(2)}, u32[]{:S(2)}) collective-permute-start(bf16[512,1536]{1,0:T(8,128)(2,1)S(1)} %get-tuple-element.29), channel_id=1, source_target_pairs={{0,4},{4,0},{8,12},{12,8},{16,20},{20,16},{24,28},{28,24},{1,5},{5... | collective-permute-start | bytes 4718600 | tf_op jit(solution)/shard_map/ppermute | solution.py:326
  7.4 10.2 %collective-permute-start.11 = (bf16[96,512]{1,0:T(8,128)(2,1)S(1)}, bf16[96,512]{1,0:T(8,128)(2,1)S(1)}, u32[]{:S(2)}, u32[]{:S(2)}) collective-permute-start(bf16[96,512]{1,0:T(8,128)(2,1)S(1)} %convert_element_type.161), channel_id=1, source_target_pairs={{0,16},{4,20},{8,24},{12,28},{16,0},{20,4},{24,8},{28,12},{1,17},{... | collective-permute-start | bytes 294920 | tf_op jit(solution)/shard_map/ppermute | solution.py:331
  20.2 10.2 %collective-permute-start.5 = (bf16[2,96,512]{2,1,0:T(8,128)(2,1)S(1)}, bf16[2,96,512]{2,1,0:T(8,128)(2,1)S(1)}, u32[]{:S(2)}, u32[]{:S(2)}) collective-permute-start(bf16[2,96,512]{2,1,0:T(8,128)(2,1)S(1)} %pad_maximum_fusion.2.refs_6_), channel_id=1, source_target_pairs={{0,2},{1,3},{2,0},{3,1},{4,6},{5,7},{6,4},{7,5},{8,10},{9,11},{10,... | collective-permute-start | bytes 589832 | tf_op jit(solution)/shard_map/ppermute | solution.py:336
  21.1 11.0 %collective-permute-start.4 = (bf16[2,96,512]{2,1,0:T(8,128)(2,1)S(1)}, bf16[2,96,512]{2,1,0:T(8,128)(2,1)S(1)}, u32[]{:S(2)}, u32[]{:S(2)}) collective-permute-start(bf16[2,96,512]{2,1,0:T(8,128)(2,1)S(1)} %pad_maximum_fusion.2.refs_6_), channel_id=1, source_target_pairs={{0,1},{1,0},{2,3},{3,2},{4,5},{5,4},{6,7},{7,6},{8,9},{9,8},{10,11... | collective-permute-start | bytes 589832 | tf_op jit(solution)/shard_map/ppermute | solution.py:336
  26.2 18.2 %collective-permute-start.15 = (bf16[2,96,512]{2,1,0:T(8,128)(2,1)S(1)}, bf16[2,96,512]{2,1,0:T(8,128)(2,1)S(1)}, u32[]{:S(2)}, u32[]{:S(2)}) collective-permute-start(bf16[2,96,512]{2,1,0:T(8,128)(2,1)S(1)} %pad_maximum_fusion.3.refs_6_), channel_id=1, source_target_pairs={{0,3},{1,2},{2,1},{3,0},{4,7},{5,6},{6,5},{7,4},{8,11},{9,10},{10,... | collective-permute-start | bytes 589832 | tf_op jit(solution)/shard_map/ppermute | solution.py:336
  30.4 14.0 %collective-permute-start.14 = (bf16[2,96,512]{2,1,0:T(8,128)(2,1)S(1)}, bf16[2,96,512]{2,1,0:T(8,128)(2,1)S(1)}, u32[]{:S(2)}, u32[]{:S(2)}) collective-permute-start(bf16[2,96,512]{2,1,0:T(8,128)(2,1)S(1)} %pad_maximum_fusion.3.refs_6_), channel_id=1, source_target_pairs={{0,2},{1,3},{2,0},{3,1},{4,6},{5,7},{6,4},{7,5},{8,10},{9,11},{10,... | collective-permute-start | bytes 589832 | tf_op jit(solution)/shard_map/ppermute | solution.py:336
  32.1 12.3 %collective-permute-start.13 = (bf16[2,96,512]{2,1,0:T(8,128)(2,1)S(1)}, bf16[2,96,512]{2,1,0:T(8,128)(2,1)S(1)}, u32[]{:S(2)}, u32[]{:S(2)}) collective-permute-start(bf16[2,96,512]{2,1,0:T(8,128)(2,1)S(1)} %pad_maximum_fusion.3.refs_6_), channel_id=1, source_target_pairs={{0,1},{1,0},{2,3},{3,2},{4,5},{5,4},{6,7},{7,6},{8,9},{9,8},{10,11... | collective-permute-start | bytes 589832 | tf_op jit(solution)/shard_map/ppermute | solution.py:336
  55.7 11.8 %collective-permute-start.17 = (bf16[2,96,512]{2,1,0:T(8,128)(2,1)S(1)}, bf16[2,96,512]{2,1,0:T(8,128)(2,1)S(1)}, u32[]{:S(2)}, u32[]{:S(2)}) collective-permute-start(bf16[2,96,512]{2,1,0:T(8,128)(2,1)S(1)} %get-tuple-element.37), channel_id=1, source_target_pairs={{0,2},{1,3},{2,0},{3,1},{4,6},{5,7},{6,4},{7,5},{8,10},{9,11},{10,... | collective-permute-start | bytes 589832 | tf_op jit(solution)/shard_map/ppermute | solution.py:336
  56.1 11.5 %collective-permute-start.18 = (bf16[2,96,512]{2,1,0:T(8,128)(2,1)S(1)}, bf16[2,96,512]{2,1,0:T(8,128)(2,1)S(1)}, u32[]{:S(2)}, u32[]{:S(2)}) collective-permute-start(bf16[2,96,512]{2,1,0:T(8,128)(2,1)S(1)} %get-tuple-element.38), channel_id=1, source_target_pairs={{0,3},{1,2},{2,1},{3,0},{4,7},{5,6},{6,5},{7,4},{8,11},{9,10},{10,... | collective-permute-start | bytes 589832 | tf_op jit(solution)/shard_map/ppermute | solution.py:336
  58.7 13.4 %collective-permute-start.7 = (bf16[2,96,512]{2,1,0:T(8,128)(2,1)S(1)}, bf16[2,96,512]{2,1,0:T(8,128)(2,1)S(1)}, u32[]{:S(2)}, u32[]{:S(2)}) collective-permute-start(bf16[2,96,512]{2,1,0:T(8,128)(2,1)S(1)} %get-tuple-element.31), channel_id=1, source_target_pairs={{0,1},{1,0},{2,3},{3,2},{4,5},{5,4},{6,7},{7,6},{8,9},{9,8},{10,11... | collective-permute-start | bytes 589832 | tf_op jit(solution)/shard_map/ppermute | solution.py:336
  59.2 15.0 %collective-permute-start.8 = (bf16[2,96,512]{2,1,0:T(8,128)(2,1)S(1)}, bf16[2,96,512]{2,1,0:T(8,128)(2,1)S(1)}, u32[]{:S(2)}, u32[]{:S(2)}) collective-permute-start(bf16[2,96,512]{2,1,0:T(8,128)(2,1)S(1)} %get-tuple-element.32), channel_id=1, source_target_pairs={{0,2},{1,3},{2,0},{3,1},{4,6},{5,7},{6,4},{7,5},{8,10},{9,11},{10,... | collective-permute-start | bytes 589832 | tf_op jit(solution)/shard_map/ppermute | solution.py:336
  63.0 11.3 %collective-permute-start.9 = (bf16[2,96,512]{2,1,0:T(8,128)(2,1)S(1)}, bf16[2,96,512]{2,1,0:T(8,128)(2,1)S(1)}, u32[]{:S(2)}, u32[]{:S(2)}) collective-permute-start(bf16[2,96,512]{2,1,0:T(8,128)(2,1)S(1)} %get-tuple-element.33), channel_id=1, source_target_pairs={{0,3},{1,2},{2,1},{3,0},{4,7},{5,6},{6,5},{7,4},{8,11},{9,10},{10,... | collective-permute-start | bytes 589832 | tf_op jit(solution)/shard_map/ppermute | solution.py:336
  85.7 11.5 %collective-permute-start.23 = (bf16[2,96,512]{2,1,0:T(8,128)(2,1)S(1)}, bf16[2,96,512]{2,1,0:T(8,128)(2,1)S(1)}, u32[]{:S(2)}, u32[]{:S(2)}) collective-permute-start(bf16[2,96,512]{2,1,0:T(8,128)(2,1)S(1)} %pad_maximum_fusion.4.refs_6_), channel_id=1, source_target_pairs={{0,2},{1,3},{2,0},{3,1},{4,6},{5,7},{6,4},{7,5},{8,10},{9,11},{10,... | collective-permute-start | bytes 589832 | tf_op jit(solution)/shard_map/ppermute | solution.py:336
  87.2 10.1 %collective-permute-start.22 = (bf16[2,96,512]{2,1,0:T(8,128)(2,1)S(1)}, bf16[2,96,512]{2,1,0:T(8,128)(2,1)S(1)}, u32[]{:S(2)}, u32[]{:S(2)}) collective-permute-start(bf16[2,96,512]{2,1,0:T(8,128)(2,1)S(1)} %pad_maximum_fusion.4.refs_6_), channel_id=1, source_target_pairs={{0,1},{1,0},{2,3},{3,2},{4,5},{5,4},{6,7},{7,6},{8,9},{9,8},{10,11... | collective-permute-start | bytes 589832 | tf_op jit(solution)/shard_map/ppermute | solution.py:336
  89.4 20.6 %collective-permute-start.33 = (bf16[2,96,512]{2,1,0:T(8,128)(2,1)S(1)}, bf16[2,96,512]{2,1,0:T(8,128)(2,1)S(1)}, u32[]{:S(2)}, u32[]{:S(2)}) collective-permute-start(bf16[2,96,512]{2,1,0:T(8,128)(2,1)S(1)} %pad_maximum_fusion.5.refs_6_), channel_id=1, source_target_pairs={{0,3},{1,2},{2,1},{3,0},{4,7},{5,6},{6,5},{7,4},{8,11},{9,10},{10,... | collective-permute-start | bytes 589832 | tf_op jit(solution)/shard_map/ppermute | solution.py:336
  91.5 20.2 %collective-permute-start.32 = (bf16[2,96,512]{2,1,0:T(8,128)(2,1)S(1)}, bf16[2,96,512]{2,1,0:T(8,128)(2,1)S(1)}, u32[]{:S(2)}, u32[]{:S(2)}) collective-permute-start(bf16[2,96,512]{2,1,0:T(8,128)(2,1)S(1)} %pad_maximum_fusion.5.refs_6_), channel_id=1, source_target_pairs={{0,2},{1,3},{2,0},{3,1},{4,6},{5,7},{6,4},{7,5},{8,10},{9,11},{10,... | collective-permute-start | bytes 589832 | tf_op jit(solution)/shard_map/ppermute | solution.py:336
  92.9 18.9 %collective-permute-start.31 = (bf16[2,96,512]{2,1,0:T(8,128)(2,1)S(1)}, bf16[2,96,512]{2,1,0:T(8,128)(2,1)S(1)}, u32[]{:S(2)}, u32[]{:S(2)}) collective-permute-start(bf16[2,96,512]{2,1,0:T(8,128)(2,1)S(1)} %pad_maximum_fusion.5.refs_6_), channel_id=1, source_target_pairs={{0,1},{1,0},{2,3},{3,2},{4,5},{5,4},{6,7},{7,6},{8,9},{9,8},{10,11... | collective-permute-start | bytes 589832 | tf_op jit(solution)/shard_map/ppermute | solution.py:336
  108.2 16.1 %collective-permute-start.25 = (bf16[2,96,512]{2,1,0:T(8,128)(2,1)S(1)}, bf16[2,96,512]{2,1,0:T(8,128)(2,1)S(1)}, u32[]{:S(2)}, u32[]{:S(2)}) collective-permute-start(bf16[2,96,512]{2,1,0:T(8,128)(2,1)S(1)} %get-tuple-element.40), channel_id=1, source_target_pairs={{0,1},{1,0},{2,3},{3,2},{4,5},{5,4},{6,7},{7,6},{8,9},{9,8},{10,11... | collective-permute-start | bytes 589832 | tf_op jit(solution)/shard_map/ppermute | solution.py:336
  109.4 16.6 %collective-permute-start.26 = (bf16[2,96,512]{2,1,0:T(8,128)(2,1)S(1)}, bf16[2,96,512]{2,1,0:T(8,128)(2,1)S(1)}, u32[]{:S(2)}, u32[]{:S(2)}) collective-permute-start(bf16[2,96,512]{2,1,0:T(8,128)(2,1)S(1)} %get-tuple-element.41), channel_id=1, source_target_pairs={{0,2},{1,3},{2,0},{3,1},{4,6},{5,7},{6,4},{7,5},{8,10},{9,11},{10,... | collective-permute-start | bytes 589832 | tf_op jit(solution)/shard_map/ppermute | solution.py:336
  110.0 16.0 %collective-permute-start.27 = (bf16[2,96,512]{2,1,0:T(8,128)(2,1)S(1)}, bf16[2,96,512]{2,1,0:T(8,128)(2,1)S(1)}, u32[]{:S(2)}, u32[]{:S(2)}) collective-permute-start(bf16[2,96,512]{2,1,0:T(8,128)(2,1)S(1)} %get-tuple-element.42), channel_id=1, source_target_pairs={{0,3},{1,2},{2,1},{3,0},{4,7},{5,6},{6,5},{7,4},{8,11},{9,10},{10,... | collective-permute-start | bytes 589832 | tf_op jit(solution)/shard_map/ppermute | solution.py:336
  131.5 9.5 %collective-permute-start.37 = (bf16[96,512]{1,0:T(8,128)(2,1)S(1)}, bf16[96,512]{1,0:T(8,128)(2,1)S(1)}, u32[]{:S(2)}, u32[]{:S(2)}) collective-permute-start(bf16[96,512]{1,0:T(8,128)(2,1)S(1)} %get-tuple-element.58), channel_id=1, source_target_pairs={{0,16},{4,20},{8,24},{12,28},{16,0},{20,4},{24,8},{28,12},{1,17},{... | collective-permute-start | bytes 294920 | tf_op jit(solution)/shard_map/ppermute | solution.py:331
  156.0 9.8 %collective-permute-start.49 = (bf16[4,2,96,512]{3,2,1,0:T(8,128)(2,1)S(1)}, bf16[4,2,96,512]{3,2,1,0:T(8,128)(2,1)S(1)}, u32[]{:S(2)}, u32[]{:S(2)}) collective-permute-start(bf16[4,2,96,512]{3,2,1,0:T(8,128)(2,1)S(1)} %pad_maximum_fusion.weight_ref), channel_id=1, source_target_pairs={{0,4},{4,0},{8,12},{12,8},{16,20},{20,16},{24,28},{28,24},{1,5},{5... | collective-permute-start | bytes 2359304 | tf_op jit(solution)/shard_map/ppermute | solution.py:326
  161.0 9.2 %collective-permute-start.48 = (bf16[4,2,96,512]{3,2,1,0:T(8,128)(2,1)S(1)}, bf16[4,2,96,512]{3,2,1,0:T(8,128)(2,1)S(1)}, u32[]{:S(2)}, u32[]{:S(2)}) collective-permute-start(bf16[4,2,96,512]{3,2,1,0:T(8,128)(2,1)S(1)} %pad_maximum_fusion.1.weight_ref), channel_id=1, source_target_pairs={{0,4},{4,0},{8,12},{12,8},{16,20},{20,16},{24,28},{28,24},{1,5},{5... | collective-permute-start | bytes 2359304 | tf_op jit(solution)/shard_map/ppermute | solution.py:326
  (36 other events, 415.7 us)

commit v6 on v5

--- a/solution.py
+++ b/solution.py
@@ -102,19 +102,23 @@
     @pl.when(step == 0)
     def _():
         fill(whole_ref, weight_refs, mine, rows_own)
-        rate_ref[:tokens, :] = rate_own[...].T.astype(BF)
-        rate_ref[tokens:, :] = rate_far[...].T.astype(BF)
+        rate_ref[...] = jnp.zeros_like(rate_ref)
+        rate_ref[:tokens, :heads] = rate_own[...].T.astype(BF)
+        rate_ref[tokens:, :heads] = rate_far[...].T.astype(BF)
 
     mean = head_mean(size, 4)
-    head_row = lax.broadcasted_iota(jnp.int32, (heads, 2 * size), 0)
-    head_col = lax.broadcasted_iota(jnp.int32, (heads, 2 * size), 1) // size
-    zof = place_ref[0] ^ (step * pairs // per + lag)
+    lanes = 2 * size
+    block_row = lax.broadcasted_iota(jnp.int32, (lanes + rate_ref.shape[1], 2 * lanes), 0)
+    block_col = lax.broadcasted_iota(jnp.int32, (lanes + rate_ref.shape[1], 2 * lanes), 1)
+    same = (block_row // size == block_col // size) & (block_row < lanes)
+    zof = place_ref[0] ^ (lag[0] + lag[1] * (step * pairs // per))
     first_pair = (zof * 2 + place_ref[1]) * per + (step * pairs) % per
     const, state = [], {}
     for j in range(pairs):
         base = pl.multiple_of((step * pairs + j) * 2 * size, 2 * size)
         gain = pair_row(gain_ref, first_pair + j)
-        pick = jnp.where(head_row == 2 * (first_pair + j) + head_col, 1.0, 0.0).astype(BF)
+        chosen = (block_col >= lanes) & (block_row - lanes == 2 * (first_pair + j) + (block_col - lanes) // size)
+        pick = jnp.where(same, 1.0 / size, jnp.where(chosen, 1.0, 0.0)).astype(BF)
         const.append((base, blocks(whole_ref[pl.ds(base, 2 * size), :], size), gain, pair_row(bias_ref, first_pair + j), gain * (1.0 / total), pick))
     sources = ((key_own, value_own), (key_far, value_far))
     starts = (first_pair * 2 * size, (zof * per + (step * pairs) % per) * 2 * size)
@@ -139,8 +143,9 @@
 
     def measure(i):
         centre = state[i, "centre"]
-        state[i, "spread"] = averaged((centre * centre).astype(BF), mean)
-        state[i, "rate"] = dot(rate_ref[at(i)[3], :], const[at(i)[0]][5])
+        j, (key, value), cols, rows, own = at(i)
+        both = dot(jnp.concatenate([(centre * centre).astype(BF), rate_ref[rows, :]], axis=1), const[j][5])
+        state[i, "spread"], state[i, "rate"] = both[:, : 2 * size], both[:, 2 * size :]
 
     def compare(i):
         j, (key, value), cols, rows, own = at(i)
@@ -196,7 +201,7 @@
     return pltpu.with_memory_space_constraint(x, pltpu.VMEM)
 
 
-def gradient(place, own, far, rates, weights, gain, bias, total, lag, pairs=1, lags=(0, 1, 2, 3, 4, 5, 6)):
+def gradient(place, own, far, rates, weights, gain, bias, total, lag, pairs=1, lags=(0, 1, 2, 3, 5, 6, 7)):
     tokens = own[0].shape[0]
     heads, size = gain.shape
     members = len(weights)
@@ -219,7 +224,7 @@
                 pltpu.VMEM((2 * pairs * tokens, two), BF),
                 pltpu.VMEM((2 * pairs * tokens, 2 * size), BF),
                 pltpu.VMEM((2 * pairs * tokens, two), BF),
-                pltpu.VMEM((2 * tokens, heads), BF),
+                pltpu.VMEM((2 * tokens, -(-heads // 128) * 128), BF),
             ],
         ),
         compiler_params=pltpu.CompilerParams(vmem_limit_bytes=40 << 20),
@@ -237,7 +242,7 @@
         fill(whole_ref, [weight_ref.at[rel] for rel in range(members)], place_ref[2], rows_own)
 
     mean = head_mean(size, 4)
-    zof = place_ref[0] ^ (step * pairs // per + lag)
+    zof = place_ref[0] ^ (lag[0] + lag[1] * (step * pairs // per))
     first_pair = (zof * 2 + (place_ref[1] ^ flip)) * per + (step * pairs) % per
     const, state = [], {}
     for j in range(pairs):
@@ -276,7 +281,7 @@
     members, groups, rows_own, two = weights.shape
     _, size = gain.shape
     per = members * rows_own // (2 * size)
-    column = lambda i, place: (((place[0] ^ (i * pairs // per + lag)) * 2 + (place[1] ^ flip)) * per + i * pairs % per) // pairs
+    column = lambda i, place: (((place[0] ^ (lag[0] + lag[1] * (i * pairs // per))) * 2 + (place[1] ^ flip)) * per + i * pairs % per) // pairs
     col = pl.BlockSpec((tokens, pairs * 2 * size), lambda i, place: (0, column(i, place)))
     more = [] if before is None else [before]
     return pl.pallas_call(
@@ -296,29 +301,36 @@
 
 
 def pick_kernel(groups, flip, place_ref, *refs):
-    half = len(refs) // 2
-    wide = refs[-1].shape[1] // groups
-    for source, target in zip(refs[:half], refs[half:]):
+    half = (len(refs) - 1) // 2
+    sems = refs[-1]
+    wide = refs[half].shape[1] // groups
+    copies = []
+    for k in range(half):
         for g in range(groups):
             start = pl.multiple_of((2 * g + (place_ref[1] ^ flip)) * wide, wide)
-            target[:, g * wide : (g + 1) * wide] = source[:, pl.ds(start, wide)]
+            target = refs[half + k].at[:, g * wide : (g + 1) * wide]
+            copies.append(pltpu.make_async_copy(refs[k].at[:, pl.ds(start, wide)], target, sems.at[k, g]))
+    for copy in copies:
+        copy.start()
+    for copy in copies:
+        copy.wait()
 
 
 def pick(place, arrays, groups, flip):
     tokens, model = arrays[0].shape
-    held = pl.BlockSpec(memory_space=pltpu.VMEM)
     return pl.pallas_call(
         functools.partial(pick_kernel, groups, flip),
         out_shape=[pltpu.VMEM((tokens, model // 2), a.dtype) for a in arrays],
         grid_spec=pltpu.PrefetchScalarGridSpec(
             num_scalar_prefetch=1,
             grid=(1,),
-            in_specs=[held] * len(arrays),
-            out_specs=[held] * len(arrays),
+            in_specs=[pl.BlockSpec(memory_space=pltpu.HBM)] * len(arrays),
+            out_specs=[pl.BlockSpec(memory_space=pltpu.VMEM)] * len(arrays),
+            scratch_shapes=[pltpu.SemaphoreType.DMA((len(arrays), groups))],
         ),
         compiler_params=pltpu.CompilerParams(vmem_limit_bytes=32 << 20),
         name="pick",
-    )(place, *map(vmem, arrays))
+    )(place, *[pltpu.with_memory_space_constraint(x, pltpu.HBM) for x in arrays])
 
 
 def core_swap(x):
@@ -337,13 +349,13 @@
 
 
 def fetch(fast, groups, members, chunks):
-    narrow = fast.astype(BF)
+    narrow = lax.optimization_barrier(fast.astype(BF))
     held = [narrow]
     for s in range(1, groups):
         held.append(z_shift(narrow, s))
     weights = []
-    for at, count in chunks:
-        mine = jnp.stack(held[at : at + count])
+    for at, stride in chunks:
+        mine = jnp.stack([held[at + stride * g] for g in range(groups // 2)])
         weights.append([mine])
         for s in range(1, members):
             weights[-1].append(plane_shift(mine, s))
@@ -352,12 +364,12 @@
 
 def collect(parts, groups, members, chunks):
     sums = {}
-    for part, (at, count) in zip(parts, chunks):
+    for part, (at, stride) in zip(parts, chunks):
         arrived = [part[0]]
         for s in range(1, members):
             arrived.append(plane_shift(part[s], s))
-        for g in range(count):
-            sums[at + g] = sum([a[g].astype(F32) for a in arrived])
+        for g in range(groups // 2):
+            sums[at + stride * g] = sum([a[g].astype(F32) for a in arrived])
     total = sums[0]
     for s in range(1, groups):
         total = total + z_shift(sums[s].astype(BF), s).astype(F32)
@@ -372,9 +384,8 @@
     total = key_rows.shape[0] * 2 * groups * members
     gx = lax.axis_index("gx")
     place = jnp.stack([gx // 2, gx % 2, lax.axis_index("gy")]).astype(jnp.int32)
-    half = groups // 2
-    near, remote = (0, half), (half, groups - half)
-    orders = [(near, remote)] * (STEPS + 1)
+    evens, odds = (0, 2), (1, 2)
+    orders = [(evens, odds)] * STEPS + [((0, 1), (groups // 2, 1))]
     pairs = members * fast_weights.shape[0] // (2 * size)
     pairs = pairs if pairs <= 3 else 1
     fast, moment = (fast_weights, momentum)
@@ -386,7 +397,7 @@
     rates = (token_rates.T, core_swap(token_rates).T)
     for step in range(STEPS):
         parts = []
-        for k, (w, (at, count)) in enumerate(zip(weights, orders[step])):
+        for k, (w, at) in enumerate(zip(weights, orders[step])):
             turn = place if k == 0 else lax.optimization_barrier((place, parts[-1][0]))[0]
             parts.append(gradient(turn, own, far, rates, w, norm_gain, norm_bias, total, at, pairs))
         grad = collect(parts, groups, members, orders[step])
@@ -395,13 +406,13 @@
         weights = fetch(fast, groups, members, orders[step + 1])
     chunk = min(512, query_rows.shape[0])
     mixed, twins = None, []
-    for w, (at, count) in zip(weights, orders[STEPS]):
+    for w, at in zip(weights, orders[STEPS]):
         if mixed is not None:
             *w, mixed = lax.optimization_barrier((*w, mixed))
         whole = jnp.stack(w)
         twins.append(core_swap(whole))
         mixed = output(place, query_rows, whole, norm_gain, norm_bias, mixed, at, 0, pairs, chunk)
-    for w, (at, count) in zip(twins, orders[STEPS]):
+    for w, at in zip(twins, orders[STEPS]):
         mixed = output(place, query_rows, w, norm_gain, norm_bias, mixed, at, 1, pairs, chunk)
     return (mixed, fast, moment)
 

time: 175 us -> 174 us (level)
  starting transfers between devices: 62.6 us -> 66.7 us
  local copies, waits for them, and re-layouts: 3.82 us -> 0.04 us
    ppermute x15, starting transfers between devices: 23 us -> 29.5 us  [z_shift(): return lax.ppermute(x, 'gx', [(i, i ^ 2 * s) for i in range(n)])]
    unnamed x20 -> x16, local copies, waits for them, and re-layouts: 3.82 us -> 0.04 us
    ppermute x30, starting transfers between devices: 38.5 us -> 35.9 us  [plane_shift(): return lax.ppermute(x, 'gy', [(i, i ^ s) for i in range(n)])]
    pallas_call x1, Pallas kernels: 0.83 us -> 2.76 us  [pick(): pl.pallas_call(functools.partial(pick_kernel, groups, flip), out_shape=[p...]
  transfers between devices with their start and end apart: 50 -> 50, of which waited for: 19 -> 17; matrix products, arithmetic and copies ran while one was open for 2% -> 1% of each run, Pallas kernels for 26% -> 26%
where the time goes in v6:
time: 174 us
  starting transfers between devices  66.7 us (38%)
  Pallas kernels  62.1 us (36%)
  waiting for transfers between devices  41.7 us (24%)
  other arithmetic  2.67 us (2%)
    pallas_call x4, Pallas kernels, gradient(): pl.pallas_call(functools.partial(grad_kernel, size, lags, pairs, per, lag...  41.6 us
    ppermute x30, starting transfers between devices, plane_shift(): return lax.ppermute(x, 'gy', [(i, i ^ s) for i in range(n)])  35.9 us
    ppermute x15, starting transfers between devices, z_shift(): return lax.ppermute(x, 'gx', [(i, i ^ 2 * s) for i in range(n)])  29.5 us
    ppermute x30, waiting for transfers between devices, plane_shift(): return lax.ppermute(x, 'gy', [(i, i ^ s) for i in range(n)])  22.8 us
    ppermute x15, waiting for transfers between devices, z_shift(): return lax.ppermute(x, 'gx', [(i, i ^ 2 * s) for i in range(n)])  18.9 us
    pallas_call x4, Pallas kernels, output(): pl.pallas_call(functools.partial(output_kernel, size, chunk, lags, pairs,...  17.7 us
  transfers between devices with their start and end apart: 50, of which 17 were waited for; matrix products, arithmetic and copies ran while one was open for 1% of the time, Pallas kernels for 26%

profile of v6, /device:TPU:0, one launch (start us, length us, event | category | flops | bytes accessed | tf_op | source)
XLA Modules:
  0.0 174.1 jit_solution(12911860857388151242)
XLA Ops:
  0.8 2.8 %pick.1 = (bf16[512,1536]{1,0:T(8,128)(2,1)S(1)}, bf16[512,1536]{1,0:T(8,128)(2,1)S(1)}) custom-call(s32[3]{0:T(128)S(1)} %pad_add_fusion.place_ref, bf16[512,3072]{1,0:T(8,128)(2,1)} %refs_0_.9, bf16[512,3072]{1,0:T(8,128)(2,1)} %refs_1_.9), custom_call_target="tpu_custom_call" | custom-call | tf_op jit(solution)/shard_map/pick/pallas_call | solution.py:321
  5.1 4.1 %collective-permute-start.3 = (bf16[96,512]{1,0:T(8,128)(2,1)S(1)}, bf16[96,512]{1,0:T(8,128)(2,1)S(1)}, u32[]{:S(2)}, u32[]{:S(2)}) collective-permute-start(bf16[96,512]{1,0:T(8,128)(2,1)S(1)} %convert_element_type.161), channel_id=1, source_target_pairs={{0,16},{4,20},{8,24},{12,28},{16,0},{20,4},{24,8},{28,12},{1,17},{... | collective-permute-start | bytes 294920 | tf_op jit(solution)/shard_map/ppermute | solution.py:343
  10.8 6.3 %collective-permute-done.3 = bf16[96,512]{1,0:T(8,128)(2,1)S(1)} collective-permute-done((bf16[96,512]{1,0:T(8,128)(2,1)S(1)}, bf16[96,512]{1,0:T(8,128)(2,1)S(1)}, u32[]{:S(2)}, u32[]{:S(2)}) %collective-permute-start.3) | collective-permute-done | bytes 98336 | tf_op jit(solution)/shard_map/ppermute | solution.py:343
  17.1 2.8 %collective-permute-start.6 = (bf16[2,96,512]{2,1,0:T(8,128)(2,1)S(1)}, bf16[2,96,512]{2,1,0:T(8,128)(2,1)S(1)}, u32[]{:S(2)}, u32[]{:S(2)}) collective-permute-start(bf16[2,96,512]{2,1,0:T(8,128)(2,1)S(1)} %pad_maximum_fusion.2.refs_6_), channel_id=1, source_target_pairs={{0,3},{1,2},{2,1},{3,0},{4,7},{5,6},{6,5},{7,4},{8,11},{9,10},{10,... | collective-permute-start | bytes 589832 | tf_op jit(solution)/shard_map/ppermute | solution.py:348
  20.9 5.0 %collective-permute-done.6.refs_9_ = bf16[2,96,512]{2,1,0:T(8,128)(2,1)S(1)} collective-permute-done((bf16[2,96,512]{2,1,0:T(8,128)(2,1)S(1)}, bf16[2,96,512]{2,1,0:T(8,128)(2,1)S(1)}, u32[]{:S(2)}, u32[]{:S(2)}) %collective-permute-start.6) | collective-permute-done | bytes 196640 | tf_op jit(solution)/shard_map/ppermute | solution.py:348
  25.9 2.8 %collective-permute-start.14 = (bf16[2,96,512]{2,1,0:T(8,128)(2,1)S(1)}, bf16[2,96,512]{2,1,0:T(8,128)(2,1)S(1)}, u32[]{:S(2)}, u32[]{:S(2)}) collective-permute-start(bf16[2,96,512]{2,1,0:T(8,128)(2,1)S(1)} %pad_maximum_fusion.3.refs_6_), channel_id=1, source_target_pairs={{0,3},{1,2},{2,1},{3,0},{4,7},{5,6},{6,5},{7,4},{8,11},{9,10},{10,... | collective-permute-start | bytes 589832 | tf_op jit(solution)/shard_map/ppermute | solution.py:348
  32.2 10.4 %fast_gradient.4 = (bf16[2,96,512]{2,1,0:T(8,128)(2,1)S(1)}, bf16[2,96,512]{2,1,0:T(8,128)(2,1)S(1)}, bf16[2,96,512]{2,1,0:T(8,128)(2,1)S(1)}, bf16[2,96,512]{2,1,0:T(8,128)(2,1)S(1)}) custom-call(s32[3]{0:T(128)S(1)} %pad_add_fusion.place_ref, bf16[512,3072]{1,0:T(8,128)(2,1)S(1)} %copy-done, bf16[512,3072]{1,0:T(8,128)(2,1)S(1)} %copy-done.1, ...), custom_call_target="tpu_custom_call" | custom-call | tf_op jit(solution)/shard_map/fast_gradient/pallas_call | solution.py:212
  42.6 10.4 %fast_gradient.5 = (bf16[2,96,512]{2,1,0:T(8,128)(2,1)S(1)}, bf16[2,96,512]{2,1,0:T(8,128)(2,1)S(1)}, bf16[2,96,512]{2,1,0:T(8,128)(2,1)S(1)}, bf16[2,96,512]{2,1,0:T(8,128)(2,1)S(1)}) custom-call(s32[3]{0:T(128)S(1)} %pad_add_fusion.place_ref, bf16[512,3072]{1,0:T(8,128)(2,1)S(1)} %copy-done, bf16[512,3072]{1,0:T(8,128)(2,1)S(1)} %copy-done.1, ...), custom_call_target="tpu_custom_call" | custom-call | tf_op jit(solution)/shard_map/fast_gradient/pallas_call | solution.py:212
  62.2 4.5 %collective-permute-done.16 = bf16[2,96,512]{2,1,0:T(8,128)(2,1)S(1)} collective-permute-done((bf16[2,96,512]{2,1,0:T(8,128)(2,1)S(1)}, bf16[2,96,512]{2,1,0:T(8,128)(2,1)S(1)}, u32[]{:S(2)}, u32[]{:S(2)}) %collective-permute-start.16) | collective-permute-done | bytes 196640 | tf_op jit(solution)/shard_map/ppermute | solution.py:348
  68.6 3.4 %collective-permute-start.20 = (bf16[96,512]{1,0:T(8,128)(2,1)S(1)}, bf16[96,512]{1,0:T(8,128)(2,1)S(1)}, u32[]{:S(2)}, u32[]{:S(2)}) collective-permute-start(bf16[96,512]{1,0:T(8,128)(2,1)S(1)} %get-tuple-element.61), channel_id=1, source_target_pairs={{0,24},{4,28},{8,16},{12,20},{16,8},{20,12},{24,0},{28,4},{1,25},{... | collective-permute-start | bytes 294920 | tf_op jit(solution)/shard_map/ppermute | solution.py:343
  73.5 3.7 %collective-permute-start.19 = (bf16[96,512]{1,0:T(8,128)(2,1)S(1)}, bf16[96,512]{1,0:T(8,128)(2,1)S(1)}, u32[]{:S(2)}, u32[]{:S(2)}) collective-permute-start(bf16[96,512]{1,0:T(8,128)(2,1)S(1)} %fusion.7), channel_id=1, source_target_pairs={{0,16},{4,20},{8,24},{12,28},{16,0},{20,4},{24,8},{28,12},{1,17},{... | collective-permute-start | bytes 294920 | tf_op jit(solution)/shard_map/ppermute | solution.py:343
  77.2 3.6 %collective-permute-done.19 = bf16[96,512]{1,0:T(8,128)(2,1)S(1)} collective-permute-done((bf16[96,512]{1,0:T(8,128)(2,1)S(1)}, bf16[96,512]{1,0:T(8,128)(2,1)S(1)}, u32[]{:S(2)}, u32[]{:S(2)}) %collective-permute-start.19) | collective-permute-done | bytes 98336 | tf_op jit(solution)/shard_map/ppermute | solution.py:343
  84.5 2.9 %collective-permute-done.21 = bf16[96,512]{1,0:T(8,128)(2,1)S(1)} collective-permute-done((bf16[96,512]{1,0:T(8,128)(2,1)S(1)}, bf16[96,512]{1,0:T(8,128)(2,1)S(1)}, u32[]{:S(2)}, u32[]{:S(2)}) %collective-permute-start.21) | collective-permute-done | bytes 98336 | tf_op jit(solution)/shard_map/ppermute | solution.py:343
  93.1 3.1 %collective-permute-done.24.refs_9_ = bf16[2,96,512]{2,1,0:T(8,128)(2,1)S(1)} collective-permute-done((bf16[2,96,512]{2,1,0:T(8,128)(2,1)S(1)}, bf16[2,96,512]{2,1,0:T(8,128)(2,1)S(1)}, u32[]{:S(2)}, u32[]{:S(2)}) %collective-permute-start.24) | collective-permute-done | bytes 196640 | tf_op jit(solution)/shard_map/ppermute | solution.py:348
  99.3 10.5 %fast_gradient.6 = (bf16[2,96,512]{2,1,0:T(8,128)(2,1)S(1)}, bf16[2,96,512]{2,1,0:T(8,128)(2,1)S(1)}, bf16[2,96,512]{2,1,0:T(8,128)(2,1)S(1)}, bf16[2,96,512]{2,1,0:T(8,128)(2,1)S(1)}) custom-call(s32[3]{0:T(128)S(1)} %pad_add_fusion.place_ref, bf16[512,3072]{1,0:T(8,128)(2,1)S(1)} %copy-done, bf16[512,3072]{1,0:T(8,128)(2,1)S(1)} %copy-done.1, ...), custom_call_target="tpu_custom_call" | custom-call | tf_op jit(solution)/shard_map/fast_gradient/pallas_call | solution.py:212
  113.4 10.4 %fast_gradient.7 = (bf16[2,96,512]{2,1,0:T(8,128)(2,1)S(1)}, bf16[2,96,512]{2,1,0:T(8,128)(2,1)S(1)}, bf16[2,96,512]{2,1,0:T(8,128)(2,1)S(1)}, bf16[2,96,512]{2,1,0:T(8,128)(2,1)S(1)}) custom-call(s32[3]{0:T(128)S(1)} %pad_add_fusion.place_ref, bf16[512,3072]{1,0:T(8,128)(2,1)S(1)} %copy-done, bf16[512,3072]{1,0:T(8,128)(2,1)S(1)} %copy-done.1, ...), custom_call_target="tpu_custom_call" | custom-call | tf_op jit(solution)/shard_map/fast_gradient/pallas_call | solution.py:212
  127.5 3.0 %collective-permute-start.37 = (bf16[96,512]{1,0:T(8,128)(2,1)S(1)}, bf16[96,512]{1,0:T(8,128)(2,1)S(1)}, u32[]{:S(2)}, u32[]{:S(2)}) collective-permute-start(bf16[96,512]{1,0:T(8,128)(2,1)S(1)} %fusion.10), channel_id=1, source_target_pairs={{0,16},{4,20},{8,24},{12,28},{16,0},{20,4},{24,8},{28,12},{1,17},{... | collective-permute-start | bytes 294920 | tf_op jit(solution)/shard_map/ppermute | solution.py:343
  133.6 3.4 %collective-permute-start.38 = (bf16[96,512]{1,0:T(8,128)(2,1)S(1)}, bf16[96,512]{1,0:T(8,128)(2,1)S(1)}, u32[]{:S(2)}, u32[]{:S(2)}) collective-permute-start(bf16[96,512]{1,0:T(8,128)(2,1)S(1)} %get-tuple-element.59), channel_id=1, source_target_pairs={{0,24},{4,28},{8,16},{12,20},{16,8},{20,12},{24,0},{28,4},{1,25},{... | collective-permute-start | bytes 294920 | tf_op jit(solution)/shard_map/ppermute | solution.py:343
  138.0 2.7 %collective-permute-done.38 = bf16[96,512]{1,0:T(8,128)(2,1)S(1)} collective-permute-done((bf16[96,512]{1,0:T(8,128)(2,1)S(1)}, bf16[96,512]{1,0:T(8,128)(2,1)S(1)}, u32[]{:S(2)}, u32[]{:S(2)}) %collective-permute-start.38) | collective-permute-done | bytes 98336 | tf_op jit(solution)/shard_map/ppermute | solution.py:343
  142.5 3.2 %collective-permute-start.40 = (bf16[96,512]{1,0:T(8,128)(2,1)S(1)}, bf16[96,512]{1,0:T(8,128)(2,1)S(1)}, u32[]{:S(2)}, u32[]{:S(2)}) collective-permute-start(bf16[96,512]{1,0:T(8,128)(2,1)S(1)} %get-tuple-element.53), channel_id=1, source_target_pairs={{0,24},{4,28},{8,16},{12,20},{16,8},{20,12},{24,0},{28,4},{1,25},{... | collective-permute-start | bytes 294920 | tf_op jit(solution)/shard_map/ppermute | solution.py:343
  155.7 4.6 %fast_output.4.refs_0_ = bf16[512,3072]{1,0:T(8,128)(2,1)} custom-call(s32[3]{0:T(128)S(1)} %pad_add_fusion.place_ref, bf16[512,3072]{1,0:T(8,128)(2,1)S(1)} %copy-done.2, bf16[4,2,96,512]{3,2,1,0:T(8,128)(2,1)S(1)} %pad_maximum_fusion.weight_ref, f32[48,64]{1,0:T(8,128)S(1)} %copy-done.4, f32[48,64]{1,0:T(8,128)S(1)} %copy-done.5), custom_call_target="tpu_custom_call" | custom-call | tf_op jit(solution)/shard_map/fast_output/pallas_call | solution.py:287
  161.0 4.4 %fast_output.5.refs_0_ = bf16[512,3072]{1,0:T(8,128)(2,1)} custom-call(s32[3]{0:T(128)S(1)} %pad_add_fusion.place_ref, bf16[512,3072]{1,0:T(8,128)(2,1)S(1)} %copy-done.2, bf16[4,2,96,512]{3,2,1,0:T(8,128)(2,1)S(1)} %pad_maximum_fusion.1.weight_ref, f32[48,64]{1,0:T(8,128)S(1)} %copy-done.4, f32[48,64]{1,0:T(8,128)S(1)} %copy-done.5, ...), custom_call_target="tpu_custom_call", output_to_operand_aliasing={{}: (5, {})} | custom-call | tf_op jit(solution)/shard_map/fast_output/pallas_call | solution.py:287
  165.4 4.4 %fast_output.6.refs_0_ = bf16[512,3072]{1,0:T(8,128)(2,1)} custom-call(s32[3]{0:T(128)S(1)} %pad_add_fusion.place_ref, bf16[512,3072]{1,0:T(8,128)(2,1)S(1)} %copy-done.2, bf16[4,2,96,512]{3,2,1,0:T(8,128)(2,1)S(1)} %collective-permute-done.49.weight_ref, f32[48,64]{1,0:T(8,128)S(1)} %copy-done.4, ...), custom_call_target="tpu_custom_call", output_to_operand_aliasing={{}: (5, {})} | custom-call | tf_op jit(solution)/shard_map/fast_output/pallas_call | solution.py:287
  169.8 4.4 %fast_output.7 = bf16[512,3072]{1,0:T(8,128)(2,1)} custom-call(s32[3]{0:T(128)S(1)} %pad_add_fusion.place_ref, bf16[512,3072]{1,0:T(8,128)(2,1)S(1)} %copy-done.2, bf16[4,2,96,512]{3,2,1,0:T(8,128)(2,1)S(1)} %collective-permute-done.48.weight_ref, f32[48,64]{1,0:T(8,128)S(1)} %copy-done.4, f32[48,64]{1,0:T(8,128)S(1)} %copy-done.5, ...), custom_call_target="tpu_custom_call", output_to_operand_aliasing={{}: (5, {})} | custom-call | tf_op jit(solution)/shard_map/fast_output/pallas_call | solution.py:287
  (117 shorter events, 56.5 us)
Async XLA Ops:
  3.5 28.6 %collective-permute-start = (bf16[512,1536]{1,0:T(8,128)(2,1)S(1)}, bf16[512,1536]{1,0:T(8,128)(2,1)S(1)}, u32[]{:S(2)}, u32[]{:S(2)}) collective-permute-start(bf16[512,1536]{1,0:T(8,128)(2,1)S(1)} %get-tuple-element.28), channel_id=1, source_target_pairs={{0,4},{4,0},{8,12},{12,8},{16,20},{20,16},{24,28},{28,24},{1,5},{5... | collective-permute-start | bytes 4718600 | tf_op jit(solution)/shard_map/ppermute | solution.py:338
  4.1 28.1 %collective-permute-start.1 = (bf16[512,1536]{1,0:T(8,128)(2,1)S(1)}, bf16[512,1536]{1,0:T(8,128)(2,1)S(1)}, u32[]{:S(2)}, u32[]{:S(2)}) collective-permute-start(bf16[512,1536]{1,0:T(8,128)(2,1)S(1)} %get-tuple-element.29), channel_id=1, source_target_pairs={{0,4},{4,0},{8,12},{12,8},{16,20},{20,16},{24,28},{28,24},{1,5},{5... | collective-permute-start | bytes 4718600 | tf_op jit(solution)/shard_map/ppermute | solution.py:338
  5.1 12.0 %collective-permute-start.3 = (bf16[96,512]{1,0:T(8,128)(2,1)S(1)}, bf16[96,512]{1,0:T(8,128)(2,1)S(1)}, u32[]{:S(2)}, u32[]{:S(2)}) collective-permute-start(bf16[96,512]{1,0:T(8,128)(2,1)S(1)} %convert_element_type.161), channel_id=1, source_target_pairs={{0,16},{4,20},{8,24},{12,28},{16,0},{20,4},{24,8},{28,12},{1,17},{... | collective-permute-start | bytes 294920 | tf_op jit(solution)/shard_map/ppermute | solution.py:343
  20.0 10.1 %collective-permute-start.5 = (bf16[2,96,512]{2,1,0:T(8,128)(2,1)S(1)}, bf16[2,96,512]{2,1,0:T(8,128)(2,1)S(1)}, u32[]{:S(2)}, u32[]{:S(2)}) collective-permute-start(bf16[2,96,512]{2,1,0:T(8,128)(2,1)S(1)} %pad_maximum_fusion.2.refs_6_), channel_id=1, source_target_pairs={{0,2},{1,3},{2,0},{3,1},{4,6},{5,7},{6,4},{7,5},{8,10},{9,11},{10,... | collective-permute-start | bytes 589832 | tf_op jit(solution)/shard_map/ppermute | solution.py:348
  20.5 11.4 %collective-permute-start.4 = (bf16[2,96,512]{2,1,0:T(8,128)(2,1)S(1)}, bf16[2,96,512]{2,1,0:T(8,128)(2,1)S(1)}, u32[]{:S(2)}, u32[]{:S(2)}) collective-permute-start(bf16[2,96,512]{2,1,0:T(8,128)(2,1)S(1)} %pad_maximum_fusion.2.refs_6_), channel_id=1, source_target_pairs={{0,1},{1,0},{2,3},{3,2},{4,5},{5,4},{6,7},{7,6},{8,9},{9,8},{10,11... | collective-permute-start | bytes 589832 | tf_op jit(solution)/shard_map/ppermute | solution.py:348
  25.9 16.7 %collective-permute-start.14 = (bf16[2,96,512]{2,1,0:T(8,128)(2,1)S(1)}, bf16[2,96,512]{2,1,0:T(8,128)(2,1)S(1)}, u32[]{:S(2)}, u32[]{:S(2)}) collective-permute-start(bf16[2,96,512]{2,1,0:T(8,128)(2,1)S(1)} %pad_maximum_fusion.3.refs_6_), channel_id=1, source_target_pairs={{0,3},{1,2},{2,1},{3,0},{4,7},{5,6},{6,5},{7,4},{8,11},{9,10},{10,... | collective-permute-start | bytes 589832 | tf_op jit(solution)/shard_map/ppermute | solution.py:348
  30.0 12.6 %collective-permute-start.13 = (bf16[2,96,512]{2,1,0:T(8,128)(2,1)S(1)}, bf16[2,96,512]{2,1,0:T(8,128)(2,1)S(1)}, u32[]{:S(2)}, u32[]{:S(2)}) collective-permute-start(bf16[2,96,512]{2,1,0:T(8,128)(2,1)S(1)} %pad_maximum_fusion.3.refs_6_), channel_id=1, source_target_pairs={{0,2},{1,3},{2,0},{3,1},{4,6},{5,7},{6,4},{7,5},{8,10},{9,11},{10,... | collective-permute-start | bytes 589832 | tf_op jit(solution)/shard_map/ppermute | solution.py:348
  31.9 10.7 %collective-permute-start.12 = (bf16[2,96,512]{2,1,0:T(8,128)(2,1)S(1)}, bf16[2,96,512]{2,1,0:T(8,128)(2,1)S(1)}, u32[]{:S(2)}, u32[]{:S(2)}) collective-permute-start(bf16[2,96,512]{2,1,0:T(8,128)(2,1)S(1)} %pad_maximum_fusion.3.refs_6_), channel_id=1, source_target_pairs={{0,1},{1,0},{2,3},{3,2},{4,5},{5,4},{6,7},{7,6},{8,9},{9,8},{10,11... | collective-permute-start | bytes 589832 | tf_op jit(solution)/shard_map/ppermute | solution.py:348
  54.8 11.9 %collective-permute-start.16 = (bf16[2,96,512]{2,1,0:T(8,128)(2,1)S(1)}, bf16[2,96,512]{2,1,0:T(8,128)(2,1)S(1)}, u32[]{:S(2)}, u32[]{:S(2)}) collective-permute-start(bf16[2,96,512]{2,1,0:T(8,128)(2,1)S(1)} %get-tuple-element.37), channel_id=1, source_target_pairs={{0,2},{1,3},{2,0},{3,1},{4,6},{5,7},{6,4},{7,5},{8,10},{9,11},{10,... | collective-permute-start | bytes 589832 | tf_op jit(solution)/shard_map/ppermute | solution.py:348
  55.0 11.7 %collective-permute-start.17 = (bf16[2,96,512]{2,1,0:T(8,128)(2,1)S(1)}, bf16[2,96,512]{2,1,0:T(8,128)(2,1)S(1)}, u32[]{:S(2)}, u32[]{:S(2)}) collective-permute-start(bf16[2,96,512]{2,1,0:T(8,128)(2,1)S(1)} %get-tuple-element.38), channel_id=1, source_target_pairs={{0,3},{1,2},{2,1},{3,0},{4,7},{5,6},{6,5},{7,4},{8,11},{9,10},{10,... | collective-permute-start | bytes 589832 | tf_op jit(solution)/shard_map/ppermute | solution.py:348
  56.5 15.4 %collective-permute-start.7 = (bf16[2,96,512]{2,1,0:T(8,128)(2,1)S(1)}, bf16[2,96,512]{2,1,0:T(8,128)(2,1)S(1)}, u32[]{:S(2)}, u32[]{:S(2)}) collective-permute-start(bf16[2,96,512]{2,1,0:T(8,128)(2,1)S(1)} %get-tuple-element.31), channel_id=1, source_target_pairs={{0,1},{1,0},{2,3},{3,2},{4,5},{5,4},{6,7},{7,6},{8,9},{9,8},{10,11... | collective-permute-start | bytes 589832 | tf_op jit(solution)/shard_map/ppermute | solution.py:348
  58.3 15.1 %collective-permute-start.8 = (bf16[2,96,512]{2,1,0:T(8,128)(2,1)S(1)}, bf16[2,96,512]{2,1,0:T(8,128)(2,1)S(1)}, u32[]{:S(2)}, u32[]{:S(2)}) collective-permute-start(bf16[2,96,512]{2,1,0:T(8,128)(2,1)S(1)} %get-tuple-element.32), channel_id=1, source_target_pairs={{0,2},{1,3},{2,0},{3,1},{4,6},{5,7},{6,4},{7,5},{8,10},{9,11},{10,... | collective-permute-start | bytes 589832 | tf_op jit(solution)/shard_map/ppermute | solution.py:348
  60.8 12.6 %collective-permute-start.9 = (bf16[2,96,512]{2,1,0:T(8,128)(2,1)S(1)}, bf16[2,96,512]{2,1,0:T(8,128)(2,1)S(1)}, u32[]{:S(2)}, u32[]{:S(2)}) collective-permute-start(bf16[2,96,512]{2,1,0:T(8,128)(2,1)S(1)} %get-tuple-element.33), channel_id=1, source_target_pairs={{0,3},{1,2},{2,1},{3,0},{4,7},{5,6},{6,5},{7,4},{8,11},{9,10},{10,... | collective-permute-start | bytes 589832 | tf_op jit(solution)/shard_map/ppermute | solution.py:348
  66.8 10.4 %collective-permute-start.18 = (bf16[96,512]{1,0:T(8,128)(2,1)S(1)}, bf16[96,512]{1,0:T(8,128)(2,1)S(1)}, u32[]{:S(2)}, u32[]{:S(2)}) collective-permute-start(bf16[96,512]{1,0:T(8,128)(2,1)S(1)} %get-tuple-element.60), channel_id=1, source_target_pairs={{0,8},{4,12},{8,0},{12,4},{16,24},{20,28},{24,16},{28,20},{1,9},{5... | collective-permute-start | bytes 294920 | tf_op jit(solution)/shard_map/ppermute | solution.py:343
  89.0 10.3 %collective-permute-start.23 = (bf16[2,96,512]{2,1,0:T(8,128)(2,1)S(1)}, bf16[2,96,512]{2,1,0:T(8,128)(2,1)S(1)}, u32[]{:S(2)}, u32[]{:S(2)}) collective-permute-start(bf16[2,96,512]{2,1,0:T(8,128)(2,1)S(1)} %pad_maximum_fusion.4.refs_6_), channel_id=1, source_target_pairs={{0,2},{1,3},{2,0},{3,1},{4,6},{5,7},{6,4},{7,5},{8,10},{9,11},{10,... | collective-permute-start | bytes 589832 | tf_op jit(solution)/shard_map/ppermute | solution.py:348
  89.5 9.8 %collective-permute-start.22 = (bf16[2,96,512]{2,1,0:T(8,128)(2,1)S(1)}, bf16[2,96,512]{2,1,0:T(8,128)(2,1)S(1)}, u32[]{:S(2)}, u32[]{:S(2)}) collective-permute-start(bf16[2,96,512]{2,1,0:T(8,128)(2,1)S(1)} %pad_maximum_fusion.4.refs_6_), channel_id=1, source_target_pairs={{0,1},{1,0},{2,3},{3,2},{4,5},{5,4},{6,7},{7,6},{8,9},{9,8},{10,11... | collective-permute-start | bytes 589832 | tf_op jit(solution)/shard_map/ppermute | solution.py:348
  91.1 20.9 %collective-permute-start.32 = (bf16[2,96,512]{2,1,0:T(8,128)(2,1)S(1)}, bf16[2,96,512]{2,1,0:T(8,128)(2,1)S(1)}, u32[]{:S(2)}, u32[]{:S(2)}) collective-permute-start(bf16[2,96,512]{2,1,0:T(8,128)(2,1)S(1)} %pad_maximum_fusion.5.refs_6_), channel_id=1, source_target_pairs={{0,3},{1,2},{2,1},{3,0},{4,7},{5,6},{6,5},{7,4},{8,11},{9,10},{10,... | collective-permute-start | bytes 589832 | tf_op jit(solution)/shard_map/ppermute | solution.py:348
  92.6 20.8 %collective-permute-start.31 = (bf16[2,96,512]{2,1,0:T(8,128)(2,1)S(1)}, bf16[2,96,512]{2,1,0:T(8,128)(2,1)S(1)}, u32[]{:S(2)}, u32[]{:S(2)}) collective-permute-start(bf16[2,96,512]{2,1,0:T(8,128)(2,1)S(1)} %pad_maximum_fusion.5.refs_6_), channel_id=1, source_target_pairs={{0,2},{1,3},{2,0},{3,1},{4,6},{5,7},{6,4},{7,5},{8,10},{9,11},{10,... | collective-permute-start | bytes 589832 | tf_op jit(solution)/shard_map/ppermute | solution.py:348
  96.2 17.2 %collective-permute-start.30 = (bf16[2,96,512]{2,1,0:T(8,128)(2,1)S(1)}, bf16[2,96,512]{2,1,0:T(8,128)(2,1)S(1)}, u32[]{:S(2)}, u32[]{:S(2)}) collective-permute-start(bf16[2,96,512]{2,1,0:T(8,128)(2,1)S(1)} %pad_maximum_fusion.5.refs_6_), channel_id=1, source_target_pairs={{0,1},{1,0},{2,3},{3,2},{4,5},{5,4},{6,7},{7,6},{8,9},{9,8},{10,11... | collective-permute-start | bytes 589832 | tf_op jit(solution)/shard_map/ppermute | solution.py:348
  109.9 16.1 %collective-permute-start.25 = (bf16[2,96,512]{2,1,0:T(8,128)(2,1)S(1)}, bf16[2,96,512]{2,1,0:T(8,128)(2,1)S(1)}, u32[]{:S(2)}, u32[]{:S(2)}) collective-permute-start(bf16[2,96,512]{2,1,0:T(8,128)(2,1)S(1)} %get-tuple-element.40), channel_id=1, source_target_pairs={{0,1},{1,0},{2,3},{3,2},{4,5},{5,4},{6,7},{7,6},{8,9},{9,8},{10,11... | collective-permute-start | bytes 589832 | tf_op jit(solution)/shard_map/ppermute | solution.py:348
  110.6 16.8 %collective-permute-start.26 = (bf16[2,96,512]{2,1,0:T(8,128)(2,1)S(1)}, bf16[2,96,512]{2,1,0:T(8,128)(2,1)S(1)}, u32[]{:S(2)}, u32[]{:S(2)}) collective-permute-start(bf16[2,96,512]{2,1,0:T(8,128)(2,1)S(1)} %get-tuple-element.41), channel_id=1, source_target_pairs={{0,2},{1,3},{2,0},{3,1},{4,6},{5,7},{6,4},{7,5},{8,10},{9,11},{10,... | collective-permute-start | bytes 589832 | tf_op jit(solution)/shard_map/ppermute | solution.py:348
  112.0 15.4 %collective-permute-start.27 = (bf16[2,96,512]{2,1,0:T(8,128)(2,1)S(1)}, bf16[2,96,512]{2,1,0:T(8,128)(2,1)S(1)}, u32[]{:S(2)}, u32[]{:S(2)}) collective-permute-start(bf16[2,96,512]{2,1,0:T(8,128)(2,1)S(1)} %get-tuple-element.42), channel_id=1, source_target_pairs={{0,3},{1,2},{2,1},{3,0},{4,7},{5,6},{6,5},{7,4},{8,11},{9,10},{10,... | collective-permute-start | bytes 589832 | tf_op jit(solution)/shard_map/ppermute | solution.py:348
  127.5 9.5 %collective-permute-start.37 = (bf16[96,512]{1,0:T(8,128)(2,1)S(1)}, bf16[96,512]{1,0:T(8,128)(2,1)S(1)}, u32[]{:S(2)}, u32[]{:S(2)}) collective-permute-start(bf16[96,512]{1,0:T(8,128)(2,1)S(1)} %fusion.10), channel_id=1, source_target_pairs={{0,16},{4,20},{8,24},{12,28},{16,0},{20,4},{24,8},{28,12},{1,17},{... | collective-permute-start | bytes 294920 | tf_op jit(solution)/shard_map/ppermute | solution.py:343
  155.6 9.8 %collective-permute-start.49 = (bf16[4,2,96,512]{3,2,1,0:T(8,128)(2,1)S(1)}, bf16[4,2,96,512]{3,2,1,0:T(8,128)(2,1)S(1)}, u32[]{:S(2)}, u32[]{:S(2)}) collective-permute-start(bf16[4,2,96,512]{3,2,1,0:T(8,128)(2,1)S(1)} %pad_maximum_fusion.weight_ref), channel_id=1, source_target_pairs={{0,4},{4,0},{8,12},{12,8},{16,20},{20,16},{24,28},{28,24},{1,5},{5... | collective-permute-start | bytes 2359304 | tf_op jit(solution)/shard_map/ppermute | solution.py:338
  (34 other events, 438.8 us)

commit v7 on v6

--- a/solution.py
+++ b/solution.py
@@ -232,29 +232,30 @@
     )(place, *map(vmem, own), *map(vmem, far), *map(vmem, rates), *map(vmem, weights), vmem(gain), vmem(bias))
 
 
-def output_kernel(size, chunk, lags, pairs, per, lag, flip, place_ref, query_ref, weight_ref, gain_ref, bias_ref, *refs):
-    out_ref, whole_ref = refs[-2:]
-    step = pl.program_id(0)
-    members, _, rows_own, _ = weight_ref.shape
-
-    @pl.when(step == 0)
-    def _():
-        fill(whole_ref, [weight_ref.at[rel] for rel in range(members)], place_ref[2], rows_own)
-
+def output_kernel(size, chunk, lags, lag, flip, place_ref, query_ref, weight_ref, gain_ref, bias_ref, *refs):
+    out_ref, whole_ref, made_ref, sems = refs[-4:]
+    members, groups, rows_own, _ = weight_ref.shape
+    per = members * rows_own // (2 * size)
+    fill(whole_ref, [weight_ref.at[rel] for rel in range(members)], place_ref[2], rows_own)
     mean = head_mean(size, 4)
-    zof = place_ref[0] ^ (lag[0] + lag[1] * (step * pairs // per))
-    first_pair = (zof * 2 + (place_ref[1] ^ flip)) * per + (step * pairs) % per
-    const, state = [], {}
-    for j in range(pairs):
-        base = pl.multiple_of((step * pairs + j) * 2 * size, 2 * size)
-        const.append((blocks(whole_ref[pl.ds(base, 2 * size), :], size), pair_row(gain_ref, first_pair + j), pair_row(bias_ref, first_pair + j)))
+    const, state, copies = [], {}, []
+    for g in range(groups):
+        first_pair = ((place_ref[0] ^ (lag[0] + lag[1] * g)) * 2 + (place_ref[1] ^ flip)) * per
+        start = pl.multiple_of(first_pair * 2 * size, 2 * size)
+        inside = slice(g * per * 2 * size, (g + 1) * per * 2 * size)
+        copies.append(pltpu.make_async_copy(made_ref.at[:, inside], out_ref.at[:, pl.ds(start, per * 2 * size)], sems.at[g]))
+        for j in range(per):
+            base = (g * per + j) * 2 * size
+            mats = blocks(whole_ref[pl.ds(base, 2 * size), :], size)
+            column = pl.multiple_of((first_pair + j) * 2 * size, 2 * size)
+            const.append((mats, pair_row(gain_ref, first_pair + j), pair_row(bias_ref, first_pair + j), column, base))
     count = query_ref.shape[0] // chunk
 
     def at(i):
         j, k = divmod(i, count)
-        start = pl.multiple_of((first_pair + j) * 2 * size, 2 * size)
+        mats, gain, bias, column, base = const[j]
         rows = pl.ds(k * chunk, chunk)
-        return const[j], (rows, pl.ds(start, 2 * size)), (rows, slice(2 * size * j, 2 * size * (j + 1)))
+        return (mats, gain, bias), (rows, pl.ds(column, 2 * size)), (rows, slice(base, base + 2 * size))
 
     def enter(i):
         (mats, gain, bias), where, target = at(i)
@@ -271,28 +272,34 @@
     def leave(i):
         (mats, gain, bias), where, target = at(i)
         unit = state.pop((i, "centre")) * lax.rsqrt(state.pop((i, "spread")) + 1e-06)
-        out_ref[target] = (query_ref[where].astype(F32) + unit * gain + bias).astype(BF)
-
-    staggered((enter, bend, measure, leave), lags, pairs * count)
-
-
-def output(place, queries, weights, gain, bias, before, lag, flip, pairs=1, chunk=256, lags=(0, 1, 2, 3)):
+        made_ref[target] = (query_ref[where].astype(F32) + unit * gain + bias).astype(BF)
+        if (i + 1) % (per * count) == 0:
+            copies[i // (per * count)].start()
+
+    staggered((enter, bend, measure, leave), lags, groups * per * count)
+    for copy in copies:
+        copy.wait()
+
+
+def output(place, queries, weights, gain, bias, before, lag, flip, chunk=256, lags=(0, 1, 2, 3)):
     tokens, model = queries.shape
     members, groups, rows_own, two = weights.shape
-    _, size = gain.shape
-    per = members * rows_own // (2 * size)
-    column = lambda i, place: (((place[0] ^ (lag[0] + lag[1] * (i * pairs // per))) * 2 + (place[1] ^ flip)) * per + i * pairs % per) // pairs
-    col = pl.BlockSpec((tokens, pairs * 2 * size), lambda i, place: (0, column(i, place)))
+    size = gain.shape[1]
+    rows = groups * members * rows_own
     more = [] if before is None else [before]
     return pl.pallas_call(
-        functools.partial(output_kernel, size, chunk, lags, pairs, per, lag, flip),
+        functools.partial(output_kernel, size, chunk, lags, lag, flip),
         out_shape=jax.ShapeDtypeStruct((tokens, model), BF),
         grid_spec=pltpu.PrefetchScalarGridSpec(
             num_scalar_prefetch=1,
-            grid=(groups * per // pairs,),
+            grid=(1,),
             in_specs=[pl.BlockSpec(memory_space=pltpu.VMEM)] * 4 + [pl.BlockSpec(memory_space=pl.ANY)] * len(more),
-            out_specs=col,
-            scratch_shapes=[pltpu.VMEM((groups * members * rows_own, two), BF)],
+            out_specs=pl.BlockSpec(memory_space=pl.ANY),
+            scratch_shapes=[
+                pltpu.VMEM((rows, two), BF),
+                pltpu.VMEM((tokens, rows), BF),
+                pltpu.SemaphoreType.DMA((groups,)),
+            ],
         ),
         input_output_aliases={5: 0} if more else {},
         compiler_params=pltpu.CompilerParams(vmem_limit_bytes=40 << 20),
@@ -384,7 +391,7 @@
     total = key_rows.shape[0] * 2 * groups * members
     gx = lax.axis_index("gx")
     place = jnp.stack([gx // 2, gx % 2, lax.axis_index("gy")]).astype(jnp.int32)
-    evens, odds = (0, 2), (1, 2)
+    evens, odds = (0, 3), (1, 1)
     orders = [(evens, odds)] * STEPS + [((0, 1), (groups // 2, 1))]
     pairs = members * fast_weights.shape[0] // (2 * size)
     pairs = pairs if pairs <= 3 else 1
@@ -411,9 +418,9 @@
             *w, mixed = lax.optimization_barrier((*w, mixed))
         whole = jnp.stack(w)
         twins.append(core_swap(whole))
-        mixed = output(place, query_rows, whole, norm_gain, norm_bias, mixed, at, 0, pairs, chunk)
+        mixed = output(place, query_rows, whole, norm_gain, norm_bias, mixed, at, 0, chunk)
     for w, at in zip(twins, orders[STEPS]):
-        mixed = output(place, query_rows, w, norm_gain, norm_bias, mixed, at, 1, pairs, chunk)
+        mixed = output(place, query_rows, w, norm_gain, norm_bias, mixed, at, 1, chunk)
     return (mixed, fast, moment)
 
 

time: 174 us -> 173 us (level)
  waiting for transfers between devices: 41.7 us -> 48.3 us
  starting transfers between devices: 66.7 us -> 61.3 us
  Pallas kernels: 62.1 us -> 59.5 us
    ppermute x30, waiting for transfers between devices: 22.8 us -> 27.6 us  [plane_shift(): return lax.ppermute(x, 'gy', [(i, i ^ s) for i in range(n)])]
    ppermute x15, starting transfers between devices: 29.5 us -> 25 us  [z_shift(): return lax.ppermute(x, 'gx', [(i, i ^ 2 * s) for i in range(n)])]
    pallas_call x4, Pallas kernels: 17.7 us -> 15 us  [output(): pl.pallas_call(functools.partial(output_kernel, size, chunk, lags, lag, f...]
    ppermute x15, waiting for transfers between devices: 18.9 us -> 20.7 us  [z_shift(): return lax.ppermute(x, 'gx', [(i, i ^ 2 * s) for i in range(n)])]
  transfers between devices with their start and end apart: 50 -> 50, of which waited for: 17 -> 19; matrix products, arithmetic and copies ran while one was open for 1% -> 1% of each run, Pallas kernels for 26% -> 25%
where the time goes in v7:
time: 173 us
  starting transfers between devices  61.3 us (35%)
  Pallas kernels  59.5 us (34%)
  waiting for transfers between devices  48.3 us (28%)
  other arithmetic  2.67 us (2%)
    pallas_call x4, Pallas kernels, gradient(): pl.pallas_call(functools.partial(grad_kernel, size, lags, pairs, per, lag...  41.8 us
    ppermute x30, starting transfers between devices, plane_shift(): return lax.ppermute(x, 'gy', [(i, i ^ s) for i in range(n)])  35.3 us
    ppermute x30, waiting for transfers between devices, plane_shift(): return lax.ppermute(x, 'gy', [(i, i ^ s) for i in range(n)])  27.6 us
    ppermute x15, starting transfers between devices, z_shift(): return lax.ppermute(x, 'gx', [(i, i ^ 2 * s) for i in range(n)])  25 us
    ppermute x15, waiting for transfers between devices, z_shift(): return lax.ppermute(x, 'gx', [(i, i ^ 2 * s) for i in range(n)])  20.7 us
    pallas_call x4, Pallas kernels, output(): pl.pallas_call(functools.partial(output_kernel, size, chunk, lags, lag, f...  15 us
  transfers between devices with their start and end apart: 50, of which 19 were waited for; matrix products, arithmetic and copies ran while one was open for 1% of the time, Pallas kernels for 25%

profile of v7, /device:TPU:0, one launch (start us, length us, event | category | flops | bytes accessed | tf_op | source)
XLA Modules:
  0.0 173.0 jit_solution(13136676819185650756)
XLA Ops:
  0.8 2.8 %pick.1 = (bf16[512,1536]{1,0:T(8,128)(2,1)S(1)}, bf16[512,1536]{1,0:T(8,128)(2,1)S(1)}) custom-call(s32[3]{0:T(128)S(1)} %pad_add_fusion.place_ref, bf16[512,3072]{1,0:T(8,128)(2,1)} %refs_0_.9, bf16[512,3072]{1,0:T(8,128)(2,1)} %refs_1_.9), custom_call_target="tpu_custom_call" | custom-call | tf_op jit(solution)/shard_map/pick/pallas_call | solution.py:328
  5.1 5.1 %collective-permute-start.3 = (bf16[96,512]{1,0:T(8,128)(2,1)S(1)}, bf16[96,512]{1,0:T(8,128)(2,1)S(1)}, u32[]{:S(2)}, u32[]{:S(2)}) collective-permute-start(bf16[96,512]{1,0:T(8,128)(2,1)S(1)} %convert_element_type.161), channel_id=1, source_target_pairs={{0,24},{4,28},{8,16},{12,20},{16,8},{20,12},{24,0},{28,4},{1,25},{... | collective-permute-start | bytes 294920 | tf_op jit(solution)/shard_map/ppermute | solution.py:350
  10.8 3.1 %collective-permute-done.3 = bf16[96,512]{1,0:T(8,128)(2,1)S(1)} collective-permute-done((bf16[96,512]{1,0:T(8,128)(2,1)S(1)}, bf16[96,512]{1,0:T(8,128)(2,1)S(1)}, u32[]{:S(2)}, u32[]{:S(2)}) %collective-permute-start.3) | collective-permute-done | bytes 98336 | tf_op jit(solution)/shard_map/ppermute | solution.py:350
  14.0 4.7 %collective-permute-done.11 = bf16[96,512]{1,0:T(8,128)(2,1)S(1)} collective-permute-done((bf16[96,512]{1,0:T(8,128)(2,1)S(1)}, bf16[96,512]{1,0:T(8,128)(2,1)S(1)}, u32[]{:S(2)}, u32[]{:S(2)}) %collective-permute-start.11) | collective-permute-done | bytes 98336 | tf_op jit(solution)/shard_map/ppermute | solution.py:350
  22.2 5.2 %collective-permute-done.6.refs_9_ = bf16[2,96,512]{2,1,0:T(8,128)(2,1)S(1)} collective-permute-done((bf16[2,96,512]{2,1,0:T(8,128)(2,1)S(1)}, bf16[2,96,512]{2,1,0:T(8,128)(2,1)S(1)}, u32[]{:S(2)}, u32[]{:S(2)}) %collective-permute-start.6) | collective-permute-done | bytes 196640 | tf_op jit(solution)/shard_map/ppermute | solution.py:355
  33.2 10.4 %fast_gradient.4 = (bf16[2,96,512]{2,1,0:T(8,128)(2,1)S(1)}, bf16[2,96,512]{2,1,0:T(8,128)(2,1)S(1)}, bf16[2,96,512]{2,1,0:T(8,128)(2,1)S(1)}, bf16[2,96,512]{2,1,0:T(8,128)(2,1)S(1)}) custom-call(s32[3]{0:T(128)S(1)} %pad_add_fusion.place_ref, bf16[512,3072]{1,0:T(8,128)(2,1)S(1)} %copy-done, bf16[512,3072]{1,0:T(8,128)(2,1)S(1)} %copy-done.1, ...), custom_call_target="tpu_custom_call" | custom-call | tf_op jit(solution)/shard_map/fast_gradient/pallas_call | solution.py:212
  43.6 10.4 %fast_gradient.5 = (bf16[2,96,512]{2,1,0:T(8,128)(2,1)S(1)}, bf16[2,96,512]{2,1,0:T(8,128)(2,1)S(1)}, bf16[2,96,512]{2,1,0:T(8,128)(2,1)S(1)}, bf16[2,96,512]{2,1,0:T(8,128)(2,1)S(1)}) custom-call(s32[3]{0:T(128)S(1)} %pad_add_fusion.place_ref, bf16[512,3072]{1,0:T(8,128)(2,1)S(1)} %copy-done, bf16[512,3072]{1,0:T(8,128)(2,1)S(1)} %copy-done.1, ...), custom_call_target="tpu_custom_call" | custom-call | tf_op jit(solution)/shard_map/fast_gradient/pallas_call | solution.py:212
  63.5 4.4 %collective-permute-done.16 = bf16[2,96,512]{2,1,0:T(8,128)(2,1)S(1)} collective-permute-done((bf16[2,96,512]{2,1,0:T(8,128)(2,1)S(1)}, bf16[2,96,512]{2,1,0:T(8,128)(2,1)S(1)}, u32[]{:S(2)}, u32[]{:S(2)}) %collective-permute-start.16) | collective-permute-done | bytes 196640 | tf_op jit(solution)/shard_map/ppermute | solution.py:355
  68.0 3.0 %collective-permute-start.19 = (bf16[96,512]{1,0:T(8,128)(2,1)S(1)}, bf16[96,512]{1,0:T(8,128)(2,1)S(1)}, u32[]{:S(2)}, u32[]{:S(2)}) collective-permute-start(bf16[96,512]{1,0:T(8,128)(2,1)S(1)} %get-tuple-element.61), channel_id=1, source_target_pairs={{0,16},{4,20},{8,24},{12,28},{16,0},{20,4},{24,8},{28,12},{1,17},{... | collective-permute-start | bytes 294920 | tf_op jit(solution)/shard_map/ppermute | solution.py:350
  71.0 3.5 %collective-permute-done.8 = bf16[2,96,512]{2,1,0:T(8,128)(2,1)S(1)} collective-permute-done((bf16[2,96,512]{2,1,0:T(8,128)(2,1)S(1)}, bf16[2,96,512]{2,1,0:T(8,128)(2,1)S(1)}, u32[]{:S(2)}, u32[]{:S(2)}) %collective-permute-start.8) | collective-permute-done | bytes 196640 | tf_op jit(solution)/shard_map/ppermute | solution.py:355
  74.6 2.5 %collective-permute-start.20 = (bf16[96,512]{1,0:T(8,128)(2,1)S(1)}, bf16[96,512]{1,0:T(8,128)(2,1)S(1)}, u32[]{:S(2)}, u32[]{:S(2)}) collective-permute-start(bf16[96,512]{1,0:T(8,128)(2,1)S(1)} %fusion.8), channel_id=1, source_target_pairs={{0,24},{4,28},{8,16},{12,20},{16,8},{20,12},{24,0},{28,4},{1,25},{... | collective-permute-start | bytes 294920 | tf_op jit(solution)/shard_map/ppermute | solution.py:350
  77.1 4.0 %collective-permute-done.20 = bf16[96,512]{1,0:T(8,128)(2,1)S(1)} collective-permute-done((bf16[96,512]{1,0:T(8,128)(2,1)S(1)}, bf16[96,512]{1,0:T(8,128)(2,1)S(1)}, u32[]{:S(2)}, u32[]{:S(2)}) %collective-permute-start.20) | collective-permute-done | bytes 98336 | tf_op jit(solution)/shard_map/ppermute | solution.py:350
  81.3 2.6 %collective-permute-start.21 = (bf16[96,512]{1,0:T(8,128)(2,1)S(1)}, bf16[96,512]{1,0:T(8,128)(2,1)S(1)}, u32[]{:S(2)}, u32[]{:S(2)}) collective-permute-start(bf16[96,512]{1,0:T(8,128)(2,1)S(1)} %get-tuple-element.56), channel_id=1, source_target_pairs={{0,24},{4,28},{8,16},{12,20},{16,8},{20,12},{24,0},{28,4},{1,25},{... | collective-permute-start | bytes 294920 | tf_op jit(solution)/shard_map/ppermute | solution.py:350
  93.4 3.3 %collective-permute-done.24.refs_9_ = bf16[2,96,512]{2,1,0:T(8,128)(2,1)S(1)} collective-permute-done((bf16[2,96,512]{2,1,0:T(8,128)(2,1)S(1)}, bf16[2,96,512]{2,1,0:T(8,128)(2,1)S(1)}, u32[]{:S(2)}, u32[]{:S(2)}) %collective-permute-start.24) | collective-permute-done | bytes 196640 | tf_op jit(solution)/shard_map/ppermute | solution.py:355
  97.0 3.8 %collective-permute-done.23.refs_8_ = bf16[2,96,512]{2,1,0:T(8,128)(2,1)S(1)} collective-permute-done((bf16[2,96,512]{2,1,0:T(8,128)(2,1)S(1)}, bf16[2,96,512]{2,1,0:T(8,128)(2,1)S(1)}, u32[]{:S(2)}, u32[]{:S(2)}) %collective-permute-start.23) | collective-permute-done | bytes 196640 | tf_op jit(solution)/shard_map/ppermute | solution.py:355
  100.9 10.5 %fast_gradient.6 = (bf16[2,96,512]{2,1,0:T(8,128)(2,1)S(1)}, bf16[2,96,512]{2,1,0:T(8,128)(2,1)S(1)}, bf16[2,96,512]{2,1,0:T(8,128)(2,1)S(1)}, bf16[2,96,512]{2,1,0:T(8,128)(2,1)S(1)}) custom-call(s32[3]{0:T(128)S(1)} %pad_add_fusion.place_ref, bf16[512,3072]{1,0:T(8,128)(2,1)S(1)} %copy-done, bf16[512,3072]{1,0:T(8,128)(2,1)S(1)} %copy-done.1, ...), custom_call_target="tpu_custom_call" | custom-call | tf_op jit(solution)/shard_map/fast_gradient/pallas_call | solution.py:212
  115.0 10.6 %fast_gradient.7 = (bf16[2,96,512]{2,1,0:T(8,128)(2,1)S(1)}, bf16[2,96,512]{2,1,0:T(8,128)(2,1)S(1)}, bf16[2,96,512]{2,1,0:T(8,128)(2,1)S(1)}, bf16[2,96,512]{2,1,0:T(8,128)(2,1)S(1)}) custom-call(s32[3]{0:T(128)S(1)} %pad_add_fusion.place_ref, bf16[512,3072]{1,0:T(8,128)(2,1)S(1)} %copy-done, bf16[512,3072]{1,0:T(8,128)(2,1)S(1)} %copy-done.1, ...), custom_call_target="tpu_custom_call" | custom-call | tf_op jit(solution)/shard_map/fast_gradient/pallas_call | solution.py:212
  129.2 2.6 %collective-permute-start.38 = (bf16[96,512]{1,0:T(8,128)(2,1)S(1)}, bf16[96,512]{1,0:T(8,128)(2,1)S(1)}, u32[]{:S(2)}, u32[]{:S(2)}) collective-permute-start(bf16[96,512]{1,0:T(8,128)(2,1)S(1)} %fusion.11), channel_id=1, source_target_pairs={{0,24},{4,28},{8,16},{12,20},{16,8},{20,12},{24,0},{28,4},{1,25},{... | collective-permute-start | bytes 294920 | tf_op jit(solution)/shard_map/ppermute | solution.py:350
  134.5 3.1 %collective-permute-start.37 = (bf16[96,512]{1,0:T(8,128)(2,1)S(1)}, bf16[96,512]{1,0:T(8,128)(2,1)S(1)}, u32[]{:S(2)}, u32[]{:S(2)}) collective-permute-start(bf16[96,512]{1,0:T(8,128)(2,1)S(1)} %get-tuple-element.59), channel_id=1, source_target_pairs={{0,16},{4,20},{8,24},{12,28},{16,0},{20,4},{24,8},{28,12},{1,17},{... | collective-permute-start | bytes 294920 | tf_op jit(solution)/shard_map/ppermute | solution.py:350
  137.5 3.1 %collective-permute-done.36 = bf16[96,512]{1,0:T(8,128)(2,1)S(1)} collective-permute-done((bf16[96,512]{1,0:T(8,128)(2,1)S(1)}, bf16[96,512]{1,0:T(8,128)(2,1)S(1)}, u32[]{:S(2)}, u32[]{:S(2)}) %collective-permute-start.36) | collective-permute-done | bytes 98336 | tf_op jit(solution)/shard_map/ppermute | solution.py:350
  157.1 3.7 %fast_output.4.refs_0_ = bf16[512,3072]{1,0:T(8,128)(2,1)} custom-call(s32[3]{0:T(128)S(1)} %pad_add_fusion.place_ref, bf16[512,3072]{1,0:T(8,128)(2,1)S(1)} %copy-done.2, bf16[4,2,96,512]{3,2,1,0:T(8,128)(2,1)S(1)} %pad_maximum_fusion.weight_ref, f32[48,64]{1,0:T(8,128)S(1)} %copy-done.4, f32[48,64]{1,0:T(8,128)S(1)} %copy-done.5), custom_call_target="tpu_custom_call" | custom-call | tf_op jit(solution)/shard_map/fast_output/pallas_call | solution.py:290
  161.5 3.7 %fast_output.5.refs_0_ = bf16[512,3072]{1,0:T(8,128)(2,1)} custom-call(s32[3]{0:T(128)S(1)} %pad_add_fusion.place_ref, bf16[512,3072]{1,0:T(8,128)(2,1)S(1)} %copy-done.2, bf16[4,2,96,512]{3,2,1,0:T(8,128)(2,1)S(1)} %pad_maximum_fusion.1.weight_ref, f32[48,64]{1,0:T(8,128)S(1)} %copy-done.4, f32[48,64]{1,0:T(8,128)S(1)} %copy-done.5, ...), custom_call_target="tpu_custom_call", output_to_operand_aliasing={{}: (5, {})} | custom-call | tf_op jit(solution)/shard_map/fast_output/pallas_call | solution.py:290
  165.3 3.7 %fast_output.6.refs_0_ = bf16[512,3072]{1,0:T(8,128)(2,1)} custom-call(s32[3]{0:T(128)S(1)} %pad_add_fusion.place_ref, bf16[512,3072]{1,0:T(8,128)(2,1)S(1)} %copy-done.2, bf16[4,2,96,512]{3,2,1,0:T(8,128)(2,1)S(1)} %collective-permute-done.49.weight_ref, f32[48,64]{1,0:T(8,128)S(1)} %copy-done.4, ...), custom_call_target="tpu_custom_call", output_to_operand_aliasing={{}: (5, {})} | custom-call | tf_op jit(solution)/shard_map/fast_output/pallas_call | solution.py:290
  169.0 3.7 %fast_output.7 = bf16[512,3072]{1,0:T(8,128)(2,1)} custom-call(s32[3]{0:T(128)S(1)} %pad_add_fusion.place_ref, bf16[512,3072]{1,0:T(8,128)(2,1)S(1)} %copy-done.2, bf16[4,2,96,512]{3,2,1,0:T(8,128)(2,1)S(1)} %collective-permute-done.48.weight_ref, f32[48,64]{1,0:T(8,128)S(1)} %copy-done.4, f32[48,64]{1,0:T(8,128)S(1)} %copy-done.5, ...), custom_call_target="tpu_custom_call", output_to_operand_aliasing={{}: (5, {})} | custom-call | tf_op jit(solution)/shard_map/fast_output/pallas_call | solution.py:290
  (117 shorter events, 58.4 us)
Async XLA Ops:
  3.5 29.6 %collective-permute-start = (bf16[512,1536]{1,0:T(8,128)(2,1)S(1)}, bf16[512,1536]{1,0:T(8,128)(2,1)S(1)}, u32[]{:S(2)}, u32[]{:S(2)}) collective-permute-start(bf16[512,1536]{1,0:T(8,128)(2,1)S(1)} %get-tuple-element.28), channel_id=1, source_target_pairs={{0,4},{4,0},{8,12},{12,8},{16,20},{20,16},{24,28},{28,24},{1,5},{5... | collective-permute-start | bytes 4718600 | tf_op jit(solution)/shard_map/ppermute | solution.py:345
  4.1 29.1 %collective-permute-start.1 = (bf16[512,1536]{1,0:T(8,128)(2,1)S(1)}, bf16[512,1536]{1,0:T(8,128)(2,1)S(1)}, u32[]{:S(2)}, u32[]{:S(2)}) collective-permute-start(bf16[512,1536]{1,0:T(8,128)(2,1)S(1)} %get-tuple-element.29), channel_id=1, source_target_pairs={{0,4},{4,0},{8,12},{12,8},{16,20},{20,16},{24,28},{28,24},{1,5},{5... | collective-permute-start | bytes 4718600 | tf_op jit(solution)/shard_map/ppermute | solution.py:345
  5.1 8.8 %collective-permute-start.3 = (bf16[96,512]{1,0:T(8,128)(2,1)S(1)}, bf16[96,512]{1,0:T(8,128)(2,1)S(1)}, u32[]{:S(2)}, u32[]{:S(2)}) collective-permute-start(bf16[96,512]{1,0:T(8,128)(2,1)S(1)} %convert_element_type.161), channel_id=1, source_target_pairs={{0,24},{4,28},{8,16},{12,20},{16,8},{20,12},{24,0},{28,4},{1,25},{... | collective-permute-start | bytes 294920 | tf_op jit(solution)/shard_map/ppermute | solution.py:350
  10.2 11.0 %collective-permute-start.10 = (bf16[96,512]{1,0:T(8,128)(2,1)S(1)}, bf16[96,512]{1,0:T(8,128)(2,1)S(1)}, u32[]{:S(2)}, u32[]{:S(2)}) collective-permute-start(bf16[96,512]{1,0:T(8,128)(2,1)S(1)} %convert_element_type.161), channel_id=1, source_target_pairs={{0,8},{4,12},{8,0},{12,4},{16,24},{20,28},{24,16},{28,20},{1,9},{5... | collective-permute-start | bytes 294920 | tf_op jit(solution)/shard_map/ppermute | solution.py:350
  21.1 10.4 %collective-permute-start.5 = (bf16[2,96,512]{2,1,0:T(8,128)(2,1)S(1)}, bf16[2,96,512]{2,1,0:T(8,128)(2,1)S(1)}, u32[]{:S(2)}, u32[]{:S(2)}) collective-permute-start(bf16[2,96,512]{2,1,0:T(8,128)(2,1)S(1)} %pad_maximum_fusion.2.refs_6_), channel_id=1, source_target_pairs={{0,2},{1,3},{2,0},{3,1},{4,6},{5,7},{6,4},{7,5},{8,10},{9,11},{10,... | collective-permute-start | bytes 589832 | tf_op jit(solution)/shard_map/ppermute | solution.py:355
  21.7 11.4 %collective-permute-start.4 = (bf16[2,96,512]{2,1,0:T(8,128)(2,1)S(1)}, bf16[2,96,512]{2,1,0:T(8,128)(2,1)S(1)}, u32[]{:S(2)}, u32[]{:S(2)}) collective-permute-start(bf16[2,96,512]{2,1,0:T(8,128)(2,1)S(1)} %pad_maximum_fusion.2.refs_6_), channel_id=1, source_target_pairs={{0,1},{1,0},{2,3},{3,2},{4,5},{5,4},{6,7},{7,6},{8,9},{9,8},{10,11... | collective-permute-start | bytes 589832 | tf_op jit(solution)/shard_map/ppermute | solution.py:355
  27.4 16.2 %collective-permute-start.14 = (bf16[2,96,512]{2,1,0:T(8,128)(2,1)S(1)}, bf16[2,96,512]{2,1,0:T(8,128)(2,1)S(1)}, u32[]{:S(2)}, u32[]{:S(2)}) collective-permute-start(bf16[2,96,512]{2,1,0:T(8,128)(2,1)S(1)} %pad_maximum_fusion.3.refs_6_), channel_id=1, source_target_pairs={{0,3},{1,2},{2,1},{3,0},{4,7},{5,6},{6,5},{7,4},{8,11},{9,10},{10,... | collective-permute-start | bytes 589832 | tf_op jit(solution)/shard_map/ppermute | solution.py:355
  31.6 12.0 %collective-permute-start.13 = (bf16[2,96,512]{2,1,0:T(8,128)(2,1)S(1)}, bf16[2,96,512]{2,1,0:T(8,128)(2,1)S(1)}, u32[]{:S(2)}, u32[]{:S(2)}) collective-permute-start(bf16[2,96,512]{2,1,0:T(8,128)(2,1)S(1)} %pad_maximum_fusion.3.refs_6_), channel_id=1, source_target_pairs={{0,2},{1,3},{2,0},{3,1},{4,6},{5,7},{6,4},{7,5},{8,10},{9,11},{10,... | collective-permute-start | bytes 589832 | tf_op jit(solution)/shard_map/ppermute | solution.py:355
  33.1 10.5 %collective-permute-start.12 = (bf16[2,96,512]{2,1,0:T(8,128)(2,1)S(1)}, bf16[2,96,512]{2,1,0:T(8,128)(2,1)S(1)}, u32[]{:S(2)}, u32[]{:S(2)}) collective-permute-start(bf16[2,96,512]{2,1,0:T(8,128)(2,1)S(1)} %pad_maximum_fusion.3.refs_6_), channel_id=1, source_target_pairs={{0,1},{1,0},{2,3},{3,2},{4,5},{5,4},{6,7},{7,6},{8,9},{9,8},{10,11... | collective-permute-start | bytes 589832 | tf_op jit(solution)/shard_map/ppermute | solution.py:355
  56.0 11.8 %collective-permute-start.16 = (bf16[2,96,512]{2,1,0:T(8,128)(2,1)S(1)}, bf16[2,96,512]{2,1,0:T(8,128)(2,1)S(1)}, u32[]{:S(2)}, u32[]{:S(2)}) collective-permute-start(bf16[2,96,512]{2,1,0:T(8,128)(2,1)S(1)} %get-tuple-element.37), channel_id=1, source_target_pairs={{0,2},{1,3},{2,0},{3,1},{4,6},{5,7},{6,4},{7,5},{8,10},{9,11},{10,... | collective-permute-start | bytes 589832 | tf_op jit(solution)/shard_map/ppermute | solution.py:355
  56.5 11.3 %collective-permute-start.17 = (bf16[2,96,512]{2,1,0:T(8,128)(2,1)S(1)}, bf16[2,96,512]{2,1,0:T(8,128)(2,1)S(1)}, u32[]{:S(2)}, u32[]{:S(2)}) collective-permute-start(bf16[2,96,512]{2,1,0:T(8,128)(2,1)S(1)} %get-tuple-element.38), channel_id=1, source_target_pairs={{0,3},{1,2},{2,1},{3,0},{4,7},{5,6},{6,5},{7,4},{8,11},{9,10},{10,... | collective-permute-start | bytes 589832 | tf_op jit(solution)/shard_map/ppermute | solution.py:355
  57.5 13.5 %collective-permute-start.7 = (bf16[2,96,512]{2,1,0:T(8,128)(2,1)S(1)}, bf16[2,96,512]{2,1,0:T(8,128)(2,1)S(1)}, u32[]{:S(2)}, u32[]{:S(2)}) collective-permute-start(bf16[2,96,512]{2,1,0:T(8,128)(2,1)S(1)} %get-tuple-element.31), channel_id=1, source_target_pairs={{0,1},{1,0},{2,3},{3,2},{4,5},{5,4},{6,7},{7,6},{8,9},{9,8},{10,11... | collective-permute-start | bytes 589832 | tf_op jit(solution)/shard_map/ppermute | solution.py:355
  59.5 15.0 %collective-permute-start.8 = (bf16[2,96,512]{2,1,0:T(8,128)(2,1)S(1)}, bf16[2,96,512]{2,1,0:T(8,128)(2,1)S(1)}, u32[]{:S(2)}, u32[]{:S(2)}) collective-permute-start(bf16[2,96,512]{2,1,0:T(8,128)(2,1)S(1)} %get-tuple-element.32), channel_id=1, source_target_pairs={{0,2},{1,3},{2,0},{3,1},{4,6},{5,7},{6,4},{7,5},{8,10},{9,11},{10,... | collective-permute-start | bytes 589832 | tf_op jit(solution)/shard_map/ppermute | solution.py:355
  61.8 12.7 %collective-permute-start.9 = (bf16[2,96,512]{2,1,0:T(8,128)(2,1)S(1)}, bf16[2,96,512]{2,1,0:T(8,128)(2,1)S(1)}, u32[]{:S(2)}, u32[]{:S(2)}) collective-permute-start(bf16[2,96,512]{2,1,0:T(8,128)(2,1)S(1)} %get-tuple-element.33), channel_id=1, source_target_pairs={{0,3},{1,2},{2,1},{3,0},{4,7},{5,6},{6,5},{7,4},{8,11},{9,10},{10,... | collective-permute-start | bytes 589832 | tf_op jit(solution)/shard_map/ppermute | solution.py:355
  67.9 9.2 %collective-permute-start.18 = (bf16[96,512]{1,0:T(8,128)(2,1)S(1)}, bf16[96,512]{1,0:T(8,128)(2,1)S(1)}, u32[]{:S(2)}, u32[]{:S(2)}) collective-permute-start(bf16[96,512]{1,0:T(8,128)(2,1)S(1)} %get-tuple-element.60), channel_id=1, source_target_pairs={{0,8},{4,12},{8,0},{12,4},{16,24},{20,28},{24,16},{28,20},{1,9},{5... | collective-permute-start | bytes 294920 | tf_op jit(solution)/shard_map/ppermute | solution.py:350
  68.0 9.1 %collective-permute-start.19 = (bf16[96,512]{1,0:T(8,128)(2,1)S(1)}, bf16[96,512]{1,0:T(8,128)(2,1)S(1)}, u32[]{:S(2)}, u32[]{:S(2)}) collective-permute-start(bf16[96,512]{1,0:T(8,128)(2,1)S(1)} %get-tuple-element.61), channel_id=1, source_target_pairs={{0,16},{4,20},{8,24},{12,28},{16,0},{20,4},{24,8},{28,12},{1,17},{... | collective-permute-start | bytes 294920 | tf_op jit(solution)/shard_map/ppermute | solution.py:350
  89.4 11.5 %collective-permute-start.23 = (bf16[2,96,512]{2,1,0:T(8,128)(2,1)S(1)}, bf16[2,96,512]{2,1,0:T(8,128)(2,1)S(1)}, u32[]{:S(2)}, u32[]{:S(2)}) collective-permute-start(bf16[2,96,512]{2,1,0:T(8,128)(2,1)S(1)} %pad_maximum_fusion.4.refs_6_), channel_id=1, source_target_pairs={{0,2},{1,3},{2,0},{3,1},{4,6},{5,7},{6,4},{7,5},{8,10},{9,11},{10,... | collective-permute-start | bytes 589832 | tf_op jit(solution)/shard_map/ppermute | solution.py:355
  89.8 11.1 %collective-permute-start.22 = (bf16[2,96,512]{2,1,0:T(8,128)(2,1)S(1)}, bf16[2,96,512]{2,1,0:T(8,128)(2,1)S(1)}, u32[]{:S(2)}, u32[]{:S(2)}) collective-permute-start(bf16[2,96,512]{2,1,0:T(8,128)(2,1)S(1)} %pad_maximum_fusion.4.refs_6_), channel_id=1, source_target_pairs={{0,1},{1,0},{2,3},{3,2},{4,5},{5,4},{6,7},{7,6},{8,9},{9,8},{10,11... | collective-permute-start | bytes 589832 | tf_op jit(solution)/shard_map/ppermute | solution.py:355
  91.5 22.1 %collective-permute-start.32 = (bf16[2,96,512]{2,1,0:T(8,128)(2,1)S(1)}, bf16[2,96,512]{2,1,0:T(8,128)(2,1)S(1)}, u32[]{:S(2)}, u32[]{:S(2)}) collective-permute-start(bf16[2,96,512]{2,1,0:T(8,128)(2,1)S(1)} %pad_maximum_fusion.5.refs_6_), channel_id=1, source_target_pairs={{0,3},{1,2},{2,1},{3,0},{4,7},{5,6},{6,5},{7,4},{8,11},{9,10},{10,... | collective-permute-start | bytes 589832 | tf_op jit(solution)/shard_map/ppermute | solution.py:355
  93.0 22.0 %collective-permute-start.31 = (bf16[2,96,512]{2,1,0:T(8,128)(2,1)S(1)}, bf16[2,96,512]{2,1,0:T(8,128)(2,1)S(1)}, u32[]{:S(2)}, u32[]{:S(2)}) collective-permute-start(bf16[2,96,512]{2,1,0:T(8,128)(2,1)S(1)} %pad_maximum_fusion.5.refs_6_), channel_id=1, source_target_pairs={{0,2},{1,3},{2,0},{3,1},{4,6},{5,7},{6,4},{7,5},{8,10},{9,11},{10,... | collective-permute-start | bytes 589832 | tf_op jit(solution)/shard_map/ppermute | solution.py:355
  96.6 18.3 %collective-permute-start.30 = (bf16[2,96,512]{2,1,0:T(8,128)(2,1)S(1)}, bf16[2,96,512]{2,1,0:T(8,128)(2,1)S(1)}, u32[]{:S(2)}, u32[]{:S(2)}) collective-permute-start(bf16[2,96,512]{2,1,0:T(8,128)(2,1)S(1)} %pad_maximum_fusion.5.refs_6_), channel_id=1, source_target_pairs={{0,1},{1,0},{2,3},{3,2},{4,5},{5,4},{6,7},{7,6},{8,9},{9,8},{10,11... | collective-permute-start | bytes 589832 | tf_op jit(solution)/shard_map/ppermute | solution.py:355
  111.4 16.3 %collective-permute-start.25 = (bf16[2,96,512]{2,1,0:T(8,128)(2,1)S(1)}, bf16[2,96,512]{2,1,0:T(8,128)(2,1)S(1)}, u32[]{:S(2)}, u32[]{:S(2)}) collective-permute-start(bf16[2,96,512]{2,1,0:T(8,128)(2,1)S(1)} %get-tuple-element.40), channel_id=1, source_target_pairs={{0,1},{1,0},{2,3},{3,2},{4,5},{5,4},{6,7},{7,6},{8,9},{9,8},{10,11... | collective-permute-start | bytes 589832 | tf_op jit(solution)/shard_map/ppermute | solution.py:355
  111.9 17.3 %collective-permute-start.26 = (bf16[2,96,512]{2,1,0:T(8,128)(2,1)S(1)}, bf16[2,96,512]{2,1,0:T(8,128)(2,1)S(1)}, u32[]{:S(2)}, u32[]{:S(2)}) collective-permute-start(bf16[2,96,512]{2,1,0:T(8,128)(2,1)S(1)} %get-tuple-element.41), channel_id=1, source_target_pairs={{0,2},{1,3},{2,0},{3,1},{4,6},{5,7},{6,4},{7,5},{8,10},{9,11},{10,... | collective-permute-start | bytes 589832 | tf_op jit(solution)/shard_map/ppermute | solution.py:355
  113.5 15.6 %collective-permute-start.27 = (bf16[2,96,512]{2,1,0:T(8,128)(2,1)S(1)}, bf16[2,96,512]{2,1,0:T(8,128)(2,1)S(1)}, u32[]{:S(2)}, u32[]{:S(2)}) collective-permute-start(bf16[2,96,512]{2,1,0:T(8,128)(2,1)S(1)} %get-tuple-element.42), channel_id=1, source_target_pairs={{0,3},{1,2},{2,1},{3,0},{4,7},{5,6},{6,5},{7,4},{8,11},{9,10},{10,... | collective-permute-start | bytes 589832 | tf_op jit(solution)/shard_map/ppermute | solution.py:355
  (34 other events, 441.6 us)
